TPU v7x, 128 devices: a whole 4x4x4 slice. The times are simulated.
128 devices in a mesh: vol: 32 (over y, x, core), surf: 4 (over z).
Axes of the slice: x: 4, y: 4, z: 4, core: 2. Of those that a mesh axis runs over, the one named last changes fastest.
Arguments:
- node_pos: float32 [2048, 3, 128], P('vol'), may hold values from -6 to 6
- centres: float32 [8192, 3, 128], P(('vol', 'surf')), may hold values from -6 to 6
- coefs: float32 [8192, 3, 128], P(('vol', 'surf')), may hold values from -0.3 to 0.3
- radii: float32 [8192, 128], P(('vol', 'surf')), may hold values from 3 to 6
- block_list: int32 [4, 2048, 16], P('surf', 'vol'), may hold values from 0 to 8191, as said below
- neighbours: int32 [2048, 8], P('vol'), may hold values from 0 to 2047, as said below
- faces: int32 [2048, 3, 256], P('vol'), may hold values from 0 to 1023
Outputs:
- velocity: float32 [2048, 3, 128], P('vol')
- swept: float32 [2048, 256], P('vol')
Inputs may be any that keep to these rules, and one draw needn't show every extreme that they name: `block_list`: A value g names block g % 64 of device g // 64 in the flat order of vol+surf. The 1024 entries held by one device name blocks of every device exactly 8 times; the 16 entries of one box on one device name blocks of distinct devices. `neighbours`: every entry of box b names a box within 4 of b.
All inputs are finite; a program needn't handle non-finite values.
Results may differ from a plain program's by a relative error of at most 0.00017.
Values sent between devices are 32-bit elements; how exact they have to be, the bound alone decides.
No kernel may reach another device: no remote copies, remote signals or barrier semaphores. Data moves between devices by JAX's collectives and lax.ppermute only.
A program may use at most 64 MiB of HBM per device.

v0:
```python
import functools

import jax
import jax.numpy as jnp
from jax import lax
from jax.experimental import pallas as pl
from jax.experimental.pallas import tpu as pltpu
from jax.sharding import PartitionSpec as P

BF = jnp.bfloat16
F = jnp.float32
I = jnp.int32
BOTH = ("vol", "surf")
DEVICES = 128
SLOTS = 8
ROWS = 3 * SLOTS
BOX_DEV = 64
QUARTER = 16
TINY = 1e-30
VMEM = pl.BlockSpec(memory_space=pltpu.VMEM)
SMEM = pl.BlockSpec(memory_space=pltpu.SMEM)


def call(kernel, name, outs, ins, scratch=()):
    specs = [SMEM if space == "s" else VMEM for space, _ in ins]
    return pl.pallas_call(
        kernel,
        name=name,
        out_shape=outs,
        in_specs=specs,
        out_specs=tuple(VMEM for _ in outs),
        scratch_shapes=list(scratch),
    )(*[array for _, array in ins])


def split3(x):
    first = x.astype(BF).astype(F)
    rest = x - first
    second = rest.astype(BF).astype(F)
    return first, second, (rest - second).astype(BF).astype(F)


def slot_table(listed):
    owner = listed >> 6
    local = (listed & 63) + 1
    lanes = lax.broadcasted_iota(I, (BOX_DEV, DEVICES), 1)
    table = jnp.zeros((BOX_DEV, DEVICES), I)
    for k in range(listed.shape[1]):
        hit = owner[:, k : k + 1] == lanes
        table = jnp.where(hit, local[:, k : k + 1], table)
    table = table.astype(F)
    used = table > 0.0
    row = lax.broadcasted_iota(I, (BOX_DEV, BOX_DEV), 0)
    col = lax.broadcasted_iota(I, (BOX_DEV, BOX_DEV), 1)
    before = (col < row).astype(F).astype(BF)
    rank = jnp.dot(before, used.astype(F).astype(BF), preferred_element_type=F)
    return table, jnp.where(used, rank, -1.0)


def prep_kernel(list_ref, node_ref, send_ref, ids_ref):
    table, slot = slot_table(list_ref[...])
    slot_t = slot.T
    nodes = jnp.concatenate([node_ref[:, c, :] for c in range(3)], 1)
    parts = [p.astype(BF) for p in split3(nodes)]
    ids = []
    for j in range(SLOTS):
        ids.append(jnp.sum(jnp.where(slot == float(j), table - 1.0, 0.0), axis=0, keepdims=True))
        sel = (slot_t == float(j)).astype(F).astype(BF)
        got = sum(jnp.dot(sel, p, preferred_element_type=F) for p in parts)
        for c in range(3):
            send_ref[pl.ds(c * SLOTS + j, DEVICES, stride=ROWS), :] = got[:, c * 128 : (c + 1) * 128]
    stacked = jnp.concatenate(ids + [jnp.zeros((120, 128), F)], 0).T
    ids_ref[...] = stacked[:, 0:SLOTS].astype(I)


def feat_kernel(cen_ref, coef_ref, rad_ref, a_ref, cf_ref):
    def one(g, carry):
        c = cen_ref[g]
        r = rad_ref[pl.ds(g, 1), :]
        inv = 1.0 / (r * r)
        sq = c[0:1] * c[0:1] + c[1:2] * c[1:2] + c[2:3] * c[2:3]
        f = jnp.concatenate([c * (-2.0 * inv), inv, inv * sq, jnp.zeros((3, 128), F)], 0)
        p, q, t = split3(f)
        s = jnp.concatenate([p, p, p, q, q, t, jnp.zeros((80, 128), F)], 0)
        a_ref[pl.ds(pl.multiple_of(g * 128, 128), 128), :] = s.T.astype(BF)
        ks = split3(4.0 * coef_ref[g])
        z = jnp.concatenate([*ks, jnp.zeros((7, 128), F)], 0).astype(BF)
        cf_ref[pl.ds(pl.multiple_of(g * 16, 16), 16), :] = jnp.concatenate([z, z], 1)
        return carry

    lax.fori_loop(0, 64, one, 0)


def terms_kernel(ids_ref, x_ref, a_ref, cf_ref, o_ref, v_ref, q_ref, w_ref):
    def stage1(i, buf):
        base = pl.multiple_of(i * ROWS, ROWS)
        x = x_ref[pl.ds(base, 8), :]
        y = x_ref[pl.ds(base + 8, 8), :]
        z = x_ref[pl.ds(base + 16, 8), :]
        sq = x * x + y * y + z * z
        for f, value in enumerate((x, y, z, sq, jnp.ones_like(x))):
            for k, part in enumerate(split3(value)):
                v_ref[buf, k, pl.ds(f * 8, 8), :] = part
        for j in range(SLOTS):
            g = ids_ref[i, j]
            v = [v_ref[buf, k, pl.ds(j, 8, stride=8), :] for k in range(3)]
            b = jnp.concatenate([v[0], v[1], v[2], v[0], v[1], v[0], jnp.zeros((80, 128), F)], 0)
            a = a_ref[pl.ds(pl.multiple_of(g * 128, 128), 128), :]
            q_ref[buf, j] = jnp.dot(a, b.astype(BF), preferred_element_type=F)

    def stage2(buf):
        for j in range(SLOTS):
            m = jnp.maximum(q_ref[buf, j], TINY)
            q = m * lax.rsqrt(m)
            t = jnp.maximum(1.0 - q, 0.0)
            t = t * t
            w = (t * t) * (q + 0.25)
            high = w.astype(BF)
            w_ref[buf, j, 0:128, :] = high
            w_ref[buf, j, 128:256, :] = (w - high.astype(F)).astype(BF)

    def stage3(i, buf):
        base = pl.multiple_of(i * ROWS, ROWS)
        for j in range(SLOTS):
            g = ids_ref[i, j]
            c = cf_ref[pl.ds(pl.multiple_of(g * 16, 16), 16), :]
            r = jnp.dot(c, w_ref[buf, j], preferred_element_type=F)
            o_ref[pl.ds(base + j, 3, stride=8), :] = r[0:3] + r[3:6] + r[6:9]

    for k in range(3):
        for buf in range(2):
            v_ref[buf, k, pl.ds(40, 24), :] = jnp.zeros((24, 128), F)
    stage1(0, 0)
    stage1(1, 1)
    stage2(0)

    def two(h, carry):
        i = 2 * h
        stage1(i + 2, 0)
        stage2(1)
        stage3(i, 0)
        stage1(i + 3, 1)
        stage2(0)
        stage3(i + 1, 1)
        return carry

    lax.fori_loop(0, DEVICES // 2 - 1, two, 0)
    stage2(1)
    stage3(DEVICES - 2, 0)
    stage3(DEVICES - 1, 1)


def sum_kernel(where_ref, list_ref, back_ref, own_ref, one_ref, two_ref, three_ref, acc_ref):
    _, slot = slot_table(list_ref[...])
    acc = jnp.zeros((BOX_DEV, 384), F)
    for j in range(SLOTS):
        sel = (slot == float(j)).astype(F).astype(BF)
        terms = jnp.concatenate(
            [back_ref[pl.ds(c * SLOTS + j, DEVICES, stride=ROWS), :] for c in range(3)], 1
        )
        for part in split3(terms):
            acc = acc + jnp.dot(sel, part.astype(BF), preferred_element_type=F)
    for c in range(3):
        acc_ref[c] = acc[:, c * 128 : (c + 1) * 128]
    surf = where_ref[0]
    for k, ref in enumerate((own_ref, one_ref, two_ref, three_ref)):
        first = pl.multiple_of(((surf + k) & 3) * QUARTER, QUARTER)
        for c in range(3):
            ref[c * QUARTER : (c + 1) * QUARTER, :] = acc_ref[c, pl.ds(first, QUARTER), :]


def reduce_kernel(where_ref, node_ref, own_ref, one_ref, two_ref, three_ref, d_ref, up_ref, down_ref):
    d = own_ref[...] + one_ref[...] + two_ref[...] + three_ref[...]
    d_ref[...] = d
    first = pl.multiple_of(where_ref[0] * QUARTER, QUARTER)
    for c in range(3):
        x = node_ref[pl.ds(first, QUARTER), c, :]
        down_ref[c * 8 : c * 8 + 8, :] = x[0:8]
        up_ref[c * 8 : c * 8 + 8, :] = x[8:16]
        down_ref[24 + c * 8 : 32 + c * 8, :] = d[c * 16 : c * 16 + 8]
        up_ref[24 + c * 8 : 32 + c * 8, :] = d[c * 16 + 8 : c * 16 + 16]


def face_kernel(where_ref, near_ref, node_ref, d_ref, low_ref, high_ref, face_ref, o_ref, tab_ref, cor_ref):
    first = pl.multiple_of(where_ref[0] * QUARTER, QUARTER)
    origin = where_ref[1] * QUARTER - 8
    zero = jnp.zeros((32, 128), F)
    for c in range(8):
        if c < 3:
            own = node_ref[pl.ds(first, QUARTER), c, :]
        elif c < 6:
            own = d_ref[(c - 3) * 16 : (c - 2) * 16, :]
        if c < 6:
            rows = jnp.concatenate(
                [low_ref[c * 8 : c * 8 + 8, :], own, high_ref[c * 8 : c * 8 + 8, :]], 0
            )
        else:
            rows = zero
        tab_ref[pl.ds(c, 32, stride=8), :] = rows

    def one_box(b, carry):
        box = first + b
        tables = []
        for j in range(8):
            at = near_ref[box, j] - origin
            tables.append(tab_ref[pl.ds(pl.multiple_of(at * 8, 8), 8), :])
        for h in range(2):
            for k in range(3):
                code = face_ref[box, k : k + 1, h * 128 : (h + 1) * 128]
                code = jnp.broadcast_to(code, (8, 128))
                lane = code & 127
                which = code >> 7
                got = None
                for j in range(8):
                    value = jnp.take_along_axis(tables[j], lane, axis=1)
                    got = value if got is None else jnp.where(which == j, value, got)
                cor_ref[k, pl.ds(b * 2 + h, 8, stride=32), :] = got
        return carry

    lax.fori_loop(0, QUARTER, one_box, 0)

    def corner(k):
        part = [cor_ref[k, pl.ds(c * 32, 32), :] for c in range(6)]
        return [part[c] + 0.5 * part[c + 3] for c in range(3)], part[3:6]

    (ma, da), (mb, db), (mc, dc) = corner(0), corner(1), corner(2)
    u = [mb[c] - ma[c] for c in range(3)]
    w = [mc[c] - ma[c] for c in range(3)]
    swept = None
    for c in range(3):
        p, q = (c + 1) % 3, (c + 2) % 3
        normal = 0.5 * (u[p] * w[q] - u[q] * w[p])
        term = ((da[c] + db[c] + dc[c]) / 3.0) * normal
        swept = term if swept is None else swept + term
    o_ref[0:48, :] = d_ref[...] * 2.0
    o_ref[48:80, :] = swept


def out_kernel(where_ref, own_ref, one_ref, two_ref, three_ref, v_ref, s_ref):
    surf = where_ref[0]
    for k, ref in enumerate((own_ref, one_ref, two_ref, three_ref)):
        first = pl.multiple_of(((surf + 4 - k) & 3) * QUARTER, QUARTER)
        for c in range(3):
            v_ref[pl.ds(first, QUARTER), c, :] = ref[c * 16 : (c + 1) * 16, :]
        for h in range(2):
            s_ref[pl.ds(first, QUARTER), h * 128 : (h + 1) * 128] = ref[
                pl.ds(48 + h, QUARTER, stride=2), :
            ]


def to_all(array):
    return lax.all_to_all(array, BOTH, split_axis=0, concat_axis=0, tiled=True)


def around(arrays):
    return [
        lax.ppermute(a, "surf", [(i, (i + k) % 4) for i in range(4)])
        for k, a in zip((1, 2, 3), arrays)
    ]


def shape(*dims, kind=F):
    return jax.ShapeDtypeStruct(dims, kind)


def body(node_pos, centres, coefs, radii, block_list, neighbours, faces):
    listed = block_list[0]
    surf = lax.axis_index("surf")
    where = jnp.stack([surf, lax.axis_index("vol") * 4 + surf]).astype(I)
    send, ids = call(
        prep_kernel,
        "prep",
        (shape(DEVICES * ROWS, 128), shape(DEVICES, SLOTS, kind=I)),
        [("v", listed), ("v", node_pos)],
    )
    arrived = to_all(send.reshape(DEVICES, ROWS, 128)).reshape(DEVICES * ROWS, 128)
    asked = to_all(ids)
    table, weights = call(
        feat_kernel,
        "feats",
        (shape(64 * 128, 128, kind=BF), shape(64 * 16, 256, kind=BF)),
        [("v", centres), ("v", coefs), ("v", radii)],
    )
    (terms,) = call(
        terms_kernel,
        "terms",
        (shape(DEVICES * ROWS, 128),),
        [("s", asked), ("v", arrived), ("v", table), ("v", weights)],
        [
            pltpu.VMEM((2, 3, 64, 128), F),
            pltpu.VMEM((2, SLOTS, 128, 128), F),
            pltpu.VMEM((2, SLOTS, 256, 128), BF),
        ],
    )
    back = to_all(terms.reshape(DEVICES, ROWS, 128)).reshape(DEVICES * ROWS, 128)
    quarter = tuple(shape(48, 128) for _ in range(4))
    own, *rest = call(
        sum_kernel,
        "sums",
        quarter,
        [("s", where), ("v", listed), ("v", back)],
        [pltpu.VMEM((3, BOX_DEV, 128), F)],
    )
    d, up, down = call(
        reduce_kernel,
        "reduce",
        quarter[:3],
        [("s", where), ("v", node_pos), ("v", own)] + [("v", r) for r in around(rest)],
    )
    low = lax.ppermute(up, BOTH, [(i, i + 1) for i in range(DEVICES - 1)])
    high = lax.ppermute(down, BOTH, [(i + 1, i) for i in range(DEVICES - 1)])
    (mine,) = call(
        face_kernel,
        "faces",
        (shape(80, 128),),
        [("s", where), ("s", neighbours), ("v", node_pos), ("v", d), ("v", low), ("v", high), ("v", faces)],
        [pltpu.VMEM((256, 128), F), pltpu.VMEM((3, 256, 128), F)],
    )
    return tuple(
        call(
            out_kernel,
            "outs",
            (shape(BOX_DEV, 3, 128), shape(BOX_DEV, 256)),
            [("s", where), ("v", mine)] + [("v", r) for r in around([mine] * 3)],
        )
    )


def solution(mesh):
    placed = (
        P("vol", None, None),
        P(("vol", "surf"), None, None),
        P(("vol", "surf"), None, None),
        P(("vol", "surf"), None),
        P("surf", "vol", None),
        P("vol", None),
        P("vol", None, None),
    )
    return jax.shard_map(
        body,
        mesh=mesh,
        in_specs=placed,
        out_specs=(P("vol", None, None), P("vol", None)),
        check_vma=False,
    )
```

profile of v0, /device:TPU:8, one launch (start us, length us, event | category | flops | bytes accessed | tf_op | source)
XLA Modules:
  0.0 183.4 jit_solution(12793134979596761487)
XLA Ops:
  0.6 1.6 copy.25.node_ref
  2.2 1.4 copy.18
  3.6 3.5 %prep.1 = (f32[3072,128]{1,0:T(8,128)}, s32[128,8]{1,0:T(8,128)}) custom-call(s32[64,16]{1,0:T(8,128)} %bitcast.15, f32[64,3,128]{2,1,0:T(4,128)} %copy.25.node_ref), custom_call_target="tpu_custom_call" | custom-call | tf_op jit(solution)/shard_map/prep/pallas_call | solution.py:26
  7.2 19.5 %all_to_all.21 = s32[128,1,8]{2,1,0:T(1,128)} all-to-all(s32[128,1,8]{2,1,0:T(1,128)} %bitcast.18), channel_id=1, replica_groups=mesh['vol'=32,'surf'=4] {'vol','surf'}, dimensions={0} | all-to-all | bytes 8192 | tf_op jit(solution)/shard_map/all_to_all | solution.py:252
  26.6 5.4 %all-to-all-start.1 = ((f32[128,24,128]{2,1,0:T(8,128)}), f32[128,24,128]{2,1,0:T(8,128)S(1)}, u32[]{:S(2)}, u32[]{:S(2)}) async-start(f32[128,24,128]{2,1,0:T(8,128)} %bitcast.14), calls=%async_computation.1 | async-start | bytes 3145728 | tf_op jit(solution)/shard_map/all_to_all | solution.py:252
  32.0 0.0 copy-done.3
  32.1 0.7 copy.21.cen_ref
  32.8 0.0 copy-done.4
  32.8 0.7 copy.22.coef_ref
  33.5 9.8 %feats.1 = (bf16[8192,128]{1,0:T(8,128)(2,1)}, bf16[1024,256]{1,0:T(8,128)(2,1)}) custom-call(f32[64,3,128]{2,1,0:T(4,128)} %copy.21.cen_ref, f32[64,3,128]{2,1,0:T(4,128)} %copy.22.coef_ref, f32[64,128]{1,0:T(8,128)} %rad_ref.1), custom_call_target="tpu_custom_call" | custom-call | tf_op jit(solution)/shard_map/feats/pallas_call | solution.py:26
  43.2 12.7 %all-to-all-done.1 = f32[128,24,128]{2,1,0:T(8,128)S(1)} async-done(((f32[128,24,128]{2,1,0:T(8,128)}), f32[128,24,128]{2,1,0:T(8,128)S(1)}, u32[]{:S(2)}, u32[]{:S(2)}) %all-to-all-start.1) | async-done | bytes 1572896 | tf_op jit(solution)/shard_map/all_to_all | solution.py:252
  55.9 1.2 copy-done.1
  57.1 57.1 %terms.1 = f32[3072,128]{1,0:T(8,128)} custom-call(s32[128,8]{1,0:T(8,128)} %bitcast.17, f32[3072,128]{1,0:T(8,128)} %bitcast.13, bf16[8192,128]{1,0:T(8,128)(2,1)} %get-tuple-element.15.a_ref, bf16[1024,256]{1,0:T(8,128)(2,1)} %get-tuple-element.16.cf_ref), custom_call_target="tpu_custom_call" | custom-call | tf_op jit(solution)/shard_map/terms/pallas_call | solution.py:26
  114.1 4.9 %all-to-all-start.2 = ((f32[128,24,128]{2,1,0:T(8,128)}), f32[128,24,128]{2,1,0:T(8,128)S(1)}, u32[]{:S(2)}, u32[]{:S(2)}) async-start(f32[128,24,128]{2,1,0:T(8,128)} %bitcast.12), calls=%async_computation.2 | async-start | bytes 3145728 | tf_op jit(solution)/shard_map/all_to_all | solution.py:252
  119.1 0.0 copy-start.2
  119.1 0.0 copy-start.13
  119.1 0.6 pad_add_fusion.where_ref
  119.7 23.3 %all-to-all-done.2 = f32[128,24,128]{2,1,0:T(8,128)S(1)} async-done(((f32[128,24,128]{2,1,0:T(8,128)}), f32[128,24,128]{2,1,0:T(8,128)S(1)}, u32[]{:S(2)}, u32[]{:S(2)}) %all-to-all-start.2) | async-done | bytes 1572896 | tf_op jit(solution)/shard_map/all_to_all | solution.py:252
  143.0 1.2 copy-done
  144.2 3.5 %sums.1 = (f32[48,128]{1,0:T(8,128)}, f32[48,128]{1,0:T(8,128)}, f32[48,128]{1,0:T(8,128)}, f32[48,128]{1,0:T(8,128)}) custom-call(s32[2]{0:T(128)} %pad_add_fusion.where_ref, s32[64,16]{1,0:T(8,128)} %bitcast.16, f32[3072,128]{1,0:T(8,128)} %bitcast.11), custom_call_target="tpu_custom_call" | custom-call | tf_op jit(solution)/shard_map/sums/pallas_call | solution.py:26
  147.7 0.8 collective-permute-start
  148.5 1.7 collective-permute-start.1
  150.2 1.0 collective-permute-start.2
  151.3 1.9 %collective-permute-done.one_ref = f32[48,128]{1,0:T(8,128)S(1)} collective-permute-done((f32[48,128]{1,0:T(8,128)}, f32[48,128]{1,0:T(8,128)S(1)}, u32[]{:S(2)}, u32[]{:S(2)}) %collective-permute-start) | collective-permute-done | bytes 24608 | tf_op jit(solution)/shard_map/ppermute | solution.py:257
  153.1 0.9 collective-permute-done.1.two_ref
  154.1 0.2 collective-permute-done.2.three_ref
  154.3 0.4 copy-done.11
  154.7 0.2 copy-done.12
  154.9 1.6 reduce.1
  156.5 3.4 %collective-permute-start.3 = (f32[48,128]{1,0:T(8,128)}, f32[48,128]{1,0:T(8,128)S(1)}, u32[]{:S(2)}, u32[]{:S(2)}) collective-permute-start(f32[48,128]{1,0:T(8,128)} %get-tuple-element.22), channel_id=1, source_target_pairs={{0,1},{1,2},{2,3},{3,4},{4,5},{5,6},{6,7},{7,8},{8,9},{9,10},{10,1... | collective-permute-start | bytes 73736 | tf_op jit(solution)/shard_map/ppermute | solution.py:310
  159.9 6.3 %collective-permute-start.4 = (f32[48,128]{1,0:T(8,128)}, f32[48,128]{1,0:T(8,128)S(1)}, u32[]{:S(2)}, u32[]{:S(2)}) collective-permute-start(f32[48,128]{1,0:T(8,128)} %get-tuple-element.23), channel_id=1, source_target_pairs={{1,0},{2,1},{3,2},{4,3},{5,4},{6,5},{7,6},{8,7},{9,8},{10,9},{11,1... | collective-permute-start | bytes 73736 | tf_op jit(solution)/shard_map/ppermute | solution.py:311
  166.3 0.8 copy.26.face_ref
  167.1 0.7 copy.24.near_ref
  167.8 0.0 collective-permute-done.3.low_ref
  167.8 0.2 collective-permute-done.4.high_ref
  168.0 0.5 copy-done.8
  168.4 0.1 copy-done.9
  168.6 4.4 %faces.1.own_ref = f32[80,128]{1,0:T(8,128)} custom-call(s32[2]{0:T(128)} %pad_add_fusion.where_ref, s32[64,8]{1,0:T(8,128)} %copy.24.near_ref, f32[64,3,128]{2,1,0:T(4,128)} %copy.25.node_ref, f32[48,128]{1,0:T(8,128)} %get-tuple-element.21.d_ref, f32[48,128]{1,0:T(8,128)} %copy-done.8, f32[48,128]{1,0:T(8,128)} %copy-done.9, s32[64,3,256]{2,1,0:T(4,128)} %copy.26.face_ref), custom_call_target="tpu_custom_call" | custom-call | tf_op jit(solution)/shard_map/faces/pallas_call | solution.py:26
  173.0 0.0 collective-permute-start.5
  173.0 0.9 collective-permute-start.6
  173.9 2.4 %collective-permute-start.7 = (f32[80,128]{1,0:T(8,128)}, f32[80,128]{1,0:T(8,128)S(1)}, u32[]{:S(2)}, u32[]{:S(2)}) collective-permute-start(f32[80,128]{1,0:T(8,128)} %faces.1.own_ref), channel_id=1, source_target_pairs={{0,3},{1,0},{2,1},{3,2},{4,7},{5,4},{6,5},{7,6},{8,11},{9,8},{10,9... | collective-permute-start | bytes 122888 | tf_op jit(solution)/shard_map/ppermute | solution.py:257
  176.2 2.6 %collective-permute-done.5.one_ref = f32[80,128]{1,0:T(8,128)S(1)} collective-permute-done((f32[80,128]{1,0:T(8,128)}, f32[80,128]{1,0:T(8,128)S(1)}, u32[]{:S(2)}, u32[]{:S(2)}) %collective-permute-start.5) | collective-permute-done | bytes 40992 | tf_op jit(solution)/shard_map/ppermute | solution.py:257
  178.8 0.0 collective-permute-done.6.two_ref
  178.8 0.8 collective-permute-done.7.three_ref
  179.7 0.0 copy-done.6
  179.7 0.6 copy-done.7
  180.3 1.6 outs.1
  181.9 1.6 copy.27
  (16 shorter events, 0.0 us)
Async XLA Ops:
  26.6 5.4 %copy-start.3 = (f32[64,3,128]{2,0,1:T(8,128)S(1)}, f32[64,3,128]{2,0,1:T(8,128)}, u32[]{:S(2)}) copy-start(f32[64,3,128]{2,0,1:T(8,128)} %param.8) | copy-start | bytes 294916
  26.6 6.1 %copy-start.4 = (f32[64,3,128]{2,0,1:T(8,128)S(1)}, f32[64,3,128]{2,0,1:T(8,128)}, u32[]{:S(2)}) copy-start(f32[64,3,128]{2,0,1:T(8,128)} %param.9) | copy-start | bytes 294916
  26.6 29.3 %all-to-all-start.1 = ((f32[128,24,128]{2,1,0:T(8,128)}), f32[128,24,128]{2,1,0:T(8,128)S(1)}, u32[]{:S(2)}, u32[]{:S(2)}) async-start(f32[128,24,128]{2,1,0:T(8,128)} %bitcast.14), calls=%async_computation.1 | async-start | bytes 3145728 | tf_op jit(solution)/shard_map/all_to_all | solution.py:252
  55.9 1.2 copy-start.1
  114.1 28.8 %all-to-all-start.2 = ((f32[128,24,128]{2,1,0:T(8,128)}), f32[128,24,128]{2,1,0:T(8,128)S(1)}, u32[]{:S(2)}, u32[]{:S(2)}) async-start(f32[128,24,128]{2,1,0:T(8,128)} %bitcast.12), calls=%async_computation.2 | async-start | bytes 3145728 | tf_op jit(solution)/shard_map/all_to_all | solution.py:252
  119.1 47.2 %copy-start.2 = (s32[64,3,256]{2,0,1:T(8,128)S(1)}, s32[64,3,256]{2,0,1:T(8,128)}, u32[]{:S(2)}) copy-start(s32[64,3,256]{2,0,1:T(8,128)} %param.13) | copy-start | bytes 589828
  119.1 48.0 %copy-start.13 = (s32[64,8]{0,1:T(8,128)S(1)}, s32[64,8]{0,1:T(8,128)}, u32[]{:S(2)}) copy-start(s32[64,8]{0,1:T(8,128)} %param.12) | copy-start | bytes 6148
  143.0 1.2 copy-start
  147.7 5.5 %collective-permute-start = (f32[48,128]{1,0:T(8,128)}, f32[48,128]{1,0:T(8,128)S(1)}, u32[]{:S(2)}, u32[]{:S(2)}) collective-permute-start(f32[48,128]{1,0:T(8,128)} %get-tuple-element.18), channel_id=1, source_target_pairs={{0,1},{1,2},{2,3},{3,0},{4,5},{5,6},{6,7},{7,4},{8,9},{9,10},{10,1... | collective-permute-start | bytes 73736 | tf_op jit(solution)/shard_map/ppermute | solution.py:257
  148.5 5.5 %collective-permute-start.1 = (f32[48,128]{1,0:T(8,128)}, f32[48,128]{1,0:T(8,128)S(1)}, u32[]{:S(2)}, u32[]{:S(2)}) collective-permute-start(f32[48,128]{1,0:T(8,128)} %get-tuple-element.19), channel_id=1, source_target_pairs={{0,2},{1,3},{2,0},{3,1},{4,6},{5,7},{6,4},{7,5},{8,10},{9,11},{10,... | collective-permute-start | bytes 73736 | tf_op jit(solution)/shard_map/ppermute | solution.py:257
  150.2 4.0 %collective-permute-start.2 = (f32[48,128]{1,0:T(8,128)}, f32[48,128]{1,0:T(8,128)S(1)}, u32[]{:S(2)}, u32[]{:S(2)}) collective-permute-start(f32[48,128]{1,0:T(8,128)} %get-tuple-element.20), channel_id=1, source_target_pairs={{0,3},{1,0},{2,1},{3,2},{4,7},{5,4},{6,5},{7,6},{8,11},{9,8},{10,9... | collective-permute-start | bytes 73736 | tf_op jit(solution)/shard_map/ppermute | solution.py:257
  153.1 1.2 copy-start.10
  154.1 0.6 copy-start.11
  154.3 0.6 copy-start.12
  156.5 11.3 %collective-permute-start.3 = (f32[48,128]{1,0:T(8,128)}, f32[48,128]{1,0:T(8,128)S(1)}, u32[]{:S(2)}, u32[]{:S(2)}) collective-permute-start(f32[48,128]{1,0:T(8,128)} %get-tuple-element.22), channel_id=1, source_target_pairs={{0,1},{1,2},{2,3},{3,4},{4,5},{5,6},{6,7},{7,8},{8,9},{9,10},{10,1... | collective-permute-start | bytes 73736 | tf_op jit(solution)/shard_map/ppermute | solution.py:310
  159.9 8.1 %collective-permute-start.4 = (f32[48,128]{1,0:T(8,128)}, f32[48,128]{1,0:T(8,128)S(1)}, u32[]{:S(2)}, u32[]{:S(2)}) collective-permute-start(f32[48,128]{1,0:T(8,128)} %get-tuple-element.23), channel_id=1, source_target_pairs={{1,0},{2,1},{3,2},{4,3},{5,4},{6,5},{7,6},{8,7},{9,8},{10,9},{11,1... | collective-permute-start | bytes 73736 | tf_op jit(solution)/shard_map/ppermute | solution.py:311
  167.8 0.6 copy-start.8
  168.0 0.6 copy-start.9
  173.0 5.9 %collective-permute-start.5 = (f32[80,128]{1,0:T(8,128)}, f32[80,128]{1,0:T(8,128)S(1)}, u32[]{:S(2)}, u32[]{:S(2)}) collective-permute-start(f32[80,128]{1,0:T(8,128)} %faces.1.own_ref), channel_id=1, source_target_pairs={{0,1},{1,2},{2,3},{3,0},{4,5},{5,6},{6,7},{7,4},{8,9},{9,10},{10,1... | collective-permute-start | bytes 122888 | tf_op jit(solution)/shard_map/ppermute | solution.py:257
  173.0 5.9 %collective-permute-start.6 = (f32[80,128]{1,0:T(8,128)}, f32[80,128]{1,0:T(8,128)S(1)}, u32[]{:S(2)}, u32[]{:S(2)}) collective-permute-start(f32[80,128]{1,0:T(8,128)} %faces.1.own_ref), channel_id=1, source_target_pairs={{0,2},{1,3},{2,0},{3,1},{4,6},{5,7},{6,4},{7,5},{8,10},{9,11},{10,... | collective-permute-start | bytes 122888 | tf_op jit(solution)/shard_map/ppermute | solution.py:257
  173.9 5.8 %collective-permute-start.7 = (f32[80,128]{1,0:T(8,128)}, f32[80,128]{1,0:T(8,128)S(1)}, u32[]{:S(2)}, u32[]{:S(2)}) collective-permute-start(f32[80,128]{1,0:T(8,128)} %faces.1.own_ref), channel_id=1, source_target_pairs={{0,3},{1,0},{2,1},{3,2},{4,7},{5,4},{6,5},{7,6},{8,11},{9,8},{10,9... | collective-permute-start | bytes 122888 | tf_op jit(solution)/shard_map/ppermute | solution.py:257
  178.8 0.9 copy-start.5
  178.8 0.9 copy-start.6
  179.7 0.6 copy-start.7
where the time goes:
time: 186 us; the launch traced here: 183 us
  Pallas kernels  81.4 us (44%)
  waiting for transfers between devices  42.6 us (23%)
  starting transfers between devices  26.9 us (14%)
  blocking collectives  19.5 us (10%)
  local copies, waits for them, and re-layouts  11.7 us (6%)
    pallas_call x7, Pallas kernels, call(): pl.pallas_call(kernel, name=name, out_shape=outs, in_specs=specs, out_spe...  81.4 us
    all_to_all x2, waiting for transfers between devices, to_all(): return lax.all_to_all(array, BOTH, split_axis=0, concat_axis=0, tiled=True)  35.9 us
    all_to_all x1, blocking collectives, to_all(): return lax.all_to_all(array, BOTH, split_axis=0, concat_axis=0, tiled=True)  19.5 us
    all_to_all x2, starting transfers between devices, to_all(): return lax.all_to_all(array, BOTH, split_axis=0, concat_axis=0, tiled=True)  10.3 us
    unnamed x34, local copies, waits for them, and re-layouts  10.2 us
    ppermute x6, starting transfers between devices, around(): lax.ppermute(a, 'surf', [(i, (i + k) % 4) for i in range(4)])  6.82 us
    ppermute x6, waiting for transfers between devices, around(): lax.ppermute(a, 'surf', [(i, (i + k) % 4) for i in range(4)])  6.5 us
    ppermute x1, starting transfers between devices, body(): high = lax.ppermute(down, BOTH, [(i + 1, i) for i in range(DEVICES - 1)])  6.35 us
  transfers between devices with their start and end apart: 10, of which 8 were waited for; matrix products, arithmetic and copies ran while one was open for 2% of the time, Pallas kernels for 5%

commit v1 on v0

v1 whole, which is shorter than its diff:
```python
import functools

import jax
import jax.numpy as jnp
from jax import lax
from jax.experimental import pallas as pl
from jax.experimental.pallas import tpu as pltpu
from jax.sharding import PartitionSpec as P

BF = jnp.bfloat16
F = jnp.float32
I = jnp.int32
BOTH = ("vol", "surf")
DEVICES = 128
SLOTS = 8
HALF = 4
ASK = 3 * HALF + 1
GIVE = 3 * HALF
BOX_DEV = 64
QUARTER = 16
HALO = 4
NEAR = QUARTER + 2 * HALO
TINY = 1e-30
VMEM = pl.BlockSpec(memory_space=pltpu.VMEM)
SMEM = pl.BlockSpec(memory_space=pltpu.SMEM)


def call(kernel, name, outs, ins, scratch=(), mib=8, us=2):
    specs = [SMEM if space == "s" else VMEM for space, _ in ins]
    return pl.pallas_call(
        kernel,
        name=name,
        out_shape=outs,
        in_specs=specs,
        out_specs=tuple(VMEM for _ in outs),
        scratch_shapes=list(scratch),
        compiler_params=pltpu.CompilerParams(vmem_limit_bytes=mib << 20),
        cost_estimate=pl.CostEstimate(flops=us * 10**9, bytes_accessed=us * 10**6, transcendentals=0),
    )(*[array for _, array in ins])


def split3(x):
    first = x.astype(BF).astype(F)
    rest = x - first
    second = rest.astype(BF).astype(F)
    return first, second, (rest - second).astype(BF).astype(F)


def slot_table(listed):
    listed = listed.astype(F).T.astype(I)
    owner = listed >> 6
    local = (listed & 63) + 1
    lanes = lax.broadcasted_iota(I, (BOX_DEV, DEVICES), 1)
    table = jnp.zeros((BOX_DEV, DEVICES), I)
    for k in range(listed.shape[1]):
        hit = owner[:, k : k + 1] == lanes
        table = jnp.where(hit, local[:, k : k + 1], table)
    table = table.astype(F)
    used = table > 0.0
    row = lax.broadcasted_iota(I, (BOX_DEV, BOX_DEV), 0)
    col = lax.broadcasted_iota(I, (BOX_DEV, BOX_DEV), 1)
    before = (col < row).astype(F).astype(BF)
    rank = jnp.dot(before, used.astype(F).astype(BF), preferred_element_type=F)
    return table, jnp.where(used, rank, -1.0)


def prep_kernel(list_ref, node_ref, low_ref, high_ref):
    table, slot = slot_table(list_ref[...])
    slot_t = slot.T
    nodes = jnp.concatenate([node_ref[c] for c in range(3)], 1)
    parts = [p.astype(BF) for p in split3(nodes)]
    for half, ref in enumerate((low_ref, high_ref)):
        ids = []
        for j in range(HALF):
            at = float(half * HALF + j)
            ids.append(jnp.sum(jnp.where(slot == at, table - 1.0, 0.0), axis=0, keepdims=True))
            sel = (slot_t == at).astype(F).astype(BF)
            got = sum(jnp.dot(sel, p, preferred_element_type=F) for p in parts)
            for c in range(3):
                ref[pl.ds(c * HALF + j, DEVICES, stride=ASK), :] = got[:, c * 128 : (c + 1) * 128]
        stacked = jnp.concatenate(ids + [jnp.zeros((128 - HALF, 128), F)], 0).T
        ref[pl.ds(ASK - 1, DEVICES, stride=ASK), :] = stacked


def feat_kernel(cen_ref, coef_ref, rad_ref, a_ref, cf_ref):
    def one(g, carry):
        c = cen_ref[:, pl.ds(g, 1), :].reshape(3, 128)
        r = rad_ref[pl.ds(g, 1), :]
        inv = 1.0 / (r * r)
        sq = c[0:1] * c[0:1] + c[1:2] * c[1:2] + c[2:3] * c[2:3]
        f = jnp.concatenate([c * (-2.0 * inv), inv, inv * sq, jnp.zeros((3, 128), F)], 0)
        p, q, t = split3(f)
        s = jnp.concatenate([p, p, p, q, q, t, jnp.zeros((80, 128), F)], 0)
        a_ref[pl.ds(pl.multiple_of(g * 128, 128), 128), :] = s.T.astype(BF)
        ks = split3(4.0 * coef_ref[:, pl.ds(g, 1), :].reshape(3, 128))
        z = jnp.concatenate([*ks, jnp.zeros((7, 128), F)], 0).astype(BF)
        cf_ref[pl.ds(pl.multiple_of(g * 16, 16), 16), :] = jnp.concatenate([z, z], 1)
        return carry

    lax.fori_loop(0, 64, one, 0)


def terms_kernel(x_ref, a_ref, cf_ref, o_ref, v_ref, q_ref, w_ref, stage_ref, ids_ref, sem):
    stage_ref[...] = x_ref[pl.ds(ASK - 1, DEVICES, stride=ASK), :].T[0:8].astype(I)
    copy = pltpu.make_async_copy(stage_ref, ids_ref, sem)
    copy.start()
    for k in range(3):
        for buf in range(2):
            v_ref[buf, k, pl.ds(40, 24), :] = jnp.zeros((24, 128), F)
    copy.wait()

    def number(i, e):
        return ids_ref[e % HALF, 2 * i + e // HALF]

    def stage1(i, buf):
        base = i * (2 * ASK)
        x, y, z = [
            jnp.concatenate(
                [x_ref[pl.ds(base + p * ASK + c * HALF, HALF), :] for p in range(2)], 0
            )
            for c in range(3)
        ]
        sq = x * x + y * y + z * z
        for f, value in enumerate((x, y, z, sq, jnp.ones_like(x))):
            for k, part in enumerate(split3(value)):
                v_ref[buf, k, pl.ds(f * 8, 8), :] = part
        for e in range(8):
            g = number(i, e)
            v = [v_ref[buf, k, pl.ds(e, 8, stride=8), :] for k in range(3)]
            b = jnp.concatenate([v[0], v[1], v[2], v[0], v[1], v[0], jnp.zeros((80, 128), F)], 0)
            a = a_ref[pl.ds(pl.multiple_of(g * 128, 128), 128), :]
            q_ref[buf, e] = jnp.dot(a, b.astype(BF), preferred_element_type=F)

    def stage2(buf):
        for e in range(8):
            m = jnp.maximum(q_ref[buf, e], TINY)
            q = m * lax.rsqrt(m)
            t = jnp.maximum(1.0 - q, 0.0)
            t = t * t
            w = (t * t) * (q + 0.25)
            high = w.astype(BF)
            w_ref[buf, e, 0:128, :] = high
            w_ref[buf, e, 128:256, :] = (w - high.astype(F)).astype(BF)

    def stage3(i, buf):
        base = pl.multiple_of(i * (2 * GIVE), 2 * GIVE)
        for e in range(8):
            g = number(i, e)
            c = cf_ref[pl.ds(pl.multiple_of(g * 16, 16), 16), :]
            r = jnp.dot(c, w_ref[buf, e], preferred_element_type=F)
            row = (e // HALF) * GIVE + e % HALF
            o_ref[pl.ds(base + row, 3, stride=HALF), :] = r[0:3] + r[3:6] + r[6:9]

    groups = DEVICES // 2
    stage1(0, 0)
    stage1(1, 1)
    stage2(0)

    def two(h, carry):
        i = 2 * h
        stage1(i + 2, 0)
        stage2(1)
        stage3(i, 0)
        stage1(i + 3, 1)
        stage2(0)
        stage3(i + 1, 1)
        return carry

    lax.fori_loop(0, groups // 2 - 1, two, 0)
    stage2(1)
    stage3(groups - 2, 0)
    stage3(groups - 1, 1)


def sum_kernel(where_ref, list_ref, node_ref, low_ref, high_ref, *refs):
    quarters, edges, acc_ref = refs[0:4], refs[4:8], refs[8]
    _, slot = slot_table(list_ref[...])
    acc = jnp.zeros((BOX_DEV, 384), F)
    for j in range(SLOTS):
        ref = (low_ref, high_ref)[j // HALF]
        sel = (slot == float(j)).astype(F).astype(BF)
        terms = jnp.concatenate(
            [ref[pl.ds(c * HALF + j % HALF, DEVICES, stride=GIVE), :] for c in range(3)], 1
        )
        for part in split3(terms):
            acc = acc + jnp.dot(sel, part.astype(BF), preferred_element_type=F)
    for c in range(3):
        acc_ref[c, 0:8, :] = jnp.zeros((8, 128), F)
        acc_ref[c, 64:72, :] = jnp.zeros((8, 128), F)
        acc_ref[c, HALO : HALO + BOX_DEV, :] = acc[:, c * 128 : (c + 1) * 128]
    surf = where_ref[0]
    for k, ref in enumerate(quarters):
        first = pl.multiple_of(((surf + k) & 3) * QUARTER, QUARTER)
        for c in range(3):
            ref[c * NEAR : (c + 1) * NEAR, :] = acc_ref[c, pl.ds(first, NEAR), :]
    zero = jnp.zeros((HALO, 128), F)
    d = [acc[:, c * 128 : (c + 1) * 128] for c in range(3)]
    x = [node_ref[c] for c in range(3)]
    head = jnp.concatenate([t[0:HALO] for t in d] + [zero] + [t[0:HALO] for t in x] + [zero], 0)
    tail = jnp.concatenate([t[60:64] for t in d] + [zero] + [t[60:64] for t in x] + [zero], 0)
    for k, ref in enumerate(edges):
        pick = jnp.where(surf == k, 1.0, 0.0)
        both = pick * tail + (1.0 - pick) * head
        ref[...] = both if k == 0 else both[0:16]


def face_kernel(where_ref, near_ref, node_ref, *refs):
    quarters, edges = refs[0:4], refs[4:8]
    face_ref, o_ref, tab_ref, cor_ref, x_ref, code_ref = refs[8:]
    surf = where_ref[0]
    first = pl.multiple_of(surf * QUARTER, QUARTER)
    origin = where_ref[1] * QUARTER - HALO
    is_low = jnp.where(surf == 0, 1.0, 0.0)
    is_high = jnp.where(surf == 3, 1.0, 0.0)
    d = quarters[0][...] + quarters[1][...] + quarters[2][...] + quarters[3][...]
    edge_d = edges[0][0:16] + edges[1][...] + edges[2][...] + edges[3][...]
    edge_x = edges[0][16:32]
    zero = jnp.zeros((QUARTER, 128), F)

    def placed(c, edge):
        part = edge[c * HALO : (c + 1) * HALO]
        return jnp.concatenate([is_low * part, zero, is_high * part], 0)

    mine = []
    for c in range(3):
        x_ref[c, 0:8, :] = jnp.zeros((8, 128), F)
        x_ref[c, 64:72, :] = jnp.zeros((8, 128), F)
        x_ref[c, HALO : HALO + BOX_DEV, :] = node_ref[c]
        disp = d[c * NEAR : (c + 1) * NEAR] + placed(c, edge_d)
        mine.append(disp[HALO : HALO + QUARTER])
        tab_ref[pl.ds(c, NEAR, stride=8), :] = x_ref[c, pl.ds(first, NEAR), :] + placed(c, edge_x)
        tab_ref[pl.ds(c + 3, NEAR, stride=8), :] = disp
    for c in (6, 7):
        tab_ref[pl.ds(c, NEAR, stride=8), :] = jnp.zeros((NEAR, 128), F)

    for k in range(3):
        for h in range(2):
            code_ref[pl.ds((k * 2 + h) * QUARTER, QUARTER), :] = face_ref[
                k, pl.ds(first, QUARTER), h * 128 : (h + 1) * 128
            ]

    def one_box(b, carry):
        box = first + b
        tables = []
        for j in range(8):
            at = near_ref[j, box] - origin
            tables.append(tab_ref[pl.ds(pl.multiple_of(at * 8, 8), 8), :])
        for h in range(2):
            for k in range(3):
                code = code_ref[pl.ds((k * 2 + h) * QUARTER + b, 1), :]
                code = jnp.broadcast_to(code, (8, 128))
                lane = code & 127
                which = code >> 7
                got = None
                for j in range(8):
                    value = jnp.take_along_axis(tables[j], lane, axis=1)
                    got = value if got is None else jnp.where(which == j, value, got)
                cor_ref[k, pl.ds(b * 2 + h, 8, stride=32), :] = got
        return carry

    lax.fori_loop(0, QUARTER, one_box, 0)

    def corner(k):
        part = [cor_ref[k, pl.ds(c * 32, 32), :] for c in range(6)]
        return [part[c] + 0.5 * part[c + 3] for c in range(3)], part[3:6]

    (ma, da), (mb, db), (mc, dc) = corner(0), corner(1), corner(2)
    u = [mb[c] - ma[c] for c in range(3)]
    w = [mc[c] - ma[c] for c in range(3)]
    swept = None
    for c in range(3):
        p, q = (c + 1) % 3, (c + 2) % 3
        normal = 0.5 * (u[p] * w[q] - u[q] * w[p])
        term = ((da[c] + db[c] + dc[c]) / 3.0) * normal
        swept = term if swept is None else swept + term
    for c in range(3):
        o_ref[c * 16 : (c + 1) * 16, :] = mine[c] * 2.0
    o_ref[48:80, :] = swept


def out_kernel(where_ref, own_ref, one_ref, two_ref, three_ref, v_ref, s_ref):
    surf = where_ref[0]
    for k, ref in enumerate((own_ref, one_ref, two_ref, three_ref)):
        first = pl.multiple_of(((surf + 4 - k) & 3) * QUARTER, QUARTER)
        for c in range(3):
            v_ref[c, pl.ds(first, QUARTER), :] = ref[c * 16 : (c + 1) * 16, :]
        for h in range(2):
            s_ref[pl.ds(first, QUARTER), h * 128 : (h + 1) * 128] = ref[
                pl.ds(48 + h, QUARTER, stride=2), :
            ]


def to_all(array):
    rows = array.shape[0] // DEVICES
    packets = array.reshape(DEVICES, rows, 1, 128)
    packets = lax.all_to_all(packets, BOTH, split_axis=0, concat_axis=0, tiled=True)
    return packets.reshape(DEVICES * rows, 128)


def around(arrays):
    return [
        lax.ppermute(a, "surf", [(i, (i + k) % 4) for i in range(4)])
        for k, a in zip((1, 2, 3), arrays)
    ]


def edge_pairs(k):
    up = [(v * 4 + k, (v + 1) * 4) for v in range(31)]
    down = [((v + 1) * 4 + (k + 1) % 4, v * 4 + 3) for v in range(31)]
    return up + down


def shape(*dims, kind=F):
    return jax.ShapeDtypeStruct(dims, kind)


def body(node_pos, centres, coefs, radii, block_list, neighbours, faces):
    listed = block_list[0].T
    nodes, cens, weights = [a.transpose(1, 0, 2) for a in (node_pos, centres, coefs)]
    surf = lax.axis_index("surf")
    where = jnp.stack([surf, lax.axis_index("vol") * 4 + surf]).astype(I)
    sent = call(
        prep_kernel,
        "prep",
        (shape(DEVICES * ASK, 128),) * 2,
        [("v", listed), ("v", nodes)],
    )
    tables = call(
        feat_kernel,
        "feats",
        (shape(64 * 128, 128, kind=BF), shape(64 * 16, 256, kind=BF)),
        [("v", cens), ("v", weights), ("v", radii)],
        us=10,
    )
    back = []
    for packet in sent:
        (terms,) = call(
            terms_kernel,
            "terms",
            (shape(DEVICES * GIVE, 128),),
            [("v", to_all(packet)), ("v", tables[0]), ("v", tables[1])],
            [
                pltpu.VMEM((2, 3, 64, 128), F),
                pltpu.VMEM((2, 8, 128, 128), F),
                pltpu.VMEM((2, 8, 256, 128), BF),
                pltpu.VMEM((8, 128), I),
                pltpu.SMEM((8, 128), I),
                pltpu.SemaphoreType.DMA,
            ],
            mib=16,
            us=30,
        )
        back.append(to_all(terms))
    own = call(
        sum_kernel,
        "sums",
        (shape(3 * NEAR, 128),) * 4 + (shape(32, 128),) + (shape(16, 128),) * 3,
        [("s", where), ("v", listed), ("v", nodes), ("v", back[0]), ("v", back[1])],
        [pltpu.VMEM((3, 72, 128), F)],
    )
    quarters = [own[0], *around(own[1:4])]
    edges = [lax.ppermute(own[4 + k], BOTH, edge_pairs(k)) for k in range(4)]
    (mine,) = call(
        face_kernel,
        "faces",
        (shape(80, 128),),
        [("s", where), ("s", neighbours.T), ("v", nodes)]
        + [("v", a) for a in quarters + edges]
        + [("v", faces.transpose(1, 0, 2))],
        [
            pltpu.VMEM((8 * NEAR, 128), F),
            pltpu.VMEM((3, 256, 128), F),
            pltpu.VMEM((3, 72, 128), F),
            pltpu.VMEM((96, 128), I),
        ],
    )
    velocity, swept = call(
        out_kernel,
        "outs",
        (shape(3, BOX_DEV, 128), shape(BOX_DEV, 256)),
        [("s", where), ("v", mine)] + [("v", r) for r in around([mine] * 3)],
    )
    return velocity.transpose(1, 0, 2), swept


def solution(mesh):
    placed = (
        P("vol", None, None),
        P(("vol", "surf"), None, None),
        P(("vol", "surf"), None, None),
        P(("vol", "surf"), None),
        P("surf", "vol", None),
        P("vol", None),
        P("vol", None, None),
    )
    return jax.shard_map(
        body,
        mesh=mesh,
        in_specs=placed,
        out_specs=(P("vol", None, None), P("vol", None)),
        check_vma=False,
    )
```

time: 186 us -> 169 us (0.909); the launches traced: 183 us -> 169 us
  starting transfers between devices: 26.9 us -> 47.5 us
  blocking collectives: 19.5 us -> 0 us
  Pallas kernels: 81.4 us -> 73 us
  local copies, waits for them, and re-layouts: 11.7 us -> 6.13 us
    all_to_all x2 -> x4, starting transfers between devices: 10.3 us -> 35.2 us  [to_all(): lax.all_to_all(packets, BOTH, split_axis=0, concat_axis=0, tiled=True)]
    all_to_all x1 -> x0, blocking collectives: 19.5 us -> none  [to_all(): return lax.all_to_all(array, BOTH, split_axis=0, concat_axis=0, tiled=True)]
    ppermute x2 -> x4, waiting for transfers between devices: 0.15 us -> 13.5 us  [body(): edges = [lax.ppermute(own[4 + k], BOTH, edge_pairs(k)) for k in range(4)]]
    all_to_all x2 -> x4, waiting for transfers between devices: 35.9 us -> 23 us  [to_all(): lax.all_to_all(packets, BOTH, split_axis=0, concat_axis=0, tiled=True)]
    pallas_call x7, Pallas kernels: 81.4 us -> 73 us  [call(): pl.pallas_call(kernel, name=name, out_shape=outs, in_specs=specs, out_spe...]
    unnamed x34 -> x24, local copies, waits for them, and re-layouts: 10.2 us -> 6.13 us
    ppermute x2 -> x4, starting transfers between devices: 9.77 us -> 6.39 us  [body(): edges = [lax.ppermute(own[4 + k], BOTH, edge_pairs(k)) for k in range(4)]]
  transfers between devices with their start and end apart: 10 -> 14, of which waited for: 8 -> 8; matrix products, arithmetic and copies ran while one was open for 2% -> 0% of each run, Pallas kernels for 5% -> 38%
where the time goes in v1:
time: 169 us
  Pallas kernels  73 us (43%)
  starting transfers between devices  47.5 us (28%)
  waiting for transfers between devices  41.2 us (24%)
  local copies, waits for them, and re-layouts  6.13 us (4%)
    pallas_call x7, Pallas kernels, call(): pl.pallas_call(kernel, name=name, out_shape=outs, in_specs=specs, out_spe...  73 us
    all_to_all x4, starting transfers between devices, to_all(): lax.all_to_all(packets, BOTH, split_axis=0, concat_axis=0, tiled=True)  35.2 us
    all_to_all x4, waiting for transfers between devices, to_all(): lax.all_to_all(packets, BOTH, split_axis=0, concat_axis=0, tiled=True)  23 us
    ppermute x4, waiting for transfers between devices, body(): edges = [lax.ppermute(own[4 + k], BOTH, edge_pairs(k)) for k in range(4)]  13.5 us
    ppermute x4, starting transfers between devices, body(): edges = [lax.ppermute(own[4 + k], BOTH, edge_pairs(k)) for k in range(4)]  6.39 us
    unnamed x24, local copies, waits for them, and re-layouts  6.13 us
    ppermute x6, starting transfers between devices, around(): lax.ppermute(a, 'surf', [(i, (i + k) % 4) for i in range(4)])  5.87 us
    ppermute x6, waiting for transfers between devices, around(): lax.ppermute(a, 'surf', [(i, (i + k) % 4) for i in range(4)])  4.66 us
  transfers between devices with their start and end apart: 14, of which 8 were waited for; matrix products, arithmetic and copies ran while one was open for 0% of the time, Pallas kernels for 38%

profile of v1, /device:TPU:8, one launch (start us, length us, event | category | flops | bytes accessed | tf_op | source)
XLA Modules:
  0.0 168.7 jit_solution(6777467258299974880)
XLA Ops:
  0.6 0.0 copy-start.3
  0.6 0.9 copy-done.3
  1.5 0.7 copy-done.6
  2.2 2.6 %prep.1 = (f32[1664,128]{1,0:T(8,128)}, f32[1664,128]{1,0:T(8,128)}) custom-call(s32[16,64]{1,0:T(8,128)S(1)} %bitcast.29, f32[3,64,128]{2,1,0:T(8,128)S(1)} %bitcast.26), custom_call_target="tpu_custom_call" | custom-call | flops 2000000000 | bytes 2000000 | tf_op jit(solution)/shard_map/prep/pallas_call | solution.py:30
  4.8 10.4 %all-to-all-start.2 = ((f32[128,13,1,128]{3,2,1,0:T(1,128)}), f32[128,13,1,128]{3,2,1,0:T(1,128)S(1)}, u32[]{:S(2)}, u32[]{:S(2)}) async-start(f32[128,13,1,128]{3,2,1,0:T(1,128)} %bitcast.13), calls=%async_computation.2 | async-start | bytes 1703936 | tf_op jit(solution)/shard_map/all_to_all | solution.py:296
  15.3 0.0 copy-done.1
  15.3 0.0 copy-done.2
  15.3 0.0 copy-done.5
  15.3 7.4 %feats.1 = (bf16[8192,128]{1,0:T(8,128)(2,1)S(1)}, bf16[1024,256]{1,0:T(8,128)(2,1)S(1)}) custom-call(f32[3,64,128]{2,1,0:T(8,128)S(1)} %bitcast.24, f32[3,64,128]{2,1,0:T(8,128)S(1)} %bitcast.25, f32[64,128]{1,0:T(8,128)S(1)} %copy-done.5), custom_call_target="tpu_custom_call" | custom-call | flops 10000000000 | bytes 10000000 | tf_op jit(solution)/shard_map/feats/pallas_call | solution.py:30
  22.8 0.0 copy-start.9
  22.8 1.4 copy-done.9
  24.1 7.5 %all-to-all-done.2 = f32[128,13,1,128]{3,2,1,0:T(1,128)S(1)} async-done(((f32[128,13,1,128]{3,2,1,0:T(1,128)}), f32[128,13,1,128]{3,2,1,0:T(1,128)S(1)}, u32[]{:S(2)}, u32[]{:S(2)}) %all-to-all-start.2) | async-done | bytes 852000 | tf_op jit(solution)/shard_map/all_to_all | solution.py:296
  31.6 5.1 %all-to-all-start = ((f32[128,13,1,128]{3,2,1,0:T(1,128)}), f32[128,13,1,128]{3,2,1,0:T(1,128)S(1)}, u32[]{:S(2)}, u32[]{:S(2)}) async-start(f32[128,13,1,128]{3,2,1,0:T(1,128)} %bitcast.7), calls=%async_computation | async-start | bytes 1703936 | tf_op jit(solution)/shard_map/all_to_all | solution.py:296
  36.7 0.0 copy-start.10
  36.7 1.6 copy-done.10
  38.3 28.4 %terms.3 = f32[1536,128]{1,0:T(8,128)} custom-call(f32[1664,128]{1,0:T(8,128)S(1)} %bitcast.19, bf16[8192,128]{1,0:T(8,128)(2,1)S(1)} %copy-done.10, bf16[1024,256]{1,0:T(8,128)(2,1)S(1)} %get-tuple-element.18.cf_ref), custom_call_target="tpu_custom_call" | custom-call | flops 30000001024 | bytes 30000000 | tf_op jit(solution)/shard_map/terms/pallas_call | solution.py:30
  66.7 0.0 all-to-all-done
  66.7 9.8 %all-to-all-start.3 = ((f32[128,12,1,128]{3,2,1,0:T(1,128)}), f32[128,12,1,128]{3,2,1,0:T(1,128)S(1)}, u32[]{:S(2)}, u32[]{:S(2)}) async-start(f32[128,12,1,128]{3,2,1,0:T(1,128)} %bitcast.15), calls=%async_computation.3 | async-start | bytes 1572864 | tf_op jit(solution)/shard_map/all_to_all | solution.py:296
  76.6 1.6 copy-done.11
  78.2 28.4 %terms.2 = f32[1536,128]{1,0:T(8,128)} custom-call(f32[1664,128]{1,0:T(8,128)S(1)} %bitcast.20, bf16[8192,128]{1,0:T(8,128)(2,1)S(1)} %copy-done.11, bf16[1024,256]{1,0:T(8,128)(2,1)S(1)} %get-tuple-element.18.cf_ref), custom_call_target="tpu_custom_call" | custom-call | flops 30000001024 | bytes 30000000 | tf_op jit(solution)/shard_map/terms/pallas_call | solution.py:30
  106.6 0.0 all-to-all-done.3
  106.6 9.8 %all-to-all-start.1 = ((f32[128,12,1,128]{3,2,1,0:T(1,128)}), f32[128,12,1,128]{3,2,1,0:T(1,128)S(1)}, u32[]{:S(2)}, u32[]{:S(2)}) async-start(f32[128,12,1,128]{3,2,1,0:T(1,128)} %bitcast.11), calls=%async_computation.1 | async-start | bytes 1572864 | tf_op jit(solution)/shard_map/all_to_all | solution.py:296
  116.5 0.1 pad_add_fusion.where_ref
  116.6 15.5 %all-to-all-done.1 = f32[128,12,1,128]{3,2,1,0:T(1,128)S(1)} async-done(((f32[128,12,1,128]{3,2,1,0:T(1,128)}), f32[128,12,1,128]{3,2,1,0:T(1,128)S(1)}, u32[]{:S(2)}, u32[]{:S(2)}) %all-to-all-start.1) | async-done | bytes 786464 | tf_op jit(solution)/shard_map/all_to_all | solution.py:296
  132.1 0.0 copy-done.4
  132.1 1.8 %sums.1 = (f32[72,128]{1,0:T(8,128)S(1)}, f32[72,128]{1,0:T(8,128)S(1)}, f32[72,128]{1,0:T(8,128)S(1)}, f32[72,128]{1,0:T(8,128)S(1)}, f32[32,128]{1,0:T(8,128)S...) custom-call(s32[2]{0:T(128)S(1)} %pad_add_fusion.where_ref, s32[16,64]{1,0:T(8,128)S(1)} %bitcast.30, ...), custom_call_target="tpu_custom_call" | custom-call | flops 2000000000 | bytes 2000000 | tf_op jit(solution)/shard_map/sums/pallas_call | solution.py:30
  133.9 0.9 collective-permute-start
  134.7 1.5 collective-permute-start.1
  136.3 1.4 collective-permute-start.2
  137.7 1.3 collective-permute-start.4
  138.9 1.3 collective-permute-start.5
  140.2 5.4 %collective-permute-done.4.refs_5_ = f32[16,128]{1,0:T(8,128)S(1)} collective-permute-done((f32[16,128]{1,0:T(8,128)S(1)}, f32[16,128]{1,0:T(8,128)S(1)}, u32[]{:S(2)}, u32[]{:S(2)}) %collective-permute-start.4) | collective-permute-done | bytes 8224 | tf_op jit(solution)/shard_map/ppermute | solution.py:362
  145.6 1.9 %collective-permute-start.3 = (f32[32,128]{1,0:T(8,128)S(1)}, f32[32,128]{1,0:T(8,128)S(1)}, u32[]{:S(2)}, u32[]{:S(2)}) collective-permute-start(f32[32,128]{1,0:T(8,128)S(1)} %get-tuple-element.24), channel_id=1, source_target_pairs={{0,4},{4,8},{8,12},{12,16},{16,20},{20,24},{24,28},{28,32},{32,36}... | collective-permute-start | bytes 49160 | tf_op jit(solution)/shard_map/ppermute | solution.py:362
  147.5 0.9 collective-permute-done.5.refs_6_
  148.4 1.9 %collective-permute-start.6 = (f32[16,128]{1,0:T(8,128)S(1)}, f32[16,128]{1,0:T(8,128)S(1)}, u32[]{:S(2)}, u32[]{:S(2)}) collective-permute-start(f32[16,128]{1,0:T(8,128)S(1)} %get-tuple-element.27), channel_id=1, source_target_pairs={{3,4},{7,8},{11,12},{15,16},{19,20},{23,24},{27,28},{31,32},{35,36... | collective-permute-start | bytes 24584 | tf_op jit(solution)/shard_map/ppermute | solution.py:362
  150.3 7.3 %collective-permute-done.6.refs_7_ = f32[16,128]{1,0:T(8,128)S(1)} collective-permute-done((f32[16,128]{1,0:T(8,128)S(1)}, f32[16,128]{1,0:T(8,128)S(1)}, u32[]{:S(2)}, u32[]{:S(2)}) %collective-permute-start.6) | collective-permute-done | bytes 8224 | tf_op jit(solution)/shard_map/ppermute | solution.py:362
  157.6 0.0 collective-permute-done.3.refs_4_
  157.6 0.0 collective-permute-done.refs_1_
  157.6 0.0 collective-permute-done.1.refs_2_
  157.6 0.0 collective-permute-done.2.refs_3_
  157.7 3.1 %faces.1.own_ref = f32[80,128]{1,0:T(8,128)S(1)} custom-call(s32[2]{0:T(128)S(1)} %pad_add_fusion.where_ref, s32[8,64]{1,0:T(8,128)S(1)} %bitcast.31, f32[3,64,128]{2,1,0:T(8,128)S(1)} %bitcast.28, f32[72,128]{1,0:T(8,128)S(1)} %get-tuple-element.20.refs_0_, f32[72,128]{1,0:T(8,128)S(1)} %collective-permute-done.refs_1_, ...), custom_call_target="tpu_custom_call" | custom-call | flops 2000000000 | bytes 2000000 | tf_op jit(solution)/shard_map/faces/pallas_call | solution.py:30
  160.7 0.1 collective-permute-start.9
  160.8 0.1 collective-permute-start.8
  160.9 1.9 %collective-permute-start.7 = (f32[80,128]{1,0:T(8,128)S(1)}, f32[80,128]{1,0:T(8,128)S(1)}, u32[]{:S(2)}, u32[]{:S(2)}) collective-permute-start(f32[80,128]{1,0:T(8,128)S(1)} %faces.1.own_ref), channel_id=1, source_target_pairs={{0,1},{1,2},{2,3},{3,0},{4,5},{5,6},{6,7},{7,4},{8,9},{9,10},{10,1... | collective-permute-start | bytes 122888 | tf_op jit(solution)/shard_map/ppermute | solution.py:302
  162.8 2.0 %collective-permute-done.9.three_ref = f32[80,128]{1,0:T(8,128)S(1)} collective-permute-done((f32[80,128]{1,0:T(8,128)S(1)}, f32[80,128]{1,0:T(8,128)S(1)}, u32[]{:S(2)}, u32[]{:S(2)}) %collective-permute-start.9) | collective-permute-done | bytes 40992 | tf_op jit(solution)/shard_map/ppermute | solution.py:302
  164.8 1.6 collective-permute-done.8.two_ref
  166.4 1.1 collective-permute-done.7.one_ref
  167.5 1.2 outs.1
  (12 shorter events, 0.0 us)
Async XLA Ops:
  0.6 0.9 copy-start.3
  1.5 0.7 copy-start.6
  2.2 13.1 %copy-start.1 = (f32[64,3,128]{2,0,1:T(8,128)S(1)}, f32[64,3,128]{2,0,1:T(8,128)}, u32[]{:S(2)}) copy-start(f32[64,3,128]{2,0,1:T(8,128)} %param.8) | copy-start | bytes 294916
  2.2 13.1 %copy-start.2 = (f32[64,3,128]{2,0,1:T(8,128)S(1)}, f32[64,3,128]{2,0,1:T(8,128)}, u32[]{:S(2)}) copy-start(f32[64,3,128]{2,0,1:T(8,128)} %param.9) | copy-start | bytes 294916
  2.2 13.1 %copy-start.5 = (f32[64,128]{1,0:T(8,128)S(1)}, f32[64,128]{1,0:T(8,128)}, u32[]{:S(2)}) copy-start(f32[64,128]{1,0:T(8,128)} %rad_ref.1) | copy-start | bytes 98308
  4.8 26.8 %all-to-all-start.2 = ((f32[128,13,1,128]{3,2,1,0:T(1,128)}), f32[128,13,1,128]{3,2,1,0:T(1,128)S(1)}, u32[]{:S(2)}, u32[]{:S(2)}) async-start(f32[128,13,1,128]{3,2,1,0:T(1,128)} %bitcast.13), calls=%async_computation.2 | async-start | bytes 1703936 | tf_op jit(solution)/shard_map/all_to_all | solution.py:296
  22.8 1.4 copy-start.9
  31.6 35.2 %all-to-all-start = ((f32[128,13,1,128]{3,2,1,0:T(1,128)}), f32[128,13,1,128]{3,2,1,0:T(1,128)S(1)}, u32[]{:S(2)}, u32[]{:S(2)}) async-start(f32[128,13,1,128]{3,2,1,0:T(1,128)} %bitcast.7), calls=%async_computation | async-start | bytes 1703936 | tf_op jit(solution)/shard_map/all_to_all | solution.py:296
  36.7 1.6 copy-start.10
  66.7 39.9 %all-to-all-start.3 = ((f32[128,12,1,128]{3,2,1,0:T(1,128)}), f32[128,12,1,128]{3,2,1,0:T(1,128)S(1)}, u32[]{:S(2)}, u32[]{:S(2)}) async-start(f32[128,12,1,128]{3,2,1,0:T(1,128)} %bitcast.15), calls=%async_computation.3 | async-start | bytes 1572864 | tf_op jit(solution)/shard_map/all_to_all | solution.py:296
  76.6 1.6 copy-start.11
  78.2 53.9 %copy-start.4 = (f32[64,3,128]{2,0,1:T(8,128)S(1)}, f32[64,3,128]{2,0,1:T(8,128)}, u32[]{:S(2)}) copy-start(f32[64,3,128]{2,0,1:T(8,128)} %param.7) | copy-start | bytes 294916
  78.2 53.9 %copy-start.7 = (s32[1,64,16]{1,2,0:T(8,128)S(1)}, s32[1,64,16]{1,2,0:T(8,128)}, u32[]{:S(2)}) copy-start(s32[1,64,16]{1,2,0:T(8,128)} %param.11) | copy-start | bytes 12292
  106.6 25.4 %all-to-all-start.1 = ((f32[128,12,1,128]{3,2,1,0:T(1,128)}), f32[128,12,1,128]{3,2,1,0:T(1,128)S(1)}, u32[]{:S(2)}, u32[]{:S(2)}) async-start(f32[128,12,1,128]{3,2,1,0:T(1,128)} %bitcast.11), calls=%async_computation.1 | async-start | bytes 1572864 | tf_op jit(solution)/shard_map/all_to_all | solution.py:296
  132.1 25.6 %copy-start = (s32[64,3,256]{2,0,1:T(8,128)S(1)}, s32[64,3,256]{2,0,1:T(8,128)}, u32[]{:S(2)}) copy-start(s32[64,3,256]{2,0,1:T(8,128)} %param.13) | copy-start | bytes 589828
  132.1 25.6 %copy-start.8 = (s32[64,8]{0,1:T(8,128)S(1)}, s32[64,8]{0,1:T(8,128)}, u32[]{:S(2)}) copy-start(s32[64,8]{0,1:T(8,128)} %param.12) | copy-start | bytes 6148
  133.9 23.7 %collective-permute-start = (f32[72,128]{1,0:T(8,128)S(1)}, f32[72,128]{1,0:T(8,128)S(1)}, u32[]{:S(2)}, u32[]{:S(2)}) collective-permute-start(f32[72,128]{1,0:T(8,128)S(1)} %get-tuple-element.21), channel_id=1, source_target_pairs={{0,1},{1,2},{2,3},{3,0},{4,5},{5,6},{6,7},{7,4},{8,9},{9,10},{10,1... | collective-permute-start | bytes 110600 | tf_op jit(solution)/shard_map/ppermute | solution.py:302
  134.7 22.9 %collective-permute-start.1 = (f32[72,128]{1,0:T(8,128)S(1)}, f32[72,128]{1,0:T(8,128)S(1)}, u32[]{:S(2)}, u32[]{:S(2)}) collective-permute-start(f32[72,128]{1,0:T(8,128)S(1)} %get-tuple-element.22), channel_id=1, source_target_pairs={{0,2},{1,3},{2,0},{3,1},{4,6},{5,7},{6,4},{7,5},{8,10},{9,11},{10,... | collective-permute-start | bytes 110600 | tf_op jit(solution)/shard_map/ppermute | solution.py:302
  136.3 21.3 %collective-permute-start.2 = (f32[72,128]{1,0:T(8,128)S(1)}, f32[72,128]{1,0:T(8,128)S(1)}, u32[]{:S(2)}, u32[]{:S(2)}) collective-permute-start(f32[72,128]{1,0:T(8,128)S(1)} %get-tuple-element.23), channel_id=1, source_target_pairs={{0,3},{1,0},{2,1},{3,2},{4,7},{5,4},{6,5},{7,6},{8,11},{9,8},{10,9... | collective-permute-start | bytes 110600 | tf_op jit(solution)/shard_map/ppermute | solution.py:302
  137.7 8.0 %collective-permute-start.4 = (f32[16,128]{1,0:T(8,128)S(1)}, f32[16,128]{1,0:T(8,128)S(1)}, u32[]{:S(2)}, u32[]{:S(2)}) collective-permute-start(f32[16,128]{1,0:T(8,128)S(1)} %get-tuple-element.25), channel_id=1, source_target_pairs={{1,4},{5,8},{9,12},{13,16},{17,20},{21,24},{25,28},{29,32},{33,36}... | collective-permute-start | bytes 24584 | tf_op jit(solution)/shard_map/ppermute | solution.py:362
  138.9 9.5 %collective-permute-start.5 = (f32[16,128]{1,0:T(8,128)S(1)}, f32[16,128]{1,0:T(8,128)S(1)}, u32[]{:S(2)}, u32[]{:S(2)}) collective-permute-start(f32[16,128]{1,0:T(8,128)S(1)} %get-tuple-element.26), channel_id=1, source_target_pairs={{2,4},{6,8},{10,12},{14,16},{18,20},{22,24},{26,28},{30,32},{34,36... | collective-permute-start | bytes 24584 | tf_op jit(solution)/shard_map/ppermute | solution.py:362
  145.6 12.0 %collective-permute-start.3 = (f32[32,128]{1,0:T(8,128)S(1)}, f32[32,128]{1,0:T(8,128)S(1)}, u32[]{:S(2)}, u32[]{:S(2)}) collective-permute-start(f32[32,128]{1,0:T(8,128)S(1)} %get-tuple-element.24), channel_id=1, source_target_pairs={{0,4},{4,8},{8,12},{12,16},{16,20},{20,24},{24,28},{28,32},{32,36}... | collective-permute-start | bytes 49160 | tf_op jit(solution)/shard_map/ppermute | solution.py:362
  148.4 9.2 %collective-permute-start.6 = (f32[16,128]{1,0:T(8,128)S(1)}, f32[16,128]{1,0:T(8,128)S(1)}, u32[]{:S(2)}, u32[]{:S(2)}) collective-permute-start(f32[16,128]{1,0:T(8,128)S(1)} %get-tuple-element.27), channel_id=1, source_target_pairs={{3,4},{7,8},{11,12},{15,16},{19,20},{23,24},{27,28},{31,32},{35,36... | collective-permute-start | bytes 24584 | tf_op jit(solution)/shard_map/ppermute | solution.py:362
  160.7 4.1 %collective-permute-start.9 = (f32[80,128]{1,0:T(8,128)S(1)}, f32[80,128]{1,0:T(8,128)S(1)}, u32[]{:S(2)}, u32[]{:S(2)}) collective-permute-start(f32[80,128]{1,0:T(8,128)S(1)} %faces.1.own_ref), channel_id=1, source_target_pairs={{0,3},{1,0},{2,1},{3,2},{4,7},{5,4},{6,5},{7,6},{8,11},{9,8},{10,9... | collective-permute-start | bytes 122888 | tf_op jit(solution)/shard_map/ppermute | solution.py:302
  160.8 5.6 %collective-permute-start.8 = (f32[80,128]{1,0:T(8,128)S(1)}, f32[80,128]{1,0:T(8,128)S(1)}, u32[]{:S(2)}, u32[]{:S(2)}) collective-permute-start(f32[80,128]{1,0:T(8,128)S(1)} %faces.1.own_ref), channel_id=1, source_target_pairs={{0,2},{1,3},{2,0},{3,1},{4,6},{5,7},{6,4},{7,5},{8,10},{9,11},{10,... | collective-permute-start | bytes 122888 | tf_op jit(solution)/shard_map/ppermute | solution.py:302
  160.9 6.6 %collective-permute-start.7 = (f32[80,128]{1,0:T(8,128)S(1)}, f32[80,128]{1,0:T(8,128)S(1)}, u32[]{:S(2)}, u32[]{:S(2)}) collective-permute-start(f32[80,128]{1,0:T(8,128)S(1)} %faces.1.own_ref), channel_id=1, source_target_pairs={{0,1},{1,2},{2,3},{3,0},{4,5},{5,6},{6,7},{7,4},{8,9},{9,10},{10,1... | collective-permute-start | bytes 122888 | tf_op jit(solution)/shard_map/ppermute | solution.py:302

commit v2 on v1

--- a/solution.py
+++ b/solution.py
@@ -13,9 +13,9 @@
 BOTH = ("vol", "surf")
 DEVICES = 128
 SLOTS = 8
-HALF = 4
-ASK = 3 * HALF + 1
-GIVE = 3 * HALF
+ASK = 3 * SLOTS + 1
+GIVE = 3 * SLOTS
+UNROLL = 8
 BOX_DEV = 64
 QUARTER = 16
 HALO = 4
@@ -64,22 +64,21 @@
     return table, jnp.where(used, rank, -1.0)
 
 
-def prep_kernel(list_ref, node_ref, low_ref, high_ref):
+def prep_kernel(list_ref, node_ref, o_ref):
     table, slot = slot_table(list_ref[...])
     slot_t = slot.T
     nodes = jnp.concatenate([node_ref[c] for c in range(3)], 1)
     parts = [p.astype(BF) for p in split3(nodes)]
-    for half, ref in enumerate((low_ref, high_ref)):
-        ids = []
-        for j in range(HALF):
-            at = float(half * HALF + j)
-            ids.append(jnp.sum(jnp.where(slot == at, table - 1.0, 0.0), axis=0, keepdims=True))
-            sel = (slot_t == at).astype(F).astype(BF)
-            got = sum(jnp.dot(sel, p, preferred_element_type=F) for p in parts)
-            for c in range(3):
-                ref[pl.ds(c * HALF + j, DEVICES, stride=ASK), :] = got[:, c * 128 : (c + 1) * 128]
-        stacked = jnp.concatenate(ids + [jnp.zeros((128 - HALF, 128), F)], 0).T
-        ref[pl.ds(ASK - 1, DEVICES, stride=ASK), :] = stacked
+    ids = []
+    for j in range(SLOTS):
+        at = float(j)
+        ids.append(jnp.sum(jnp.where(slot == at, table - 1.0, 0.0), axis=0, keepdims=True))
+        sel = (slot_t == at).astype(F).astype(BF)
+        got = sum(jnp.dot(sel, p, preferred_element_type=F) for p in parts)
+        for c in range(3):
+            o_ref[pl.ds(c * SLOTS + j, DEVICES, stride=ASK), :] = got[:, c * 128 : (c + 1) * 128]
+    stacked = jnp.concatenate(ids + [jnp.zeros((128 - SLOTS, 128), F)], 0).T
+    o_ref[pl.ds(ASK - 1, DEVICES, stride=ASK), :] = stacked
 
 
 def feat_kernel(cen_ref, coef_ref, rad_ref, a_ref, cf_ref):
@@ -100,87 +99,88 @@
     lax.fori_loop(0, 64, one, 0)
 
 
-def terms_kernel(x_ref, a_ref, cf_ref, o_ref, v_ref, q_ref, w_ref, stage_ref, ids_ref, sem):
-    stage_ref[...] = x_ref[pl.ds(ASK - 1, DEVICES, stride=ASK), :].T[0:8].astype(I)
+def terms_kernel(x_ref, a_ref, cf_ref, o_ref, v_ref, b_ref, q_ref, w_ref, stage_ref, ids_ref, sem):
+    stage_ref[...] = x_ref[pl.ds(ASK - 1, DEVICES, stride=ASK), :].T[0:SLOTS].astype(I)
     copy = pltpu.make_async_copy(stage_ref, ids_ref, sem)
     copy.start()
-    for k in range(3):
-        for buf in range(2):
-            v_ref[buf, k, pl.ds(40, 24), :] = jnp.zeros((24, 128), F)
+    for buf in range(2):
+        for j in range(SLOTS):
+            b_ref[buf, j, 48:128, :] = jnp.zeros((80, 128), BF)
+        for k in range(3):
+            v_ref[buf, k, pl.ds(32, 32), :] = jnp.zeros((32, 128), F)
+        v_ref[buf, 0, pl.ds(32, 8), :] = jnp.ones((8, 128), F)
     copy.wait()
 
-    def number(i, e):
-        return ids_ref[e % HALF, 2 * i + e // HALF]
-
-    def stage1(i, buf):
-        base = i * (2 * ASK)
-        x, y, z = [
-            jnp.concatenate(
-                [x_ref[pl.ds(base + p * ASK + c * HALF, HALF), :] for p in range(2)], 0
-            )
-            for c in range(3)
-        ]
-        sq = x * x + y * y + z * z
-        for f, value in enumerate((x, y, z, sq, jnp.ones_like(x))):
-            for k, part in enumerate(split3(value)):
+    def stage0(i, buf):
+        base = jnp.minimum(i, DEVICES - 1) * ASK
+        x, y, z = [x_ref[pl.ds(base + c * SLOTS, SLOTS), :] for c in range(3)]
+        for f, value in enumerate((x, y, z, x * x + y * y + z * z)):
+            first = value.astype(BF).astype(F)
+            rest = value - first
+            second = rest.astype(BF).astype(F)
+            for k, part in enumerate((first, second, rest - second)):
                 v_ref[buf, k, pl.ds(f * 8, 8), :] = part
-        for e in range(8):
-            g = number(i, e)
-            v = [v_ref[buf, k, pl.ds(e, 8, stride=8), :] for k in range(3)]
-            b = jnp.concatenate([v[0], v[1], v[2], v[0], v[1], v[0], jnp.zeros((80, 128), F)], 0)
-            a = a_ref[pl.ds(pl.multiple_of(g * 128, 128), 128), :]
-            q_ref[buf, e] = jnp.dot(a, b.astype(BF), preferred_element_type=F)
-
-    def stage2(buf):
-        for e in range(8):
-            m = jnp.maximum(q_ref[buf, e], TINY)
-            q = m * lax.rsqrt(m)
-            t = jnp.maximum(1.0 - q, 0.0)
-            t = t * t
-            w = (t * t) * (q + 0.25)
-            high = w.astype(BF)
-            w_ref[buf, e, 0:128, :] = high
-            w_ref[buf, e, 128:256, :] = (w - high.astype(F)).astype(BF)
-
-    def stage3(i, buf):
-        base = pl.multiple_of(i * (2 * GIVE), 2 * GIVE)
-        for e in range(8):
-            g = number(i, e)
-            c = cf_ref[pl.ds(pl.multiple_of(g * 16, 16), 16), :]
-            r = jnp.dot(c, w_ref[buf, e], preferred_element_type=F)
-            row = (e // HALF) * GIVE + e % HALF
-            o_ref[pl.ds(base + row, 3, stride=HALF), :] = r[0:3] + r[3:6] + r[6:9]
-
-    groups = DEVICES // 2
-    stage1(0, 0)
-    stage1(1, 1)
-    stage2(0)
-
-    def two(h, carry):
-        i = 2 * h
-        stage1(i + 2, 0)
-        stage2(1)
-        stage3(i, 0)
-        stage1(i + 3, 1)
-        stage2(0)
-        stage3(i + 1, 1)
+        for j in range(SLOTS):
+            v = [v_ref[buf, k, pl.ds(j, 8, stride=8), :] for k in range(3)]
+            b_ref[buf, j, 0:48, :] = jnp.concatenate(
+                [v[0], v[1], v[2], v[0], v[1], v[0]], 0
+            ).astype(BF)
+
+    def stage1(i, buf, j):
+        g = ids_ref[j, jnp.minimum(i, DEVICES - 1)]
+        a = a_ref[pl.ds(pl.multiple_of(g * 128, 128), 128), :]
+        q_ref[buf, j] = jnp.dot(a, b_ref[buf, j], preferred_element_type=F)
+
+    def stage2(buf, j):
+        m = jnp.maximum(q_ref[buf, j], TINY)
+        q = m * lax.rsqrt(m)
+        t = jnp.maximum(1.0 - q, 0.0)
+        t = t * t
+        w = (t * t) * (q + 0.25)
+        high = w.astype(BF)
+        w_ref[buf, j, 0:128, :] = high
+        w_ref[buf, j, 128:256, :] = (w - high.astype(F)).astype(BF)
+
+    def stage3(i, buf, j):
+        base = pl.multiple_of(i * GIVE, GIVE)
+        g = ids_ref[j, i]
+        c = cf_ref[pl.ds(pl.multiple_of(g * 16, 16), 16), :]
+        r = jnp.dot(c, w_ref[buf, j], preferred_element_type=F)
+        o_ref[pl.ds(base + j, 3, stride=SLOTS), :] = r[0:3] + r[3:6] + r[6:9]
+
+    slots = range(SLOTS)
+    stage0(0, 0)
+    stage0(1, 1)
+    for j in slots:
+        stage1(0, 0, j)
+    stage0(2, 0)
+    for j in slots:
+        stage1(1, 1, j)
+    for j in slots:
+        stage2(0, j)
+
+    def some(h, carry):
+        for u in range(UNROLL):
+            i = h * UNROLL + u
+            buf = u % 2
+            for j in slots:
+                stage1(i + 2, buf, j)
+                stage2(1 - buf, j)
+                stage3(i, buf, j)
+            stage0(i + 3, 1 - buf)
         return carry
 
-    lax.fori_loop(0, groups // 2 - 1, two, 0)
-    stage2(1)
-    stage3(groups - 2, 0)
-    stage3(groups - 1, 1)
-
-
-def sum_kernel(where_ref, list_ref, node_ref, low_ref, high_ref, *refs):
+    lax.fori_loop(0, DEVICES // UNROLL, some, 0)
+
+
+def sum_kernel(where_ref, list_ref, node_ref, back_ref, *refs):
     quarters, edges, acc_ref = refs[0:4], refs[4:8], refs[8]
     _, slot = slot_table(list_ref[...])
     acc = jnp.zeros((BOX_DEV, 384), F)
     for j in range(SLOTS):
-        ref = (low_ref, high_ref)[j // HALF]
         sel = (slot == float(j)).astype(F).astype(BF)
         terms = jnp.concatenate(
-            [ref[pl.ds(c * HALF + j % HALF, DEVICES, stride=GIVE), :] for c in range(3)], 1
+            [back_ref[pl.ds(c * SLOTS + j, DEVICES, stride=GIVE), :] for c in range(3)], 1
         )
         for part in split3(terms):
             acc = acc + jnp.dot(sel, part.astype(BF), preferred_element_type=F)
@@ -319,10 +319,10 @@
     nodes, cens, weights = [a.transpose(1, 0, 2) for a in (node_pos, centres, coefs)]
     surf = lax.axis_index("surf")
     where = jnp.stack([surf, lax.axis_index("vol") * 4 + surf]).astype(I)
-    sent = call(
+    (sent,) = call(
         prep_kernel,
         "prep",
-        (shape(DEVICES * ASK, 128),) * 2,
+        (shape(DEVICES * ASK, 128),),
         [("v", listed), ("v", nodes)],
     )
     tables = call(
@@ -332,30 +332,28 @@
         [("v", cens), ("v", weights), ("v", radii)],
         us=10,
     )
-    back = []
-    for packet in sent:
-        (terms,) = call(
-            terms_kernel,
-            "terms",
-            (shape(DEVICES * GIVE, 128),),
-            [("v", to_all(packet)), ("v", tables[0]), ("v", tables[1])],
-            [
-                pltpu.VMEM((2, 3, 64, 128), F),
-                pltpu.VMEM((2, 8, 128, 128), F),
-                pltpu.VMEM((2, 8, 256, 128), BF),
-                pltpu.VMEM((8, 128), I),
-                pltpu.SMEM((8, 128), I),
-                pltpu.SemaphoreType.DMA,
-            ],
-            mib=16,
-            us=30,
-        )
-        back.append(to_all(terms))
+    (terms,) = call(
+        terms_kernel,
+        "terms",
+        (shape(DEVICES * GIVE, 128),),
+        [("v", to_all(sent)), ("v", tables[0]), ("v", tables[1])],
+        [
+            pltpu.VMEM((2, 3, 64, 128), F),
+            pltpu.VMEM((2, SLOTS, 128, 128), BF),
+            pltpu.VMEM((2, SLOTS, 128, 128), F),
+            pltpu.VMEM((2, SLOTS, 256, 128), BF),
+            pltpu.VMEM((SLOTS, 128), I),
+            pltpu.SMEM((SLOTS, 128), I),
+            pltpu.SemaphoreType.DMA,
+        ],
+        mib=16,
+        us=45,
+    )
     own = call(
         sum_kernel,
         "sums",
         (shape(3 * NEAR, 128),) * 4 + (shape(32, 128),) + (shape(16, 128),) * 3,
-        [("s", where), ("v", listed), ("v", nodes), ("v", back[0]), ("v", back[1])],
+        [("s", where), ("v", listed), ("v", nodes), ("v", to_all(terms))],
         [pltpu.VMEM((3, 72, 128), F)],
     )
     quarters = [own[0], *around(own[1:4])]

time: 169 us -> 147 us (0.87)
  starting transfers between devices: 47.5 us -> 27.7 us
  Pallas kernels: 73 us -> 56 us
  waiting for transfers between devices: 41.2 us -> 57.7 us
    all_to_all x4 -> x2, starting transfers between devices: 35.2 us -> 15.5 us  [to_all(): lax.all_to_all(packets, BOTH, split_axis=0, concat_axis=0, tiled=True)]
    pallas_call x7 -> x6, Pallas kernels: 73 us -> 56 us  [call(): pl.pallas_call(kernel, name=name, out_shape=outs, in_specs=specs, out_spe...]
    all_to_all x4 -> x2, waiting for transfers between devices: 23 us -> 39.6 us  [to_all(): lax.all_to_all(packets, BOTH, split_axis=0, concat_axis=0, tiled=True)]
    unnamed x24 -> x22, local copies, waits for them, and re-layouts: 6.13 us -> 4.53 us
  transfers between devices with their start and end apart: 14 -> 12, of which waited for: 8 -> 8; matrix products, arithmetic and copies ran while one was open for 0% -> 0% of each run, Pallas kernels for 38% -> 5%
where the time goes in v2:
time: 147 us
  waiting for transfers between devices  57.7 us (39%)
  Pallas kernels  56 us (38%)
  starting transfers between devices  27.7 us (19%)
  local copies, waits for them, and re-layouts  4.53 us (3%)
    pallas_call x6, Pallas kernels, call(): pl.pallas_call(kernel, name=name, out_shape=outs, in_specs=specs, out_spe...  56 us
    all_to_all x2, waiting for transfers between devices, to_all(): lax.all_to_all(packets, BOTH, split_axis=0, concat_axis=0, tiled=True)  39.6 us
    all_to_all x2, starting transfers between devices, to_all(): lax.all_to_all(packets, BOTH, split_axis=0, concat_axis=0, tiled=True)  15.5 us
    ppermute x4, waiting for transfers between devices, body(): edges = [lax.ppermute(own[4 + k], BOTH, edge_pairs(k)) for k in range(4)]  13.4 us
    ppermute x4, starting transfers between devices, body(): edges = [lax.ppermute(own[4 + k], BOTH, edge_pairs(k)) for k in range(4)]  6.48 us
    ppermute x6, starting transfers between devices, around(): lax.ppermute(a, 'surf', [(i, (i + k) % 4) for i in range(4)])  5.75 us
    ppermute x6, waiting for transfers between devices, around(): lax.ppermute(a, 'surf', [(i, (i + k) % 4) for i in range(4)])  4.66 us
    unnamed x22, local copies, waits for them, and re-layouts  4.53 us
  transfers between devices with their start and end apart: 12, of which 8 were waited for; matrix products, arithmetic and copies ran while one was open for 0% of the time, Pallas kernels for 5%

profile of v2, /device:TPU:8, one launch (start us, length us, event | category | flops | bytes accessed | tf_op | source)
XLA Modules:
  0.0 146.9 jit_solution(4478452738602289758)
XLA Ops:
  0.6 0.0 copy-start.3
  0.6 0.9 copy-done.3
  1.5 0.0 copy-start.6
  1.5 0.7 copy-done.6
  2.2 2.7 %prep.1 = f32[3200,128]{1,0:T(8,128)} custom-call(s32[16,64]{1,0:T(8,128)S(1)} %bitcast.25, f32[3,64,128]{2,1,0:T(8,128)S(1)} %bitcast.22), custom_call_target="tpu_custom_call" | custom-call | flops 2000000000 | bytes 2000000 | tf_op jit(solution)/shard_map/prep/pallas_call | solution.py:30
  4.9 0.0 copy-start.1
  4.9 10.4 %all-to-all-start = ((f32[128,25,1,128]{3,2,1,0:T(1,128)}), f32[128,25,1,128]{3,2,1,0:T(1,128)S(1)}, u32[]{:S(2)}, u32[]{:S(2)}) async-start(f32[128,25,1,128]{3,2,1,0:T(1,128)} %bitcast.7), calls=%async_computation | async-start | bytes 3276800 | tf_op jit(solution)/shard_map/all_to_all | solution.py:296
  15.4 0.0 copy-done.1
  15.4 0.0 copy-done.2
  15.4 0.0 copy-done.5
  15.4 7.4 %feats.1 = (bf16[8192,128]{1,0:T(8,128)(2,1)S(1)}, bf16[1024,256]{1,0:T(8,128)(2,1)S(1)}) custom-call(f32[3,64,128]{2,1,0:T(8,128)S(1)} %bitcast.20, f32[3,64,128]{2,1,0:T(8,128)S(1)} %bitcast.21, f32[64,128]{1,0:T(8,128)S(1)} %copy-done.5), custom_call_target="tpu_custom_call" | custom-call | flops 10000000000 | bytes 10000000 | tf_op jit(solution)/shard_map/feats/pallas_call | solution.py:30
  22.8 0.0 copy-start.9
  22.9 1.3 copy-done.9
  24.2 15.8 %all-to-all-done = f32[128,25,1,128]{3,2,1,0:T(1,128)S(1)} async-done(((f32[128,25,1,128]{3,2,1,0:T(1,128)}), f32[128,25,1,128]{3,2,1,0:T(1,128)S(1)}, u32[]{:S(2)}, u32[]{:S(2)}) %all-to-all-start) | async-done | bytes 1638432 | tf_op jit(solution)/shard_map/all_to_all | solution.py:296
  39.9 1.6 %copy-done.10 = bf16[8192,128]{1,0:T(8,128)(2,1)S(1)} copy-done((bf16[8192,128]{1,0:T(8,128)(2,1)S(1)}, bf16[8192,128]{1,0:T(8,128)(2,1)}, u32[]{:S(2)}) %copy-start.10) | copy-done | bytes 2097176
  41.5 39.6 %terms.1 = f32[3072,128]{1,0:T(8,128)} custom-call(f32[3200,128]{1,0:T(8,128)S(1)} %bitcast.17, bf16[8192,128]{1,0:T(8,128)(2,1)S(1)} %copy-done.10, bf16[1024,256]{1,0:T(8,128)(2,1)S(1)} %get-tuple-element.15.cf_ref), custom_call_target="tpu_custom_call" | custom-call | flops 44999999488 | bytes 45000000 | tf_op jit(solution)/shard_map/terms/pallas_call | solution.py:30
  81.1 0.0 copy-start.4
  81.1 0.0 copy-start.7
  81.1 5.0 %all-to-all-start.1 = ((f32[128,24,1,128]{3,1,2,0:T(8,128)}), f32[128,24,1,128]{3,1,2,0:T(8,128)S(1)}, u32[]{:S(2)}, u32[]{:S(2)}) async-start(f32[128,24,1,128]{3,1,2,0:T(8,128)} %bitcast.12), calls=%async_computation.1 | async-start | bytes 3145728 | tf_op jit(solution)/shard_map/all_to_all | solution.py:296
  86.1 0.1 pad_add_fusion.where_ref
  86.2 23.9 %all-to-all-done.1 = f32[128,24,1,128]{3,1,2,0:T(8,128)S(1)} async-done(((f32[128,24,1,128]{3,1,2,0:T(8,128)}), f32[128,24,1,128]{3,1,2,0:T(8,128)S(1)}, u32[]{:S(2)}, u32[]{:S(2)}) %all-to-all-start.1) | async-done | bytes 1572896 | tf_op jit(solution)/shard_map/all_to_all | solution.py:296
  110.1 0.0 copy-done.4
  110.1 0.0 copy-done.7
  110.1 2.1 %sums.1 = (f32[72,128]{1,0:T(8,128)S(1)}, f32[72,128]{1,0:T(8,128)S(1)}, f32[72,128]{1,0:T(8,128)S(1)}, f32[72,128]{1,0:T(8,128)S(1)}, f32[32,128]{1,0:T(8,128)S...) custom-call(s32[2]{0:T(128)S(1)} %pad_add_fusion.where_ref, s32[16,64]{1,0:T(8,128)S(1)} %bitcast.26, ...), custom_call_target="tpu_custom_call" | custom-call | flops 2000000000 | bytes 2000000 | tf_op jit(solution)/shard_map/sums/pallas_call | solution.py:30
  112.2 0.9 collective-permute-start
  113.1 1.7 %collective-permute-start.1 = (f32[72,128]{1,0:T(8,128)S(1)}, f32[72,128]{1,0:T(8,128)S(1)}, u32[]{:S(2)}, u32[]{:S(2)}) collective-permute-start(f32[72,128]{1,0:T(8,128)S(1)} %get-tuple-element.18), channel_id=1, source_target_pairs={{0,2},{1,3},{2,0},{3,1},{4,6},{5,7},{6,4},{7,5},{8,10},{9,11},{10,... | collective-permute-start | bytes 110600 | tf_op jit(solution)/shard_map/ppermute | solution.py:302
  114.8 1.0 collective-permute-start.2
  115.8 1.3 collective-permute-start.4
  117.1 1.3 collective-permute-start.5
  118.4 5.4 %collective-permute-done.4.refs_5_ = f32[16,128]{1,0:T(8,128)S(1)} collective-permute-done((f32[16,128]{1,0:T(8,128)S(1)}, f32[16,128]{1,0:T(8,128)S(1)}, u32[]{:S(2)}, u32[]{:S(2)}) %collective-permute-start.4) | collective-permute-done | bytes 8224 | tf_op jit(solution)/shard_map/ppermute | solution.py:360
  123.8 1.9 %collective-permute-start.3 = (f32[32,128]{1,0:T(8,128)S(1)}, f32[32,128]{1,0:T(8,128)S(1)}, u32[]{:S(2)}, u32[]{:S(2)}) collective-permute-start(f32[32,128]{1,0:T(8,128)S(1)} %get-tuple-element.20), channel_id=1, source_target_pairs={{0,4},{4,8},{8,12},{12,16},{16,20},{20,24},{24,28},{28,32},{32,36}... | collective-permute-start | bytes 49160 | tf_op jit(solution)/shard_map/ppermute | solution.py:360
  125.7 0.9 collective-permute-done.5.refs_6_
  126.6 2.0 %collective-permute-start.6 = (f32[16,128]{1,0:T(8,128)S(1)}, f32[16,128]{1,0:T(8,128)S(1)}, u32[]{:S(2)}, u32[]{:S(2)}) collective-permute-start(f32[16,128]{1,0:T(8,128)S(1)} %get-tuple-element.23), channel_id=1, source_target_pairs={{3,4},{7,8},{11,12},{15,16},{19,20},{23,24},{27,28},{31,32},{35,36... | collective-permute-start | bytes 24584 | tf_op jit(solution)/shard_map/ppermute | solution.py:360
  128.6 7.2 %collective-permute-done.6.refs_7_ = f32[16,128]{1,0:T(8,128)S(1)} collective-permute-done((f32[16,128]{1,0:T(8,128)S(1)}, f32[16,128]{1,0:T(8,128)S(1)}, u32[]{:S(2)}, u32[]{:S(2)}) %collective-permute-start.6) | collective-permute-done | bytes 8224 | tf_op jit(solution)/shard_map/ppermute | solution.py:360
  135.8 0.0 collective-permute-done.3.refs_4_
  135.8 0.0 collective-permute-done.refs_1_
  135.8 0.0 collective-permute-done.1.refs_2_
  135.8 0.0 collective-permute-done.2.refs_3_
  135.8 0.0 copy-done
  135.8 0.0 copy-done.8
  135.8 3.1 %faces.1.own_ref = f32[80,128]{1,0:T(8,128)S(1)} custom-call(s32[2]{0:T(128)S(1)} %pad_add_fusion.where_ref, s32[8,64]{1,0:T(8,128)S(1)} %bitcast.27, f32[3,64,128]{2,1,0:T(8,128)S(1)} %bitcast.24, f32[72,128]{1,0:T(8,128)S(1)} %get-tuple-element.16.refs_0_, f32[72,128]{1,0:T(8,128)S(1)} %collective-permute-done.refs_1_, ...), custom_call_target="tpu_custom_call" | custom-call | flops 2000000000 | bytes 2000000 | tf_op jit(solution)/shard_map/faces/pallas_call | solution.py:30
  138.9 0.1 collective-permute-start.9
  139.0 0.1 collective-permute-start.8
  139.1 1.9 %collective-permute-start.7 = (f32[80,128]{1,0:T(8,128)S(1)}, f32[80,128]{1,0:T(8,128)S(1)}, u32[]{:S(2)}, u32[]{:S(2)}) collective-permute-start(f32[80,128]{1,0:T(8,128)S(1)} %faces.1.own_ref), channel_id=1, source_target_pairs={{0,1},{1,2},{2,3},{3,0},{4,5},{5,6},{6,7},{7,4},{8,9},{9,10},{10,1... | collective-permute-start | bytes 122888 | tf_op jit(solution)/shard_map/ppermute | solution.py:302
  141.0 2.0 %collective-permute-done.9.three_ref = f32[80,128]{1,0:T(8,128)S(1)} collective-permute-done((f32[80,128]{1,0:T(8,128)S(1)}, f32[80,128]{1,0:T(8,128)S(1)}, u32[]{:S(2)}, u32[]{:S(2)}) %collective-permute-start.9) | collective-permute-done | bytes 40992 | tf_op jit(solution)/shard_map/ppermute | solution.py:302
  143.0 1.6 %collective-permute-done.8.two_ref = f32[80,128]{1,0:T(8,128)S(1)} collective-permute-done((f32[80,128]{1,0:T(8,128)S(1)}, f32[80,128]{1,0:T(8,128)S(1)}, u32[]{:S(2)}, u32[]{:S(2)}) %collective-permute-start.8) | collective-permute-done | bytes 40992 | tf_op jit(solution)/shard_map/ppermute | solution.py:302
  144.6 1.1 collective-permute-done.7.one_ref
  145.7 1.2 outs.1
  (5 shorter events, 0.0 us)
Async XLA Ops:
  0.6 0.9 copy-start.3
  1.5 0.7 copy-start.6
  4.9 10.5 %copy-start.1 = (f32[64,3,128]{2,0,1:T(8,128)S(1)}, f32[64,3,128]{2,0,1:T(8,128)}, u32[]{:S(2)}) copy-start(f32[64,3,128]{2,0,1:T(8,128)} %param.8) | copy-start | bytes 294916
  4.9 10.5 %copy-start.2 = (f32[64,3,128]{2,0,1:T(8,128)S(1)}, f32[64,3,128]{2,0,1:T(8,128)}, u32[]{:S(2)}) copy-start(f32[64,3,128]{2,0,1:T(8,128)} %param.9) | copy-start | bytes 294916
  4.9 10.5 %copy-start.5 = (f32[64,128]{1,0:T(8,128)S(1)}, f32[64,128]{1,0:T(8,128)}, u32[]{:S(2)}) copy-start(f32[64,128]{1,0:T(8,128)} %rad_ref.1) | copy-start | bytes 98308
  4.9 35.0 %all-to-all-start = ((f32[128,25,1,128]{3,2,1,0:T(1,128)}), f32[128,25,1,128]{3,2,1,0:T(1,128)S(1)}, u32[]{:S(2)}, u32[]{:S(2)}) async-start(f32[128,25,1,128]{3,2,1,0:T(1,128)} %bitcast.7), calls=%async_computation | async-start | bytes 3276800 | tf_op jit(solution)/shard_map/all_to_all | solution.py:296
  22.8 1.3 copy-start.9
  39.9 1.6 %copy-start.10 = (bf16[8192,128]{1,0:T(8,128)(2,1)S(1)}, bf16[8192,128]{1,0:T(8,128)(2,1)}, u32[]{:S(2)}) copy-start(bf16[8192,128]{1,0:T(8,128)(2,1)} %copy-done.9) | copy-start | bytes 6291460
  81.1 29.0 %copy-start.4 = (f32[64,3,128]{2,0,1:T(8,128)S(1)}, f32[64,3,128]{2,0,1:T(8,128)}, u32[]{:S(2)}) copy-start(f32[64,3,128]{2,0,1:T(8,128)} %param.7) | copy-start | bytes 294916
  81.1 29.0 %copy-start.7 = (s32[1,64,16]{1,2,0:T(8,128)S(1)}, s32[1,64,16]{1,2,0:T(8,128)}, u32[]{:S(2)}) copy-start(s32[1,64,16]{1,2,0:T(8,128)} %param.11) | copy-start | bytes 12292
  81.1 29.0 %all-to-all-start.1 = ((f32[128,24,1,128]{3,1,2,0:T(8,128)}), f32[128,24,1,128]{3,1,2,0:T(8,128)S(1)}, u32[]{:S(2)}, u32[]{:S(2)}) async-start(f32[128,24,1,128]{3,1,2,0:T(8,128)} %bitcast.12), calls=%async_computation.1 | async-start | bytes 3145728 | tf_op jit(solution)/shard_map/all_to_all | solution.py:296
  110.1 25.7 %copy-start = (s32[64,3,256]{2,0,1:T(8,128)S(1)}, s32[64,3,256]{2,0,1:T(8,128)}, u32[]{:S(2)}) copy-start(s32[64,3,256]{2,0,1:T(8,128)} %param.13) | copy-start | bytes 589828
  110.1 25.7 %copy-start.8 = (s32[64,8]{0,1:T(8,128)S(1)}, s32[64,8]{0,1:T(8,128)}, u32[]{:S(2)}) copy-start(s32[64,8]{0,1:T(8,128)} %param.12) | copy-start | bytes 6148
  112.2 23.6 %collective-permute-start = (f32[72,128]{1,0:T(8,128)S(1)}, f32[72,128]{1,0:T(8,128)S(1)}, u32[]{:S(2)}, u32[]{:S(2)}) collective-permute-start(f32[72,128]{1,0:T(8,128)S(1)} %get-tuple-element.17), channel_id=1, source_target_pairs={{0,1},{1,2},{2,3},{3,0},{4,5},{5,6},{6,7},{7,4},{8,9},{9,10},{10,1... | collective-permute-start | bytes 110600 | tf_op jit(solution)/shard_map/ppermute | solution.py:302
  113.1 22.7 %collective-permute-start.1 = (f32[72,128]{1,0:T(8,128)S(1)}, f32[72,128]{1,0:T(8,128)S(1)}, u32[]{:S(2)}, u32[]{:S(2)}) collective-permute-start(f32[72,128]{1,0:T(8,128)S(1)} %get-tuple-element.18), channel_id=1, source_target_pairs={{0,2},{1,3},{2,0},{3,1},{4,6},{5,7},{6,4},{7,5},{8,10},{9,11},{10,... | collective-permute-start | bytes 110600 | tf_op jit(solution)/shard_map/ppermute | solution.py:302
  114.8 21.0 %collective-permute-start.2 = (f32[72,128]{1,0:T(8,128)S(1)}, f32[72,128]{1,0:T(8,128)S(1)}, u32[]{:S(2)}, u32[]{:S(2)}) collective-permute-start(f32[72,128]{1,0:T(8,128)S(1)} %get-tuple-element.19), channel_id=1, source_target_pairs={{0,3},{1,0},{2,1},{3,2},{4,7},{5,4},{6,5},{7,6},{8,11},{9,8},{10,9... | collective-permute-start | bytes 110600 | tf_op jit(solution)/shard_map/ppermute | solution.py:302
  115.8 8.0 %collective-permute-start.4 = (f32[16,128]{1,0:T(8,128)S(1)}, f32[16,128]{1,0:T(8,128)S(1)}, u32[]{:S(2)}, u32[]{:S(2)}) collective-permute-start(f32[16,128]{1,0:T(8,128)S(1)} %get-tuple-element.21), channel_id=1, source_target_pairs={{1,4},{5,8},{9,12},{13,16},{17,20},{21,24},{25,28},{29,32},{33,36}... | collective-permute-start | bytes 24584 | tf_op jit(solution)/shard_map/ppermute | solution.py:360
  117.1 9.5 %collective-permute-start.5 = (f32[16,128]{1,0:T(8,128)S(1)}, f32[16,128]{1,0:T(8,128)S(1)}, u32[]{:S(2)}, u32[]{:S(2)}) collective-permute-start(f32[16,128]{1,0:T(8,128)S(1)} %get-tuple-element.22), channel_id=1, source_target_pairs={{2,4},{6,8},{10,12},{14,16},{18,20},{22,24},{26,28},{30,32},{34,36... | collective-permute-start | bytes 24584 | tf_op jit(solution)/shard_map/ppermute | solution.py:360
  123.8 12.0 %collective-permute-start.3 = (f32[32,128]{1,0:T(8,128)S(1)}, f32[32,128]{1,0:T(8,128)S(1)}, u32[]{:S(2)}, u32[]{:S(2)}) collective-permute-start(f32[32,128]{1,0:T(8,128)S(1)} %get-tuple-element.20), channel_id=1, source_target_pairs={{0,4},{4,8},{8,12},{12,16},{16,20},{20,24},{24,28},{28,32},{32,36}... | collective-permute-start | bytes 49160 | tf_op jit(solution)/shard_map/ppermute | solution.py:360
  126.6 9.2 %collective-permute-start.6 = (f32[16,128]{1,0:T(8,128)S(1)}, f32[16,128]{1,0:T(8,128)S(1)}, u32[]{:S(2)}, u32[]{:S(2)}) collective-permute-start(f32[16,128]{1,0:T(8,128)S(1)} %get-tuple-element.23), channel_id=1, source_target_pairs={{3,4},{7,8},{11,12},{15,16},{19,20},{23,24},{27,28},{31,32},{35,36... | collective-permute-start | bytes 24584 | tf_op jit(solution)/shard_map/ppermute | solution.py:360
  138.9 4.1 %collective-permute-start.9 = (f32[80,128]{1,0:T(8,128)S(1)}, f32[80,128]{1,0:T(8,128)S(1)}, u32[]{:S(2)}, u32[]{:S(2)}) collective-permute-start(f32[80,128]{1,0:T(8,128)S(1)} %faces.1.own_ref), channel_id=1, source_target_pairs={{0,3},{1,0},{2,1},{3,2},{4,7},{5,4},{6,5},{7,6},{8,11},{9,8},{10,9... | collective-permute-start | bytes 122888 | tf_op jit(solution)/shard_map/ppermute | solution.py:302
  139.0 5.6 %collective-permute-start.8 = (f32[80,128]{1,0:T(8,128)S(1)}, f32[80,128]{1,0:T(8,128)S(1)}, u32[]{:S(2)}, u32[]{:S(2)}) collective-permute-start(f32[80,128]{1,0:T(8,128)S(1)} %faces.1.own_ref), channel_id=1, source_target_pairs={{0,2},{1,3},{2,0},{3,1},{4,6},{5,7},{6,4},{7,5},{8,10},{9,11},{10,... | collective-permute-start | bytes 122888 | tf_op jit(solution)/shard_map/ppermute | solution.py:302
  139.1 6.6 %collective-permute-start.7 = (f32[80,128]{1,0:T(8,128)S(1)}, f32[80,128]{1,0:T(8,128)S(1)}, u32[]{:S(2)}, u32[]{:S(2)}) collective-permute-start(f32[80,128]{1,0:T(8,128)S(1)} %faces.1.own_ref), channel_id=1, source_target_pairs={{0,1},{1,2},{2,3},{3,0},{4,5},{5,6},{6,7},{7,4},{8,9},{9,10},{10,1... | collective-permute-start | bytes 122888 | tf_op jit(solution)/shard_map/ppermute | solution.py:302

commit v3 on v2

--- a/solution.py
+++ b/solution.py
@@ -17,9 +17,8 @@
 GIVE = 3 * SLOTS
 UNROLL = 8
 BOX_DEV = 64
-QUARTER = 16
 HALO = 4
-NEAR = QUARTER + 2 * HALO
+NEAR = BOX_DEV + 2 * HALO
 TINY = 1e-30
 VMEM = pl.BlockSpec(memory_space=pltpu.VMEM)
 SMEM = pl.BlockSpec(memory_space=pltpu.SMEM)
@@ -173,8 +172,7 @@
     lax.fori_loop(0, DEVICES // UNROLL, some, 0)
 
 
-def sum_kernel(where_ref, list_ref, node_ref, back_ref, *refs):
-    quarters, edges, acc_ref = refs[0:4], refs[4:8], refs[8]
+def sum_kernel(list_ref, back_ref, o_ref):
     _, slot = slot_table(list_ref[...])
     acc = jnp.zeros((BOX_DEV, 384), F)
     for j in range(SLOTS):
@@ -185,109 +183,74 @@
         for part in split3(terms):
             acc = acc + jnp.dot(sel, part.astype(BF), preferred_element_type=F)
     for c in range(3):
-        acc_ref[c, 0:8, :] = jnp.zeros((8, 128), F)
-        acc_ref[c, 64:72, :] = jnp.zeros((8, 128), F)
-        acc_ref[c, HALO : HALO + BOX_DEV, :] = acc[:, c * 128 : (c + 1) * 128]
-    surf = where_ref[0]
-    for k, ref in enumerate(quarters):
-        first = pl.multiple_of(((surf + k) & 3) * QUARTER, QUARTER)
-        for c in range(3):
-            ref[c * NEAR : (c + 1) * NEAR, :] = acc_ref[c, pl.ds(first, NEAR), :]
+        o_ref[c * BOX_DEV : (c + 1) * BOX_DEV, :] = acc[:, c * 128 : (c + 1) * 128]
+
+
+def reduce_kernel(node_ref, own_ref, one_ref, two_ref, three_ref, d_ref, up_ref, down_ref):
+    d_ref[...] = own_ref[...] + one_ref[...] + two_ref[...] + three_ref[...]
     zero = jnp.zeros((HALO, 128), F)
-    d = [acc[:, c * 128 : (c + 1) * 128] for c in range(3)]
     x = [node_ref[c] for c in range(3)]
-    head = jnp.concatenate([t[0:HALO] for t in d] + [zero] + [t[0:HALO] for t in x] + [zero], 0)
-    tail = jnp.concatenate([t[60:64] for t in d] + [zero] + [t[60:64] for t in x] + [zero], 0)
-    for k, ref in enumerate(edges):
-        pick = jnp.where(surf == k, 1.0, 0.0)
-        both = pick * tail + (1.0 - pick) * head
-        ref[...] = both if k == 0 else both[0:16]
-
-
-def face_kernel(where_ref, near_ref, node_ref, *refs):
-    quarters, edges = refs[0:4], refs[4:8]
-    face_ref, o_ref, tab_ref, cor_ref, x_ref, code_ref = refs[8:]
-    surf = where_ref[0]
-    first = pl.multiple_of(surf * QUARTER, QUARTER)
-    origin = where_ref[1] * QUARTER - HALO
-    is_low = jnp.where(surf == 0, 1.0, 0.0)
-    is_high = jnp.where(surf == 3, 1.0, 0.0)
-    d = quarters[0][...] + quarters[1][...] + quarters[2][...] + quarters[3][...]
-    edge_d = edges[0][0:16] + edges[1][...] + edges[2][...] + edges[3][...]
-    edge_x = edges[0][16:32]
-    zero = jnp.zeros((QUARTER, 128), F)
-
-    def placed(c, edge):
-        part = edge[c * HALO : (c + 1) * HALO]
-        return jnp.concatenate([is_low * part, zero, is_high * part], 0)
-
-    mine = []
-    for c in range(3):
-        x_ref[c, 0:8, :] = jnp.zeros((8, 128), F)
-        x_ref[c, 64:72, :] = jnp.zeros((8, 128), F)
-        x_ref[c, HALO : HALO + BOX_DEV, :] = node_ref[c]
-        disp = d[c * NEAR : (c + 1) * NEAR] + placed(c, edge_d)
-        mine.append(disp[HALO : HALO + QUARTER])
-        tab_ref[pl.ds(c, NEAR, stride=8), :] = x_ref[c, pl.ds(first, NEAR), :] + placed(c, edge_x)
-        tab_ref[pl.ds(c + 3, NEAR, stride=8), :] = disp
+    d = [d_ref[c * BOX_DEV : (c + 1) * BOX_DEV, :] for c in range(3)]
+    for ref, first in ((up_ref, BOX_DEV - HALO), (down_ref, 0)):
+        ref[...] = jnp.concatenate([t[first : first + HALO] for t in x + d] + [zero, zero], 0)
+
+
+def face_kernel(where_ref, near_ref, node_ref, d_ref, low_ref, high_ref, face_ref, v_ref, s_ref, tab_ref, cor_ref, code_ref):
+    origin = where_ref[0] * BOX_DEV - HALO
+    for c in range(6):
+        own = node_ref[c] if c < 3 else d_ref[(c - 3) * BOX_DEV : (c - 2) * BOX_DEV, :]
+        edge = slice(c * HALO, (c + 1) * HALO)
+        tab_ref[pl.ds(c, NEAR, stride=8), :] = jnp.concatenate(
+            [low_ref[edge, :], own, high_ref[edge, :]], 0
+        )
     for c in (6, 7):
         tab_ref[pl.ds(c, NEAR, stride=8), :] = jnp.zeros((NEAR, 128), F)
-
     for k in range(3):
         for h in range(2):
-            code_ref[pl.ds((k * 2 + h) * QUARTER, QUARTER), :] = face_ref[
-                k, pl.ds(first, QUARTER), h * 128 : (h + 1) * 128
+            code_ref[pl.ds((k * 2 + h) * BOX_DEV, BOX_DEV), :] = face_ref[
+                k, :, h * 128 : (h + 1) * 128
             ]
 
-    def one_box(b, carry):
-        box = first + b
-        tables = []
-        for j in range(8):
-            at = near_ref[j, box] - origin
-            tables.append(tab_ref[pl.ds(pl.multiple_of(at * 8, 8), 8), :])
-        for h in range(2):
-            for k in range(3):
-                code = code_ref[pl.ds((k * 2 + h) * QUARTER + b, 1), :]
-                code = jnp.broadcast_to(code, (8, 128))
-                lane = code & 127
-                which = code >> 7
-                got = None
-                for j in range(8):
-                    value = jnp.take_along_axis(tables[j], lane, axis=1)
-                    got = value if got is None else jnp.where(which == j, value, got)
-                cor_ref[k, pl.ds(b * 2 + h, 8, stride=32), :] = got
+    def some(g, carry):
+        for u in range(8):
+            b = g * 8 + u
+            tables = []
+            for j in range(8):
+                at = near_ref[j, b] - origin
+                tables.append(tab_ref[pl.ds(pl.multiple_of(at * 8, 8), 8), :])
+            for h in range(2):
+                for k in range(3):
+                    code = code_ref[pl.ds((k * 2 + h) * BOX_DEV + b, 1), :]
+                    code = jnp.broadcast_to(code, (8, 128))
+                    lane = code & 127
+                    which = code >> 7
+                    got = None
+                    for j in range(8):
+                        value = jnp.take_along_axis(tables[j], lane, axis=1)
+                        got = value if got is None else jnp.where(which == j, value, got)
+                    cor_ref[k, pl.ds(h * BOX_DEV + b, 8, stride=128), :] = got
         return carry
 
-    lax.fori_loop(0, QUARTER, one_box, 0)
-
-    def corner(k):
-        part = [cor_ref[k, pl.ds(c * 32, 32), :] for c in range(6)]
-        return [part[c] + 0.5 * part[c + 3] for c in range(3)], part[3:6]
-
-    (ma, da), (mb, db), (mc, dc) = corner(0), corner(1), corner(2)
-    u = [mb[c] - ma[c] for c in range(3)]
-    w = [mc[c] - ma[c] for c in range(3)]
-    swept = None
+    lax.fori_loop(0, BOX_DEV // 8, some, 0)
+
+    for h in range(2):
+
+        def corner(k):
+            part = [cor_ref[k, pl.ds(c * 128 + h * BOX_DEV, BOX_DEV), :] for c in range(6)]
+            return [part[c] + 0.5 * part[c + 3] for c in range(3)], part[3:6]
+
+        (ma, da), (mb, db), (mc, dc) = corner(0), corner(1), corner(2)
+        u = [mb[c] - ma[c] for c in range(3)]
+        w = [mc[c] - ma[c] for c in range(3)]
+        swept = None
+        for c in range(3):
+            p, q = (c + 1) % 3, (c + 2) % 3
+            normal = 0.5 * (u[p] * w[q] - u[q] * w[p])
+            term = ((da[c] + db[c] + dc[c]) / 3.0) * normal
+            swept = term if swept is None else swept + term
+        s_ref[:, h * 128 : (h + 1) * 128] = swept
     for c in range(3):
-        p, q = (c + 1) % 3, (c + 2) % 3
-        normal = 0.5 * (u[p] * w[q] - u[q] * w[p])
-        term = ((da[c] + db[c] + dc[c]) / 3.0) * normal
-        swept = term if swept is None else swept + term
-    for c in range(3):
-        o_ref[c * 16 : (c + 1) * 16, :] = mine[c] * 2.0
-    o_ref[48:80, :] = swept
-
-
-def out_kernel(where_ref, own_ref, one_ref, two_ref, three_ref, v_ref, s_ref):
-    surf = where_ref[0]
-    for k, ref in enumerate((own_ref, one_ref, two_ref, three_ref)):
-        first = pl.multiple_of(((surf + 4 - k) & 3) * QUARTER, QUARTER)
-        for c in range(3):
-            v_ref[c, pl.ds(first, QUARTER), :] = ref[c * 16 : (c + 1) * 16, :]
-        for h in range(2):
-            s_ref[pl.ds(first, QUARTER), h * 128 : (h + 1) * 128] = ref[
-                pl.ds(48 + h, QUARTER, stride=2), :
-            ]
+        v_ref[c] = d_ref[c * BOX_DEV : (c + 1) * BOX_DEV, :] * 2.0
 
 
 def to_all(array):
@@ -297,17 +260,8 @@
     return packets.reshape(DEVICES * rows, 128)
 
 
-def around(arrays):
-    return [
-        lax.ppermute(a, "surf", [(i, (i + k) % 4) for i in range(4)])
-        for k, a in zip((1, 2, 3), arrays)
-    ]
-
-
-def edge_pairs(k):
-    up = [(v * 4 + k, (v + 1) * 4) for v in range(31)]
-    down = [((v + 1) * 4 + (k + 1) % 4, v * 4 + 3) for v in range(31)]
-    return up + down
+def around(array):
+    return [lax.ppermute(array, "surf", [(i, (i + k) % 4) for i in range(4)]) for k in (1, 2, 3)]
 
 
 def shape(*dims, kind=F):
@@ -317,8 +271,7 @@
 def body(node_pos, centres, coefs, radii, block_list, neighbours, faces):
     listed = block_list[0].T
     nodes, cens, weights = [a.transpose(1, 0, 2) for a in (node_pos, centres, coefs)]
-    surf = lax.axis_index("surf")
-    where = jnp.stack([surf, lax.axis_index("vol") * 4 + surf]).astype(I)
+    where = lax.axis_index("vol").astype(I).reshape(1)
     (sent,) = call(
         prep_kernel,
         "prep",
@@ -349,34 +302,31 @@
         mib=16,
         us=45,
     )
-    own = call(
+    (own,) = call(
         sum_kernel,
         "sums",
-        (shape(3 * NEAR, 128),) * 4 + (shape(32, 128),) + (shape(16, 128),) * 3,
-        [("s", where), ("v", listed), ("v", nodes), ("v", to_all(terms))],
-        [pltpu.VMEM((3, 72, 128), F)],
-    )
-    quarters = [own[0], *around(own[1:4])]
-    edges = [lax.ppermute(own[4 + k], BOTH, edge_pairs(k)) for k in range(4)]
-    (mine,) = call(
+        (shape(3 * BOX_DEV, 128),),
+        [("v", listed), ("v", to_all(terms))],
+    )
+    d, up, down = call(
+        reduce_kernel,
+        "reduce",
+        (shape(3 * BOX_DEV, 128), shape(32, 128), shape(32, 128)),
+        [("v", nodes), ("v", own)] + [("v", r) for r in around(own)],
+    )
+    low = lax.ppermute(up, "vol", [(i, i + 1) for i in range(31)])
+    high = lax.ppermute(down, "vol", [(i + 1, i) for i in range(31)])
+    velocity, swept = call(
         face_kernel,
         "faces",
-        (shape(80, 128),),
-        [("s", where), ("s", neighbours.T), ("v", nodes)]
-        + [("v", a) for a in quarters + edges]
+        (shape(3, BOX_DEV, 128), shape(BOX_DEV, 256)),
+        [("s", where), ("s", neighbours.T), ("v", nodes), ("v", d), ("v", low), ("v", high)]
         + [("v", faces.transpose(1, 0, 2))],
         [
             pltpu.VMEM((8 * NEAR, 128), F),
-            pltpu.VMEM((3, 256, 128), F),
-            pltpu.VMEM((3, 72, 128), F),
-            pltpu.VMEM((96, 128), I),
+            pltpu.VMEM((3, 1024, 128), F),
+            pltpu.VMEM((6 * BOX_DEV, 128), I),
         ],
-    )
-    velocity, swept = call(
-        out_kernel,
-        "outs",
-        (shape(3, BOX_DEV, 128), shape(BOX_DEV, 256)),
-        [("s", where), ("v", mine)] + [("v", r) for r in around([mine] * 3)],
     )
     return velocity.transpose(1, 0, 2), swept
 

time: 147 us -> 137 us (0.932); the launches traced: 147 us -> 135 us
  waiting for transfers between devices: 57.7 us -> 22.2 us
  blocking collectives: 0 us -> 28.6 us
  starting transfers between devices: 27.7 us -> 21.8 us
    all_to_all x0 -> x1, blocking collectives: none -> 28.6 us  [to_all(): lax.all_to_all(packets, BOTH, split_axis=0, concat_axis=0, tiled=True)]
    all_to_all x2 -> x1, waiting for transfers between devices: 39.6 us -> 15.8 us  [to_all(): lax.all_to_all(packets, BOTH, split_axis=0, concat_axis=0, tiled=True)]
    ppermute x10 -> x5, waiting for transfers between devices: 18.1 us -> 6.46 us  [the longest x3 5.05 us: around(): lax.ppermute(array, 'surf', [(i, (i + k) % 4) for i in range(4)])]
    all_to_all x2 -> x1, starting transfers between devices: 15.5 us -> 10.4 us  [to_all(): lax.all_to_all(packets, BOTH, split_axis=0, concat_axis=0, tiled=True)]
    ppermute x10 -> x5, starting transfers between devices: 12.2 us -> 11.4 us  [the longest x1 5.75 us: body(): high = lax.ppermute(down, 'vol', [(i + 1, i) for i in range(31)])]
  transfers between devices with their start and end apart: 12 -> 6, of which waited for: 8 -> 4; matrix products, arithmetic and copies ran while one was open for 0% -> 0% of each run, Pallas kernels for 5% -> 6%
where the time goes in v3:
time: 137 us; the launch traced here: 135 us
  Pallas kernels  56.6 us (41%)
  blocking collectives  28.6 us (21%)
  waiting for transfers between devices  22.2 us (16%)
  starting transfers between devices  21.8 us (16%)
  local copies, waits for them, and re-layouts  4.54 us (3%)
    pallas_call x6, Pallas kernels, call(): pl.pallas_call(kernel, name=name, out_shape=outs, in_specs=specs, out_spe...  56.6 us
    all_to_all x1, blocking collectives, to_all(): lax.all_to_all(packets, BOTH, split_axis=0, concat_axis=0, tiled=True)  28.6 us
    all_to_all x1, waiting for transfers between devices, to_all(): lax.all_to_all(packets, BOTH, split_axis=0, concat_axis=0, tiled=True)  15.8 us
    all_to_all x1, starting transfers between devices, to_all(): lax.all_to_all(packets, BOTH, split_axis=0, concat_axis=0, tiled=True)  10.4 us
    ppermute x1, starting transfers between devices, body(): high = lax.ppermute(down, 'vol', [(i + 1, i) for i in range(31)])  5.75 us
    ppermute x3, waiting for transfers between devices, around(): lax.ppermute(array, 'surf', [(i, (i + k) % 4) for i in range(4)])  5.05 us
    unnamed x22, local copies, waits for them, and re-layouts  4.54 us
    ppermute x3, starting transfers between devices, around(): lax.ppermute(array, 'surf', [(i, (i + k) % 4) for i in range(4)])  3.68 us
  transfers between devices with their start and end apart: 6, of which 4 were waited for; matrix products, arithmetic and copies ran while one was open for 0% of the time, Pallas kernels for 6%

profile of v3, /device:TPU:8, one launch (start us, length us, event | category | flops | bytes accessed | tf_op | source)
XLA Modules:
  0.0 134.5 jit_solution(1695358535273621866)
XLA Ops:
  0.6 0.0 copy-start.3
  0.6 0.9 copy-done.3
  1.5 0.0 copy-start.6
  1.5 0.7 copy-done.6
  2.2 2.7 %prep.1 = f32[3200,128]{1,0:T(8,128)} custom-call(s32[16,64]{1,0:T(8,128)S(1)} %bitcast.25, f32[3,64,128]{2,1,0:T(8,128)S(1)} %bitcast.22), custom_call_target="tpu_custom_call" | custom-call | flops 2000000000 | bytes 2000000 | tf_op jit(solution)/shard_map/prep/pallas_call | solution.py:29
  4.9 0.0 copy-start.1
  4.9 0.0 copy-start.2
  4.9 0.0 copy-start.5
  4.9 10.4 %all-to-all-start = ((f32[128,25,1,128]{3,2,1,0:T(1,128)}), f32[128,25,1,128]{3,2,1,0:T(1,128)S(1)}, u32[]{:S(2)}, u32[]{:S(2)}) async-start(f32[128,25,1,128]{3,2,1,0:T(1,128)} %bitcast.6), calls=%async_computation | async-start | bytes 3276800 | tf_op jit(solution)/shard_map/all_to_all | solution.py:259
  15.4 0.0 copy-done.1
  15.4 0.0 copy-done.2
  15.4 0.0 copy-done.5
  15.4 7.4 %feats.1 = (bf16[8192,128]{1,0:T(8,128)(2,1)S(1)}, bf16[1024,256]{1,0:T(8,128)(2,1)S(1)}) custom-call(f32[3,64,128]{2,1,0:T(8,128)S(1)} %bitcast.20, f32[3,64,128]{2,1,0:T(8,128)S(1)} %bitcast.21, f32[64,128]{1,0:T(8,128)S(1)} %copy-done.5), custom_call_target="tpu_custom_call" | custom-call | flops 10000000000 | bytes 10000000 | tf_op jit(solution)/shard_map/feats/pallas_call | solution.py:29
  22.8 0.0 copy-start.9
  22.9 1.3 copy-done.9
  24.2 15.8 %all-to-all-done = f32[128,25,1,128]{3,2,1,0:T(1,128)S(1)} async-done(((f32[128,25,1,128]{3,2,1,0:T(1,128)}), f32[128,25,1,128]{3,2,1,0:T(1,128)S(1)}, u32[]{:S(2)}, u32[]{:S(2)}) %all-to-all-start) | async-done | bytes 1638432 | tf_op jit(solution)/shard_map/all_to_all | solution.py:259
  39.9 0.0 copy-start.10
  39.9 1.6 %copy-done.10 = bf16[8192,128]{1,0:T(8,128)(2,1)S(1)} copy-done((bf16[8192,128]{1,0:T(8,128)(2,1)S(1)}, bf16[8192,128]{1,0:T(8,128)(2,1)}, u32[]{:S(2)}) %copy-start.10) | copy-done | bytes 2097176
  41.5 38.4 %terms.1 = f32[3072,128]{1,0:T(8,128)S(1)} custom-call(f32[3200,128]{1,0:T(8,128)S(1)} %bitcast.16, bf16[8192,128]{1,0:T(8,128)(2,1)S(1)} %copy-done.10, bf16[1024,256]{1,0:T(8,128)(2,1)S(1)} %get-tuple-element.10.cf_ref), custom_call_target="tpu_custom_call" | custom-call | flops 44999999488 | bytes 45000000 | tf_op jit(solution)/shard_map/terms/pallas_call | solution.py:29
  80.0 0.0 copy-start.7
  80.0 28.6 %all_to_all.10 = f32[128,24,1,128]{3,1,2,0:T(8,128)S(1)} all-to-all(f32[128,24,1,128]{3,1,2,0:T(8,128)S(1)} %bitcast.17), channel_id=1, replica_groups=mesh['vol'=32,'surf'=4] {'vol','surf'}, dimensions={0} | all-to-all | bytes 3145728 | tf_op jit(solution)/shard_map/all_to_all | solution.py:259
  108.6 0.0 copy-done.7
  108.6 0.0 copy-start.4
  108.6 1.5 %sums.1.own_ref = f32[192,128]{1,0:T(8,128)S(1)} custom-call(s32[16,64]{1,0:T(8,128)S(1)} %bitcast.26, f32[3072,128]{1,0:T(8,128)S(1)} %bitcast.18), custom_call_target="tpu_custom_call" | custom-call | flops 2000000000 | bytes 2000000 | tf_op jit(solution)/shard_map/sums/pallas_call | solution.py:29
  110.1 0.0 copy-start
  110.1 0.0 copy-start.8
  110.1 0.9 collective-permute-start
  111.0 1.7 %collective-permute-start.1 = (f32[192,128]{1,0:T(8,128)S(1)}, f32[192,128]{1,0:T(8,128)S(1)}, u32[]{:S(2)}, u32[]{:S(2)}) collective-permute-start(f32[192,128]{1,0:T(8,128)S(1)} %sums.1.own_ref), channel_id=1, source_target_pairs={{0,2},{1,3},{2,0},{3,1},{4,6},{5,7},{6,4},{7,5},{8,10},{9,11},{10,... | collective-permute-start | bytes 294920 | tf_op jit(solution)/shard_map/ppermute | solution.py:264
  112.8 1.0 collective-permute-start.2
  113.8 4.5 %collective-permute-done.one_ref = f32[192,128]{1,0:T(8,128)S(1)} collective-permute-done((f32[192,128]{1,0:T(8,128)S(1)}, f32[192,128]{1,0:T(8,128)S(1)}, u32[]{:S(2)}, u32[]{:S(2)}) %collective-permute-start) | collective-permute-done | bytes 98336 | tf_op jit(solution)/shard_map/ppermute | solution.py:264
  118.3 0.0 collective-permute-done.1.two_ref
  118.3 0.6 collective-permute-done.2.three_ref
  118.8 0.0 copy-done.4
  118.9 1.9 %collective-permute-start.3 = (f32[32,128]{1,0:T(8,128)S(1)}, f32[32,128]{1,0:T(8,128)S(1)}, u32[]{:S(2)}, u32[]{:S(2)}) collective-permute-start(f32[32,128]{1,0:T(8,128)S(1)} %get-tuple-element.12), channel_id=1, source_target_pairs={{0,4},{4,8},{8,12},{12,16},{16,20},{20,24},{24,28},{28,32},{32,36}... | collective-permute-start | bytes 49160 | tf_op jit(solution)/shard_map/ppermute | solution.py:317
  120.8 5.8 %collective-permute-start.4 = (f32[32,128]{1,0:T(8,128)S(1)}, f32[32,128]{1,0:T(8,128)S(1)}, u32[]{:S(2)}, u32[]{:S(2)}) collective-permute-start(f32[32,128]{1,0:T(8,128)S(1)} %get-tuple-element.13), channel_id=1, source_target_pairs={{4,0},{8,4},{12,8},{16,12},{20,16},{24,20},{28,24},{32,28},{36,32}... | collective-permute-start | bytes 49160 | tf_op jit(solution)/shard_map/ppermute | solution.py:318
  126.6 0.0 collective-permute-done.3.low_ref
  126.6 1.4 %collective-permute-done.4.high_ref = f32[32,128]{1,0:T(8,128)S(1)} collective-permute-done((f32[32,128]{1,0:T(8,128)S(1)}, f32[32,128]{1,0:T(8,128)S(1)}, u32[]{:S(2)}, u32[]{:S(2)}) %collective-permute-start.4) | collective-permute-done | bytes 16416 | tf_op jit(solution)/shard_map/ppermute | solution.py:318
  128.0 0.0 copy-done
  128.0 0.0 copy-done.8
  128.0 6.5 %faces.1 = (f32[3,64,128]{2,1,0:T(8,128)}, f32[64,256]{1,0:T(8,128)}) custom-call(s32[1]{0:T(128)} %bitcast.where_ref, s32[8,64]{1,0:T(8,128)S(1)} %bitcast.27, f32[3,64,128]{2,1,0:T(8,128)S(1)} %bitcast.24, f32[192,128]{1,0:T(8,128)S(1)} %get-tuple-element.11.d_ref, f32[32,128]{1,0:T(8,128)S(1)} %collective-permute-done.3.low_ref, ...), custom_call_target="tpu_custom_call" | custom-call | flops 2000000000 | bytes 2000000 | tf_op jit(solution)/shard_map/faces/pallas_call | solution.py:29
  (1 shorter events, 0.0 us)
Async XLA Ops:
  0.6 0.9 copy-start.3
  1.5 0.7 copy-start.6
  4.9 10.5 %copy-start.1 = (f32[64,3,128]{2,0,1:T(8,128)S(1)}, f32[64,3,128]{2,0,1:T(8,128)}, u32[]{:S(2)}) copy-start(f32[64,3,128]{2,0,1:T(8,128)} %param.8) | copy-start | bytes 294916
  4.9 10.5 %copy-start.2 = (f32[64,3,128]{2,0,1:T(8,128)S(1)}, f32[64,3,128]{2,0,1:T(8,128)}, u32[]{:S(2)}) copy-start(f32[64,3,128]{2,0,1:T(8,128)} %param.9) | copy-start | bytes 294916
  4.9 10.5 %copy-start.5 = (f32[64,128]{1,0:T(8,128)S(1)}, f32[64,128]{1,0:T(8,128)}, u32[]{:S(2)}) copy-start(f32[64,128]{1,0:T(8,128)} %rad_ref.1) | copy-start | bytes 98308
  4.9 35.0 %all-to-all-start = ((f32[128,25,1,128]{3,2,1,0:T(1,128)}), f32[128,25,1,128]{3,2,1,0:T(1,128)S(1)}, u32[]{:S(2)}, u32[]{:S(2)}) async-start(f32[128,25,1,128]{3,2,1,0:T(1,128)} %bitcast.6), calls=%async_computation | async-start | bytes 3276800 | tf_op jit(solution)/shard_map/all_to_all | solution.py:259
  22.8 1.3 copy-start.9
  39.9 1.6 %copy-start.10 = (bf16[8192,128]{1,0:T(8,128)(2,1)S(1)}, bf16[8192,128]{1,0:T(8,128)(2,1)}, u32[]{:S(2)}) copy-start(bf16[8192,128]{1,0:T(8,128)(2,1)} %copy-done.9) | copy-start | bytes 6291460
  80.0 28.6 %copy-start.7 = (s32[1,64,16]{1,2,0:T(8,128)S(1)}, s32[1,64,16]{1,2,0:T(8,128)}, u32[]{:S(2)}) copy-start(s32[1,64,16]{1,2,0:T(8,128)} %param.11) | copy-start | bytes 12292
  108.6 10.3 %copy-start.4 = (f32[64,3,128]{2,0,1:T(8,128)S(1)}, f32[64,3,128]{2,0,1:T(8,128)}, u32[]{:S(2)}) copy-start(f32[64,3,128]{2,0,1:T(8,128)} %param.7) | copy-start | bytes 294916
  110.1 17.9 %copy-start = (s32[64,3,256]{2,0,1:T(8,128)S(1)}, s32[64,3,256]{2,0,1:T(8,128)}, u32[]{:S(2)}) copy-start(s32[64,3,256]{2,0,1:T(8,128)} %param.13) | copy-start | bytes 589828
  110.1 17.9 %copy-start.8 = (s32[64,8]{0,1:T(8,128)S(1)}, s32[64,8]{0,1:T(8,128)}, u32[]{:S(2)}) copy-start(s32[64,8]{0,1:T(8,128)} %param.12) | copy-start | bytes 6148
  110.1 8.2 %collective-permute-start = (f32[192,128]{1,0:T(8,128)S(1)}, f32[192,128]{1,0:T(8,128)S(1)}, u32[]{:S(2)}, u32[]{:S(2)}) collective-permute-start(f32[192,128]{1,0:T(8,128)S(1)} %sums.1.own_ref), channel_id=1, source_target_pairs={{0,1},{1,2},{2,3},{3,0},{4,5},{5,6},{6,7},{7,4},{8,9},{9,10},{10,1... | collective-permute-start | bytes 294920 | tf_op jit(solution)/shard_map/ppermute | solution.py:264
  111.0 7.2 %collective-permute-start.1 = (f32[192,128]{1,0:T(8,128)S(1)}, f32[192,128]{1,0:T(8,128)S(1)}, u32[]{:S(2)}, u32[]{:S(2)}) collective-permute-start(f32[192,128]{1,0:T(8,128)S(1)} %sums.1.own_ref), channel_id=1, source_target_pairs={{0,2},{1,3},{2,0},{3,1},{4,6},{5,7},{6,4},{7,5},{8,10},{9,11},{10,... | collective-permute-start | bytes 294920 | tf_op jit(solution)/shard_map/ppermute | solution.py:264
  112.8 6.1 %collective-permute-start.2 = (f32[192,128]{1,0:T(8,128)S(1)}, f32[192,128]{1,0:T(8,128)S(1)}, u32[]{:S(2)}, u32[]{:S(2)}) collective-permute-start(f32[192,128]{1,0:T(8,128)S(1)} %sums.1.own_ref), channel_id=1, source_target_pairs={{0,3},{1,0},{2,1},{3,2},{4,7},{5,4},{6,5},{7,6},{8,11},{9,8},{10,9... | collective-permute-start | bytes 294920 | tf_op jit(solution)/shard_map/ppermute | solution.py:264
  118.9 7.7 %collective-permute-start.3 = (f32[32,128]{1,0:T(8,128)S(1)}, f32[32,128]{1,0:T(8,128)S(1)}, u32[]{:S(2)}, u32[]{:S(2)}) collective-permute-start(f32[32,128]{1,0:T(8,128)S(1)} %get-tuple-element.12), channel_id=1, source_target_pairs={{0,4},{4,8},{8,12},{12,16},{16,20},{20,24},{24,28},{28,32},{32,36}... | collective-permute-start | bytes 49160 | tf_op jit(solution)/shard_map/ppermute | solution.py:317
  120.8 7.2 %collective-permute-start.4 = (f32[32,128]{1,0:T(8,128)S(1)}, f32[32,128]{1,0:T(8,128)S(1)}, u32[]{:S(2)}, u32[]{:S(2)}) collective-permute-start(f32[32,128]{1,0:T(8,128)S(1)} %get-tuple-element.13), channel_id=1, source_target_pairs={{4,0},{8,4},{12,8},{16,12},{20,16},{24,20},{28,24},{32,28},{36,32}... | collective-permute-start | bytes 49160 | tf_op jit(solution)/shard_map/ppermute | solution.py:318

commit v4 on v3

--- a/solution.py
+++ b/solution.py
@@ -91,14 +91,16 @@
         s = jnp.concatenate([p, p, p, q, q, t, jnp.zeros((80, 128), F)], 0)
         a_ref[pl.ds(pl.multiple_of(g * 128, 128), 128), :] = s.T.astype(BF)
         ks = split3(4.0 * coef_ref[:, pl.ds(g, 1), :].reshape(3, 128))
-        z = jnp.concatenate([*ks, jnp.zeros((7, 128), F)], 0).astype(BF)
+        z = jnp.concatenate([ks[0], ks[1], jnp.zeros((10, 128), F)], 0).astype(BF)
         cf_ref[pl.ds(pl.multiple_of(g * 16, 16), 16), :] = jnp.concatenate([z, z], 1)
         return carry
 
     lax.fori_loop(0, 64, one, 0)
 
 
-def terms_kernel(x_ref, a_ref, cf_ref, o_ref, v_ref, b_ref, q_ref, w_ref, stage_ref, ids_ref, sem):
+def terms_kernel(
+    x_ref, a_ref, cf_ref, o_ref, v_ref, b_ref, q_ref, w_ref, r_ref, stage_ref, ids_ref, sem
+):
     stage_ref[...] = x_ref[pl.ds(ASK - 1, DEVICES, stride=ASK), :].T[0:SLOTS].astype(I)
     copy = pltpu.make_async_copy(stage_ref, ids_ref, sem)
     copy.start()
@@ -111,7 +113,8 @@
     copy.wait()
 
     def stage0(i, buf):
-        base = jnp.minimum(i, DEVICES - 1) * ASK
+        i = jnp.minimum(i, DEVICES - 1)
+        base = i * ASK
         x, y, z = [x_ref[pl.ds(base + c * SLOTS, SLOTS), :] for c in range(3)]
         for f, value in enumerate((x, y, z, x * x + y * y + z * z)):
             first = value.astype(BF).astype(F)
@@ -141,11 +144,14 @@
         w_ref[buf, j, 128:256, :] = (w - high.astype(F)).astype(BF)
 
     def stage3(i, buf, j):
-        base = pl.multiple_of(i * GIVE, GIVE)
         g = ids_ref[j, i]
         c = cf_ref[pl.ds(pl.multiple_of(g * 16, 16), 16), :]
         r = jnp.dot(c, w_ref[buf, j], preferred_element_type=F)
-        o_ref[pl.ds(base + j, 3, stride=SLOTS), :] = r[0:3] + r[3:6] + r[6:9]
+        r_ref[buf, pl.ds(j, 6, stride=SLOTS), :] = r[0:6]
+
+    def stage4(i, buf):
+        base = pl.multiple_of(i * GIVE, GIVE)
+        o_ref[pl.ds(base, GIVE), :] = r_ref[buf, 0:GIVE, :] + r_ref[buf, GIVE : 2 * GIVE, :]
 
     slots = range(SLOTS)
     stage0(0, 0)
@@ -166,6 +172,7 @@
                 stage1(i + 2, buf, j)
                 stage2(1 - buf, j)
                 stage3(i, buf, j)
+            stage4(i, buf)
             stage0(i + 3, 1 - buf)
         return carry
 
@@ -195,8 +202,74 @@
         ref[...] = jnp.concatenate([t[first : first + HALO] for t in x + d] + [zero, zero], 0)
 
 
-def face_kernel(where_ref, near_ref, node_ref, d_ref, low_ref, high_ref, face_ref, v_ref, s_ref, tab_ref, cor_ref, code_ref):
-    origin = where_ref[0] * BOX_DEV - HALO
+def corners(near_ref, tab_ref, code_ref, cor_ref, box, at, origin, count):
+    tables = []
+    for j in range(8):
+        row = near_ref[j, box] - origin
+        tables.append(tab_ref[pl.ds(pl.multiple_of(row * 8, 8), 8), :])
+    for h in range(2):
+        for k in range(3):
+            code = code_ref[pl.ds((k * 2 + h) * BOX_DEV + box, 1), :]
+            code = jnp.broadcast_to(code, (8, 128))
+            lane = code & 127
+            which = code >> 7
+            got = None
+            for j in range(8):
+                value = jnp.take_along_axis(tables[j], lane, axis=1)
+                got = value if got is None else jnp.where(which == j, value, got)
+            cor_ref[k, pl.ds(h * count + at, 8, stride=2 * count), :] = got
+
+
+def volumes(cor_ref, h, count):
+    def corner(k):
+        part = [cor_ref[k, pl.ds((c * 2 + h) * count, count), :] for c in range(6)]
+        return [part[c] + 0.5 * part[c + 3] for c in range(3)], part[3:6]
+
+    (ma, da), (mb, db), (mc, dc) = corner(0), corner(1), corner(2)
+    u = [mb[c] - ma[c] for c in range(3)]
+    w = [mc[c] - ma[c] for c in range(3)]
+    swept = None
+    for c in range(3):
+        p, q = (c + 1) % 3, (c + 2) % 3
+        normal = 0.5 * (u[p] * w[q] - u[q] * w[p])
+        term = ((da[c] + db[c] + dc[c]) / 3.0) * normal
+        swept = term if swept is None else swept + term
+    return swept
+
+
+def split_codes(face_ref, code_ref):
+    for k in range(3):
+        for h in range(2):
+            code_ref[pl.ds((k * 2 + h) * BOX_DEV, BOX_DEV), :] = face_ref[
+                k, :, h * 128 : (h + 1) * 128
+            ]
+
+
+def inner_kernel(where_ref, near_ref, node_ref, d_ref, face_ref, v_ref, s_ref, tab_ref, cor_ref, code_ref):
+    for c in range(6):
+        own = node_ref[c] if c < 3 else d_ref[(c - 3) * BOX_DEV : (c - 2) * BOX_DEV, :]
+        tab_ref[pl.ds(c, BOX_DEV, stride=8), :] = own
+    for c in (6, 7):
+        tab_ref[pl.ds(c, BOX_DEV, stride=8), :] = jnp.zeros((BOX_DEV, 128), F)
+    split_codes(face_ref, code_ref)
+    origin = where_ref[0] * BOX_DEV
+
+    def some(g, carry):
+        for u in range(8):
+            box = g * 8 + HALO + u
+            corners(near_ref, tab_ref, code_ref, cor_ref, box, box, origin, BOX_DEV)
+        return carry
+
+    lax.fori_loop(0, (BOX_DEV - 2 * HALO) // 8, some, 0)
+    for h in range(2):
+        s_ref[:, h * 128 : (h + 1) * 128] = volumes(cor_ref, h, BOX_DEV)
+    for c in range(3):
+        v_ref[c] = d_ref[c * BOX_DEV : (c + 1) * BOX_DEV, :] * 2.0
+
+
+def edge_kernel(
+    where_ref, near_ref, node_ref, d_ref, low_ref, high_ref, face_ref, in_ref, s_ref, tab_ref, cor_ref, code_ref
+):
     for c in range(6):
         own = node_ref[c] if c < 3 else d_ref[(c - 3) * BOX_DEV : (c - 2) * BOX_DEV, :]
         edge = slice(c * HALO, (c + 1) * HALO)
@@ -205,52 +278,16 @@
         )
     for c in (6, 7):
         tab_ref[pl.ds(c, NEAR, stride=8), :] = jnp.zeros((NEAR, 128), F)
-    for k in range(3):
-        for h in range(2):
-            code_ref[pl.ds((k * 2 + h) * BOX_DEV, BOX_DEV), :] = face_ref[
-                k, :, h * 128 : (h + 1) * 128
-            ]
-
-    def some(g, carry):
-        for u in range(8):
-            b = g * 8 + u
-            tables = []
-            for j in range(8):
-                at = near_ref[j, b] - origin
-                tables.append(tab_ref[pl.ds(pl.multiple_of(at * 8, 8), 8), :])
-            for h in range(2):
-                for k in range(3):
-                    code = code_ref[pl.ds((k * 2 + h) * BOX_DEV + b, 1), :]
-                    code = jnp.broadcast_to(code, (8, 128))
-                    lane = code & 127
-                    which = code >> 7
-                    got = None
-                    for j in range(8):
-                        value = jnp.take_along_axis(tables[j], lane, axis=1)
-                        got = value if got is None else jnp.where(which == j, value, got)
-                    cor_ref[k, pl.ds(h * BOX_DEV + b, 8, stride=128), :] = got
-        return carry
-
-    lax.fori_loop(0, BOX_DEV // 8, some, 0)
-
+    split_codes(face_ref, code_ref)
+    origin = where_ref[0] * BOX_DEV - HALO
+    for at in range(2 * HALO):
+        box = at if at < HALO else BOX_DEV - 2 * HALO + at
+        corners(near_ref, tab_ref, code_ref, cor_ref, box, at, origin, 2 * HALO)
+    s_ref[...] = in_ref[...]
     for h in range(2):
-
-        def corner(k):
-            part = [cor_ref[k, pl.ds(c * 128 + h * BOX_DEV, BOX_DEV), :] for c in range(6)]
-            return [part[c] + 0.5 * part[c + 3] for c in range(3)], part[3:6]
-
-        (ma, da), (mb, db), (mc, dc) = corner(0), corner(1), corner(2)
-        u = [mb[c] - ma[c] for c in range(3)]
-        w = [mc[c] - ma[c] for c in range(3)]
-        swept = None
-        for c in range(3):
-            p, q = (c + 1) % 3, (c + 2) % 3
-            normal = 0.5 * (u[p] * w[q] - u[q] * w[p])
-            term = ((da[c] + db[c] + dc[c]) / 3.0) * normal
-            swept = term if swept is None else swept + term
-        s_ref[:, h * 128 : (h + 1) * 128] = swept
-    for c in range(3):
-        v_ref[c] = d_ref[c * BOX_DEV : (c + 1) * BOX_DEV, :] * 2.0
+        swept = volumes(cor_ref, h, 2 * HALO)
+        s_ref[0:HALO, h * 128 : (h + 1) * 128] = swept[0:HALO]
+        s_ref[BOX_DEV - HALO : BOX_DEV, h * 128 : (h + 1) * 128] = swept[HALO:]
 
 
 def to_all(array):
@@ -295,6 +332,7 @@
             pltpu.VMEM((2, SLOTS, 128, 128), BF),
             pltpu.VMEM((2, SLOTS, 128, 128), F),
             pltpu.VMEM((2, SLOTS, 256, 128), BF),
+            pltpu.VMEM((2, 2 * GIVE, 128), F),
             pltpu.VMEM((SLOTS, 128), I),
             pltpu.SMEM((SLOTS, 128), I),
             pltpu.SemaphoreType.DMA,
@@ -316,15 +354,27 @@
     )
     low = lax.ppermute(up, "vol", [(i, i + 1) for i in range(31)])
     high = lax.ppermute(down, "vol", [(i + 1, i) for i in range(31)])
-    velocity, swept = call(
-        face_kernel,
-        "faces",
+    near, codes = neighbours.T, faces.transpose(1, 0, 2)
+    velocity, inner = call(
+        inner_kernel,
+        "inner",
         (shape(3, BOX_DEV, 128), shape(BOX_DEV, 256)),
-        [("s", where), ("s", neighbours.T), ("v", nodes), ("v", d), ("v", low), ("v", high)]
-        + [("v", faces.transpose(1, 0, 2))],
+        [("s", where), ("s", near), ("v", nodes), ("v", d), ("v", codes)],
+        [
+            pltpu.VMEM((8 * BOX_DEV, 128), F),
+            pltpu.VMEM((3, 16 * BOX_DEV, 128), F),
+            pltpu.VMEM((6 * BOX_DEV, 128), I),
+        ],
+        us=6,
+    )
+    (swept,) = call(
+        edge_kernel,
+        "edges",
+        (shape(BOX_DEV, 256),),
+        [("s", where), ("s", near), ("v", nodes), ("v", d), ("v", low), ("v", high), ("v", codes), ("v", inner)],
         [
             pltpu.VMEM((8 * NEAR, 128), F),
-            pltpu.VMEM((3, 1024, 128), F),
+            pltpu.VMEM((3, 128, 128), F),
             pltpu.VMEM((6 * BOX_DEV, 128), I),
         ],
     )

time: 137 us -> 134 us (0.978); the launches traced: 135 us -> 133 us
  waiting for transfers between devices: 22.2 us -> 20.8 us
    ppermute x1, waiting for transfers between devices: 1.41 us -> 0.01 us  [body(): high = lax.ppermute(down, 'vol', [(i + 1, i) for i in range(31)])]
    pallas_call x6 -> x7, Pallas kernels: 56.6 us -> 56.6 us  [call(): pl.pallas_call(kernel, name=name, out_shape=outs, in_specs=specs, out_spe...]
  transfers between devices with their start and end apart: 6 -> 6, of which waited for: 4 -> 3; matrix products, arithmetic and copies ran while one was open for 0% -> 0% of each run, Pallas kernels for 6% -> 10%
where the time goes in v4:
time: 134 us; the launch traced here: 133 us
  Pallas kernels  56.6 us (42%)
  blocking collectives  28.6 us (21%)
  starting transfers between devices  21.8 us (16%)
  waiting for transfers between devices  20.8 us (16%)
  local copies, waits for them, and re-layouts  4.54 us (3%)
    pallas_call x7, Pallas kernels, call(): pl.pallas_call(kernel, name=name, out_shape=outs, in_specs=specs, out_spe...  56.6 us
    all_to_all x1, blocking collectives, to_all(): lax.all_to_all(packets, BOTH, split_axis=0, concat_axis=0, tiled=True)  28.6 us
    all_to_all x1, waiting for transfers between devices, to_all(): lax.all_to_all(packets, BOTH, split_axis=0, concat_axis=0, tiled=True)  15.8 us
    all_to_all x1, starting transfers between devices, to_all(): lax.all_to_all(packets, BOTH, split_axis=0, concat_axis=0, tiled=True)  10.4 us
    ppermute x1, starting transfers between devices, body(): high = lax.ppermute(down, 'vol', [(i + 1, i) for i in range(31)])  5.75 us
    ppermute x3, waiting for transfers between devices, around(): lax.ppermute(array, 'surf', [(i, (i + k) % 4) for i in range(4)])  5.07 us
    unnamed x22, local copies, waits for them, and re-layouts  4.54 us
    ppermute x3, starting transfers between devices, around(): lax.ppermute(array, 'surf', [(i, (i + k) % 4) for i in range(4)])  3.65 us
  transfers between devices with their start and end apart: 6, of which 3 were waited for; matrix products, arithmetic and copies ran while one was open for 0% of the time, Pallas kernels for 10%

profile of v4, /device:TPU:8, one launch (start us, length us, event | category | flops | bytes accessed | tf_op | source)
XLA Modules:
  0.0 133.1 jit_solution(15767390367245529043)
XLA Ops:
  0.6 0.0 copy-start.3
  0.6 0.9 copy-done.3
  1.5 0.0 copy-start.6
  1.5 0.7 copy-done.6
  2.2 2.7 %prep.1 = f32[3200,128]{1,0:T(8,128)} custom-call(s32[16,64]{1,0:T(8,128)S(1)} %bitcast.27, f32[3,64,128]{2,1,0:T(8,128)S(1)} %bitcast.23), custom_call_target="tpu_custom_call" | custom-call | flops 2000000000 | bytes 2000000 | tf_op jit(solution)/shard_map/prep/pallas_call | solution.py:29
  4.9 0.0 copy-start.1
  4.9 0.0 copy-start.2
  4.9 0.0 copy-start.5
  4.9 10.4 %all-to-all-start = ((f32[128,25,1,128]{3,2,1,0:T(1,128)}), f32[128,25,1,128]{3,2,1,0:T(1,128)S(1)}, u32[]{:S(2)}, u32[]{:S(2)}) async-start(f32[128,25,1,128]{3,2,1,0:T(1,128)} %bitcast.6), calls=%async_computation | async-start | bytes 3276800 | tf_op jit(solution)/shard_map/all_to_all | solution.py:296
  15.4 0.0 copy-done.1
  15.4 0.0 copy-done.2
  15.4 0.0 copy-done.5
  15.4 7.4 %feats.1 = (bf16[8192,128]{1,0:T(8,128)(2,1)S(1)}, bf16[1024,256]{1,0:T(8,128)(2,1)S(1)}) custom-call(f32[3,64,128]{2,1,0:T(8,128)S(1)} %bitcast.21, f32[3,64,128]{2,1,0:T(8,128)S(1)} %bitcast.22, f32[64,128]{1,0:T(8,128)S(1)} %copy-done.5), custom_call_target="tpu_custom_call" | custom-call | flops 10000000000 | bytes 10000000 | tf_op jit(solution)/shard_map/feats/pallas_call | solution.py:29
  22.8 0.0 copy-start.9
  22.9 1.3 %copy-done.9 = bf16[8192,128]{1,0:T(8,128)(2,1)} copy-done((bf16[8192,128]{1,0:T(8,128)(2,1)}, bf16[8192,128]{1,0:T(8,128)(2,1)S(1)}, u32[]{:S(2)}) %copy-start.9) | copy-done | bytes 2097176
  24.2 15.8 %all-to-all-done = f32[128,25,1,128]{3,2,1,0:T(1,128)S(1)} async-done(((f32[128,25,1,128]{3,2,1,0:T(1,128)}), f32[128,25,1,128]{3,2,1,0:T(1,128)S(1)}, u32[]{:S(2)}, u32[]{:S(2)}) %all-to-all-start) | async-done | bytes 1638432 | tf_op jit(solution)/shard_map/all_to_all | solution.py:296
  39.9 0.0 copy-start.10
  39.9 1.6 %copy-done.10 = bf16[8192,128]{1,0:T(8,128)(2,1)S(1)} copy-done((bf16[8192,128]{1,0:T(8,128)(2,1)S(1)}, bf16[8192,128]{1,0:T(8,128)(2,1)}, u32[]{:S(2)}) %copy-start.10) | copy-done | bytes 2097176
  41.5 37.2 %terms.1 = f32[3072,128]{1,0:T(8,128)S(1)} custom-call(f32[3200,128]{1,0:T(8,128)S(1)} %bitcast.16, bf16[8192,128]{1,0:T(8,128)(2,1)S(1)} %copy-done.10, bf16[1024,256]{1,0:T(8,128)(2,1)S(1)} %get-tuple-element.10.cf_ref), custom_call_target="tpu_custom_call" | custom-call | flops 44999999488 | bytes 45000000 | tf_op jit(solution)/shard_map/terms/pallas_call | solution.py:29
  78.8 0.0 copy-start.7
  78.8 28.6 %all_to_all.10 = f32[128,24,1,128]{3,1,2,0:T(8,128)S(1)} all-to-all(f32[128,24,1,128]{3,1,2,0:T(8,128)S(1)} %bitcast.17), channel_id=1, replica_groups=mesh['vol'=32,'surf'=4] {'vol','surf'}, dimensions={0} | all-to-all | bytes 3145728 | tf_op jit(solution)/shard_map/all_to_all | solution.py:296
  107.4 0.0 copy-done.7
  107.4 0.0 copy-start.4
  107.4 1.5 %sums.1.own_ref = f32[192,128]{1,0:T(8,128)S(1)} custom-call(s32[16,64]{1,0:T(8,128)S(1)} %bitcast.28, f32[3072,128]{1,0:T(8,128)S(1)} %bitcast.18), custom_call_target="tpu_custom_call" | custom-call | flops 2000000000 | bytes 2000000 | tf_op jit(solution)/shard_map/sums/pallas_call | solution.py:29
  108.9 0.9 collective-permute-start
  109.8 1.7 %collective-permute-start.1 = (f32[192,128]{1,0:T(8,128)S(1)}, f32[192,128]{1,0:T(8,128)S(1)}, u32[]{:S(2)}, u32[]{:S(2)}) collective-permute-start(f32[192,128]{1,0:T(8,128)S(1)} %sums.1.own_ref), channel_id=1, source_target_pairs={{0,2},{1,3},{2,0},{3,1},{4,6},{5,7},{6,4},{7,5},{8,10},{9,11},{10,... | collective-permute-start | bytes 294920 | tf_op jit(solution)/shard_map/ppermute | solution.py:301
  111.6 1.0 collective-permute-start.2
  112.6 0.0 copy-start
  112.6 0.0 copy-start.8
  112.6 4.5 %collective-permute-done.one_ref = f32[192,128]{1,0:T(8,128)S(1)} collective-permute-done((f32[192,128]{1,0:T(8,128)S(1)}, f32[192,128]{1,0:T(8,128)S(1)}, u32[]{:S(2)}, u32[]{:S(2)}) %collective-permute-start) | collective-permute-done | bytes 98336 | tf_op jit(solution)/shard_map/ppermute | solution.py:301
  117.1 0.0 collective-permute-done.1.two_ref
  117.1 0.6 collective-permute-done.2.three_ref
  117.7 0.0 copy-done.4
  117.7 1.9 %collective-permute-start.3 = (f32[32,128]{1,0:T(8,128)S(1)}, f32[32,128]{1,0:T(8,128)S(1)}, u32[]{:S(2)}, u32[]{:S(2)}) collective-permute-start(f32[32,128]{1,0:T(8,128)S(1)} %get-tuple-element.13), channel_id=1, source_target_pairs={{0,4},{4,8},{8,12},{12,16},{16,20},{20,24},{24,28},{28,32},{32,36}... | collective-permute-start | bytes 49160 | tf_op jit(solution)/shard_map/ppermute | solution.py:355
  119.6 5.8 %collective-permute-start.4 = (f32[32,128]{1,0:T(8,128)S(1)}, f32[32,128]{1,0:T(8,128)S(1)}, u32[]{:S(2)}, u32[]{:S(2)}) collective-permute-start(f32[32,128]{1,0:T(8,128)S(1)} %get-tuple-element.14), channel_id=1, source_target_pairs={{4,0},{8,4},{12,8},{16,12},{20,16},{24,20},{28,24},{32,28},{36,32}... | collective-permute-start | bytes 49160 | tf_op jit(solution)/shard_map/ppermute | solution.py:356
  125.4 0.0 copy-done
  125.4 0.0 copy-done.8
  125.4 5.7 %inner.1 = (f32[3,64,128]{2,1,0:T(8,128)}, f32[64,256]{1,0:T(8,128)S(1)}) custom-call(s32[1]{0:T(128)} %bitcast.where_ref, s32[8,64]{1,0:T(8,128)S(1)} %bitcast.29, f32[3,64,128]{2,1,0:T(8,128)S(1)} %bitcast.25, f32[192,128]{1,0:T(8,128)S(1)} %get-tuple-element.11.d_ref, s32[3,64,256]{2,1,0:T(8,128)S(1)} %bitcast.19), custom_call_target="tpu_custom_call" | custom-call | flops 6000000000 | bytes 6000000 | tf_op jit(solution)/shard_map/inner/pallas_call | solution.py:29
  131.2 0.0 collective-permute-done.3.low_ref
  131.2 0.0 collective-permute-done.4.high_ref
  131.2 2.0 %edges.1 = f32[64,256]{1,0:T(8,128)} custom-call(s32[1]{0:T(128)} %bitcast.where_ref, s32[8,64]{1,0:T(8,128)S(1)} %bitcast.30, f32[3,64,128]{2,1,0:T(8,128)S(1)} %bitcast.26, f32[192,128]{1,0:T(8,128)S(1)} %get-tuple-element.11.d_ref, f32[32,128]{1,0:T(8,128)S(1)} %collective-permute-done.3.low_ref, f32[32,128]{1,0:T(8,128)S(1)} %collective-permute-done.4.high_ref, ...), custom_call_target="tpu_custom_call" | custom-call | flops 2000000000 | bytes 2000000 | tf_op jit(solution)/shard_map/edges/pallas_call | solution.py:29
  (1 shorter events, 0.0 us)
Async XLA Ops:
  0.6 0.9 copy-start.3
  1.5 0.7 copy-start.6
  4.9 10.5 %copy-start.1 = (f32[64,3,128]{2,0,1:T(8,128)S(1)}, f32[64,3,128]{2,0,1:T(8,128)}, u32[]{:S(2)}) copy-start(f32[64,3,128]{2,0,1:T(8,128)} %param.8) | copy-start | bytes 294916
  4.9 10.5 %copy-start.2 = (f32[64,3,128]{2,0,1:T(8,128)S(1)}, f32[64,3,128]{2,0,1:T(8,128)}, u32[]{:S(2)}) copy-start(f32[64,3,128]{2,0,1:T(8,128)} %param.9) | copy-start | bytes 294916
  4.9 10.5 %copy-start.5 = (f32[64,128]{1,0:T(8,128)S(1)}, f32[64,128]{1,0:T(8,128)}, u32[]{:S(2)}) copy-start(f32[64,128]{1,0:T(8,128)} %rad_ref.1) | copy-start | bytes 98308
  4.9 35.0 %all-to-all-start = ((f32[128,25,1,128]{3,2,1,0:T(1,128)}), f32[128,25,1,128]{3,2,1,0:T(1,128)S(1)}, u32[]{:S(2)}, u32[]{:S(2)}) async-start(f32[128,25,1,128]{3,2,1,0:T(1,128)} %bitcast.6), calls=%async_computation | async-start | bytes 3276800 | tf_op jit(solution)/shard_map/all_to_all | solution.py:296
  22.8 1.3 %copy-start.9 = (bf16[8192,128]{1,0:T(8,128)(2,1)}, bf16[8192,128]{1,0:T(8,128)(2,1)S(1)}, u32[]{:S(2)}) copy-start(bf16[8192,128]{1,0:T(8,128)(2,1)S(1)} %get-tuple-element.9.a_ref) | copy-start | bytes 6291460
  39.9 1.6 %copy-start.10 = (bf16[8192,128]{1,0:T(8,128)(2,1)S(1)}, bf16[8192,128]{1,0:T(8,128)(2,1)}, u32[]{:S(2)}) copy-start(bf16[8192,128]{1,0:T(8,128)(2,1)} %copy-done.9) | copy-start | bytes 6291460
  78.8 28.6 %copy-start.7 = (s32[1,64,16]{1,2,0:T(8,128)S(1)}, s32[1,64,16]{1,2,0:T(8,128)}, u32[]{:S(2)}) copy-start(s32[1,64,16]{1,2,0:T(8,128)} %param.11) | copy-start | bytes 12292
  107.4 10.2 %copy-start.4 = (f32[64,3,128]{2,0,1:T(8,128)S(1)}, f32[64,3,128]{2,0,1:T(8,128)}, u32[]{:S(2)}) copy-start(f32[64,3,128]{2,0,1:T(8,128)} %param.7) | copy-start | bytes 294916
  108.9 8.2 %collective-permute-start = (f32[192,128]{1,0:T(8,128)S(1)}, f32[192,128]{1,0:T(8,128)S(1)}, u32[]{:S(2)}, u32[]{:S(2)}) collective-permute-start(f32[192,128]{1,0:T(8,128)S(1)} %sums.1.own_ref), channel_id=1, source_target_pairs={{0,1},{1,2},{2,3},{3,0},{4,5},{5,6},{6,7},{7,4},{8,9},{9,10},{10,1... | collective-permute-start | bytes 294920 | tf_op jit(solution)/shard_map/ppermute | solution.py:301
  109.8 7.3 %collective-permute-start.1 = (f32[192,128]{1,0:T(8,128)S(1)}, f32[192,128]{1,0:T(8,128)S(1)}, u32[]{:S(2)}, u32[]{:S(2)}) collective-permute-start(f32[192,128]{1,0:T(8,128)S(1)} %sums.1.own_ref), channel_id=1, source_target_pairs={{0,2},{1,3},{2,0},{3,1},{4,6},{5,7},{6,4},{7,5},{8,10},{9,11},{10,... | collective-permute-start | bytes 294920 | tf_op jit(solution)/shard_map/ppermute | solution.py:301
  111.6 6.1 %collective-permute-start.2 = (f32[192,128]{1,0:T(8,128)S(1)}, f32[192,128]{1,0:T(8,128)S(1)}, u32[]{:S(2)}, u32[]{:S(2)}) collective-permute-start(f32[192,128]{1,0:T(8,128)S(1)} %sums.1.own_ref), channel_id=1, source_target_pairs={{0,3},{1,0},{2,1},{3,2},{4,7},{5,4},{6,5},{7,6},{8,11},{9,8},{10,9... | collective-permute-start | bytes 294920 | tf_op jit(solution)/shard_map/ppermute | solution.py:301
  112.6 12.8 %copy-start = (s32[64,3,256]{2,0,1:T(8,128)S(1)}, s32[64,3,256]{2,0,1:T(8,128)}, u32[]{:S(2)}) copy-start(s32[64,3,256]{2,0,1:T(8,128)} %param.13) | copy-start | bytes 589828
  112.6 12.8 %copy-start.8 = (s32[64,8]{0,1:T(8,128)S(1)}, s32[64,8]{0,1:T(8,128)}, u32[]{:S(2)}) copy-start(s32[64,8]{0,1:T(8,128)} %param.12) | copy-start | bytes 6148
  117.7 13.5 %collective-permute-start.3 = (f32[32,128]{1,0:T(8,128)S(1)}, f32[32,128]{1,0:T(8,128)S(1)}, u32[]{:S(2)}, u32[]{:S(2)}) collective-permute-start(f32[32,128]{1,0:T(8,128)S(1)} %get-tuple-element.13), channel_id=1, source_target_pairs={{0,4},{4,8},{8,12},{12,16},{16,20},{20,24},{24,28},{28,32},{32,36}... | collective-permute-start | bytes 49160 | tf_op jit(solution)/shard_map/ppermute | solution.py:355
  119.6 11.5 %collective-permute-start.4 = (f32[32,128]{1,0:T(8,128)S(1)}, f32[32,128]{1,0:T(8,128)S(1)}, u32[]{:S(2)}, u32[]{:S(2)}) collective-permute-start(f32[32,128]{1,0:T(8,128)S(1)} %get-tuple-element.14), channel_id=1, source_target_pairs={{4,0},{8,4},{12,8},{16,12},{20,16},{24,20},{28,24},{32,28},{36,32}... | collective-permute-start | bytes 49160 | tf_op jit(solution)/shard_map/ppermute | solution.py:356

commit v5 on v4

--- a/solution.py
+++ b/solution.py
@@ -80,22 +80,33 @@
     o_ref[pl.ds(ASK - 1, DEVICES, stride=ASK), :] = stacked
 
 
-def feat_kernel(cen_ref, coef_ref, rad_ref, a_ref, cf_ref):
-    def one(g, carry):
-        c = cen_ref[:, pl.ds(g, 1), :].reshape(3, 128)
-        r = rad_ref[pl.ds(g, 1), :]
-        inv = 1.0 / (r * r)
-        sq = c[0:1] * c[0:1] + c[1:2] * c[1:2] + c[2:3] * c[2:3]
-        f = jnp.concatenate([c * (-2.0 * inv), inv, inv * sq, jnp.zeros((3, 128), F)], 0)
-        p, q, t = split3(f)
-        s = jnp.concatenate([p, p, p, q, q, t, jnp.zeros((80, 128), F)], 0)
-        a_ref[pl.ds(pl.multiple_of(g * 128, 128), 128), :] = s.T.astype(BF)
-        ks = split3(4.0 * coef_ref[:, pl.ds(g, 1), :].reshape(3, 128))
-        z = jnp.concatenate([ks[0], ks[1], jnp.zeros((10, 128), F)], 0).astype(BF)
-        cf_ref[pl.ds(pl.multiple_of(g * 16, 16), 16), :] = jnp.concatenate([z, z], 1)
-        return carry
-
-    lax.fori_loop(0, 64, one, 0)
+def feat_kernel(where_ref, own_ref, one_ref, two_ref, three_ref, a_ref, cf_ref):
+    for k, ref in enumerate((own_ref, one_ref, two_ref, three_ref)):
+        first = ((where_ref[1] + 4 - k) & 3) * BOX_DEV
+
+        def some(h, carry):
+            base = pl.multiple_of(h * 8, 8)
+            x, y, z, r, kx, ky, kz = [ref[pl.ds(c * BOX_DEV + base, 8), :] for c in range(7)]
+            inv = 1.0 / (r * r)
+            scale = -2.0 * inv
+            rows = [x * scale, y * scale, z * scale, inv, inv * (x * x + y * y + z * z)]
+            rows = [split3(t) for t in rows]
+            ks = [split3(4.0 * t) for t in (kx, ky, kz)]
+            for u in range(8):
+                def part(n):
+                    return [t[n][u : u + 1] for t in rows] + [jnp.zeros((3, 128), F)]
+
+                p, q, t = part(0), part(1), part(2)
+                s = jnp.concatenate(p * 3 + q * 2 + t, 0).astype(BF)
+                at = first + base + u
+                a_ref[pl.ds(pl.multiple_of(at * 48, 16), 48), :] = s
+                c = jnp.concatenate(
+                    [t[n][u : u + 1] for n in range(2) for t in ks] + [jnp.zeros((10, 128), F)], 0
+                ).astype(BF)
+                cf_ref[pl.ds(pl.multiple_of(at * 16, 16), 16), :] = c
+            return carry
+
+        lax.fori_loop(0, BOX_DEV // 8, some, 0)
 
 
 def terms_kernel(
@@ -105,8 +116,6 @@
     copy = pltpu.make_async_copy(stage_ref, ids_ref, sem)
     copy.start()
     for buf in range(2):
-        for j in range(SLOTS):
-            b_ref[buf, j, 48:128, :] = jnp.zeros((80, 128), BF)
         for k in range(3):
             v_ref[buf, k, pl.ds(32, 32), :] = jnp.zeros((32, 128), F)
         v_ref[buf, 0, pl.ds(32, 8), :] = jnp.ones((8, 128), F)
@@ -124,14 +133,17 @@
                 v_ref[buf, k, pl.ds(f * 8, 8), :] = part
         for j in range(SLOTS):
             v = [v_ref[buf, k, pl.ds(j, 8, stride=8), :] for k in range(3)]
-            b_ref[buf, j, 0:48, :] = jnp.concatenate(
+            b_ref[buf, j] = jnp.concatenate(
                 [v[0], v[1], v[2], v[0], v[1], v[0]], 0
             ).astype(BF)
 
     def stage1(i, buf, j):
-        g = ids_ref[j, jnp.minimum(i, DEVICES - 1)]
-        a = a_ref[pl.ds(pl.multiple_of(g * 128, 128), 128), :]
-        q_ref[buf, j] = jnp.dot(a, b_ref[buf, j], preferred_element_type=F)
+        i = jnp.minimum(i, DEVICES - 1)
+        g = (i & 3) * BOX_DEV + ids_ref[j, i]
+        a = a_ref[pl.ds(pl.multiple_of(g * 48, 16), 48), :]
+        q_ref[buf, j] = lax.dot_general(
+            a, b_ref[buf, j], (((0,), (0,)), ((), ())), preferred_element_type=F
+        )
 
     def stage2(buf, j):
         m = jnp.maximum(q_ref[buf, j], TINY)
@@ -144,8 +156,9 @@
         w_ref[buf, j, 128:256, :] = (w - high.astype(F)).astype(BF)
 
     def stage3(i, buf, j):
-        g = ids_ref[j, i]
+        g = (i & 3) * BOX_DEV + ids_ref[j, i]
         c = cf_ref[pl.ds(pl.multiple_of(g * 16, 16), 16), :]
+        c = jnp.concatenate([c, c], 1)
         r = jnp.dot(c, w_ref[buf, j], preferred_element_type=F)
         r_ref[buf, pl.ds(j, 6, stride=SLOTS), :] = r[0:6]
 
@@ -291,10 +304,11 @@
 
 
 def to_all(array):
-    rows = array.shape[0] // DEVICES
-    packets = array.reshape(DEVICES, rows, 1, 128)
-    packets = lax.all_to_all(packets, BOTH, split_axis=0, concat_axis=0, tiled=True)
-    return packets.reshape(DEVICES * rows, 128)
+    peers = DEVICES // 4
+    rows = array.shape[0] // peers
+    packets = array.reshape(peers, rows, 1, 128)
+    packets = lax.all_to_all(packets, "vol", split_axis=0, concat_axis=0, tiled=True)
+    return packets.reshape(peers * rows, 128)
 
 
 def around(array):
@@ -308,7 +322,10 @@
 def body(node_pos, centres, coefs, radii, block_list, neighbours, faces):
     listed = block_list[0].T
     nodes, cens, weights = [a.transpose(1, 0, 2) for a in (node_pos, centres, coefs)]
-    where = lax.axis_index("vol").astype(I).reshape(1)
+    where = jnp.stack([lax.axis_index("vol"), lax.axis_index("surf")]).astype(I)
+    blocks = jnp.concatenate(
+        [cens.reshape(3 * BOX_DEV, 128), radii, weights.reshape(3 * BOX_DEV, 128)], 0
+    )
     (sent,) = call(
         prep_kernel,
         "prep",
@@ -318,9 +335,9 @@
     tables = call(
         feat_kernel,
         "feats",
-        (shape(64 * 128, 128, kind=BF), shape(64 * 16, 256, kind=BF)),
-        [("v", cens), ("v", weights), ("v", radii)],
-        us=10,
+        (shape(4 * BOX_DEV * 48, 128, kind=BF), shape(4 * BOX_DEV * 16, 128, kind=BF)),
+        [("s", where), ("v", blocks)] + [("v", r) for r in around(blocks)],
+        us=5,
     )
     (terms,) = call(
         terms_kernel,
@@ -329,7 +346,7 @@
         [("v", to_all(sent)), ("v", tables[0]), ("v", tables[1])],
         [
             pltpu.VMEM((2, 3, 64, 128), F),
-            pltpu.VMEM((2, SLOTS, 128, 128), BF),
+            pltpu.VMEM((2, SLOTS, 48, 128), BF),
             pltpu.VMEM((2, SLOTS, 128, 128), F),
             pltpu.VMEM((2, SLOTS, 256, 128), BF),
             pltpu.VMEM((2, 2 * GIVE, 128), F),

time: 134 us -> 131 us (0.978)
  Pallas kernels: 56.6 us -> 51.3 us
  local copies, waits for them, and re-layouts: 4.54 us -> 7.36 us
  starting transfers between devices: 21.8 us -> 23.7 us
    all_to_all x1, waiting for transfers between devices: 15.8 us -> 0.01 us  [to_all(): lax.all_to_all(packets, 'vol', split_axis=0, concat_axis=0, tiled=True)]
    ppermute x3 -> x6, waiting for transfers between devices: 5.07 us -> 19.5 us  [around(): lax.ppermute(array, 'surf', [(i, (i + k) % 4) for i in range(4)])]
    pallas_call x7, Pallas kernels: 56.6 us -> 51.3 us  [call(): pl.pallas_call(kernel, name=name, out_shape=outs, in_specs=specs, out_spe...]
    ppermute x3 -> x6, starting transfers between devices: 3.65 us -> 8.39 us  [around(): lax.ppermute(array, 'surf', [(i, (i + k) % 4) for i in range(4)])]
    unnamed x22 -> x26, local copies, waits for them, and re-layouts: 4.54 us -> 7.36 us
    all_to_all x1, starting transfers between devices: 10.4 us -> 7.67 us  [to_all(): lax.all_to_all(packets, 'vol', split_axis=0, concat_axis=0, tiled=True)]
  transfers between devices with their start and end apart: 6 -> 9, of which waited for: 3 -> 5; matrix products, arithmetic and copies ran while one was open for 0% -> 0% of each run, Pallas kernels for 10% -> 6%
where the time goes in v5:
time: 131 us
  Pallas kernels  51.3 us (39%)
  blocking collectives  28.1 us (21%)
  starting transfers between devices  23.7 us (18%)
  waiting for transfers between devices  19.5 us (15%)
  local copies, waits for them, and re-layouts  7.36 us (6%)
    pallas_call x7, Pallas kernels, call(): pl.pallas_call(kernel, name=name, out_shape=outs, in_specs=specs, out_spe...  51.3 us
    all_to_all x1, blocking collectives, to_all(): lax.all_to_all(packets, 'vol', split_axis=0, concat_axis=0, tiled=True)  28.1 us
    ppermute x6, waiting for transfers between devices, around(): lax.ppermute(array, 'surf', [(i, (i + k) % 4) for i in range(4)])  19.5 us
    ppermute x6, starting transfers between devices, around(): lax.ppermute(array, 'surf', [(i, (i + k) % 4) for i in range(4)])  8.39 us
    all_to_all x1, starting transfers between devices, to_all(): lax.all_to_all(packets, 'vol', split_axis=0, concat_axis=0, tiled=True)  7.67 us
    unnamed x26, local copies, waits for them, and re-layouts  7.36 us
    ppermute x1, starting transfers between devices, body(): high = lax.ppermute(down, 'vol', [(i + 1, i) for i in range(31)])  5.75 us
  transfers between devices with their start and end apart: 9, of which 5 were waited for; matrix products, arithmetic and copies ran while one was open for 0% of the time, Pallas kernels for 6%

profile of v5, /device:TPU:8, one launch (start us, length us, event | category | flops | bytes accessed | tf_op | source)
XLA Modules:
  0.0 130.8 jit_solution(2389791498150506262)
XLA Ops:
  0.6 0.0 copy-start.1
  0.6 0.9 copy-done.1
  1.5 0.0 copy-start.3
  1.5 0.7 copy-done.3
  2.2 2.7 %prep.1 = f32[3200,128]{1,0:T(8,128)} custom-call(s32[16,64]{1,0:T(8,128)S(1)} %bitcast.30, f32[3,64,128]{2,1,0:T(8,128)S(1)} %bitcast.26), custom_call_target="tpu_custom_call" | custom-call | flops 2000000000 | bytes 2000000 | tf_op jit(solution)/shard_map/prep/pallas_call | solution.py:29
  5.0 0.0 copy-start.10
  5.0 0.0 copy-start.11
  5.0 0.0 copy-start.12
  5.0 7.7 %all-to-all-start = ((f32[32,100,1,128]{3,2,1,0:T(1,128)}), f32[32,100,1,128]{3,2,1,0:T(1,128)S(1)}, u32[]{:S(2)}, u32[]{:S(2)}) async-start(f32[32,100,1,128]{3,2,1,0:T(1,128)} %bitcast.7), calls=%async_computation | async-start | bytes 3276800 | tf_op jit(solution)/shard_map/all_to_all | solution.py:310
  12.6 0.0 copy-done.10
  12.6 0.0 copy-done.11
  12.7 0.0 copy-done.12
  12.7 4.1 %collective-permute-start.2 = (f32[448,128]{1,0:T(8,128)S(1)}, f32[448,128]{1,0:T(8,128)S(1)}, u32[]{:S(2)}, u32[]{:S(2)}) collective-permute-start(f32[448,128]{1,0:T(8,128)S(1)} %pad_maximum_fusion.own_ref), channel_id=1, source_target_pairs={{0,3},{1,0},{2,1},{3,2},{4,7},{5,4},{6,5},{7,6},{8,11},{9,8},{10,9... | collective-permute-start | bytes 688136 | tf_op jit(solution)/shard_map/ppermute | solution.py:315
  16.8 0.0 collective-permute-start.1
  16.8 1.3 collective-permute-start
  18.1 0.1 pad_add_fusion.where_ref
  18.1 8.7 %collective-permute-done.2.three_ref = f32[448,128]{1,0:T(8,128)S(1)} collective-permute-done((f32[448,128]{1,0:T(8,128)S(1)}, f32[448,128]{1,0:T(8,128)S(1)}, u32[]{:S(2)}, u32[]{:S(2)}) %collective-permute-start.2) | collective-permute-done | bytes 229408 | tf_op jit(solution)/shard_map/ppermute | solution.py:315
  26.9 0.0 collective-permute-done.1.two_ref
  26.9 3.4 %collective-permute-done.one_ref = f32[448,128]{1,0:T(8,128)S(1)} collective-permute-done((f32[448,128]{1,0:T(8,128)S(1)}, f32[448,128]{1,0:T(8,128)S(1)}, u32[]{:S(2)}, u32[]{:S(2)}) %collective-permute-start) | collective-permute-done | bytes 229408 | tf_op jit(solution)/shard_map/ppermute | solution.py:315
  30.3 2.6 %feats.1 = (bf16[12288,128]{1,0:T(8,128)(2,1)S(1)}, bf16[4096,128]{1,0:T(8,128)(2,1)S(1)}) custom-call(s32[2]{0:T(128)S(1)} %pad_add_fusion.where_ref, f32[448,128]{1,0:T(8,128)S(1)} %pad_maximum_fusion.own_ref, f32[448,128]{1,0:T(8,128)S(1)} %collective-permute-done.one_ref, f32[448,128]{1,0:T(8,128)S(1)} %collective-permute-done.1.two_ref, ...), custom_call_target="tpu_custom_call" | custom-call | flops 5000000000 | bytes 5000000 | tf_op jit(solution)/shard_map/feats/pallas_call | solution.py:29
  32.8 0.0 copy-start.6
  32.8 1.6 %copy-done.6 = bf16[12288,128]{1,0:T(8,128)(2,1)} copy-done((bf16[12288,128]{1,0:T(8,128)(2,1)}, bf16[12288,128]{1,0:T(8,128)(2,1)S(1)}, u32[]{:S(2)}) %copy-start.6) | copy-done | bytes 3145752
  34.5 1.0 copy-done.8
  35.5 0.0 all-to-all-done
  35.5 1.9 %copy-done.7 = bf16[12288,128]{1,0:T(8,128)(2,1)S(1)} copy-done((bf16[12288,128]{1,0:T(8,128)(2,1)S(1)}, bf16[12288,128]{1,0:T(8,128)(2,1)}, u32[]{:S(2)}) %copy-start.7) | copy-done | bytes 3145752
  37.4 1.2 copy-done.9
  38.6 36.7 %terms.1 = f32[3072,128]{1,0:T(8,128)S(1)} custom-call(f32[3200,128]{1,0:T(8,128)S(1)} %bitcast.21, bf16[12288,128]{1,0:T(8,128)(2,1)S(1)} %copy-done.7, bf16[4096,128]{1,0:T(8,128)(2,1)S(1)} %copy-done.9), custom_call_target="tpu_custom_call" | custom-call | flops 44999999488 | bytes 45000000 | tf_op jit(solution)/shard_map/terms/pallas_call | solution.py:29
  75.3 0.0 copy-start.4
  75.4 28.1 %all_to_all.10 = f32[32,96,1,128]{3,1,2,0:T(8,128)S(1)} all-to-all(f32[32,96,1,128]{3,1,2,0:T(8,128)S(1)} %bitcast.22), channel_id=1, replica_groups=mesh['vol'=32,'surf'=4] {'vol'}, dimensions={0} | all-to-all | bytes 3145728 | tf_op jit(solution)/shard_map/all_to_all | solution.py:310
  103.4 0.0 copy-done.4
  103.4 1.5 %sums.1.own_ref = f32[192,128]{1,0:T(8,128)S(1)} custom-call(s32[16,64]{1,0:T(8,128)S(1)} %bitcast.31, f32[3072,128]{1,0:T(8,128)S(1)} %bitcast.23), custom_call_target="tpu_custom_call" | custom-call | flops 2000000000 | bytes 2000000 | tf_op jit(solution)/shard_map/sums/pallas_call | solution.py:29
  104.9 0.0 copy-start
  104.9 0.0 copy-start.5
  105.0 1.8 %collective-permute-start.5 = (f32[192,128]{1,0:T(8,128)S(1)}, f32[192,128]{1,0:T(8,128)S(1)}, u32[]{:S(2)}, u32[]{:S(2)}) collective-permute-start(f32[192,128]{1,0:T(8,128)S(1)} %sums.1.own_ref), channel_id=1, source_target_pairs={{0,3},{1,0},{2,1},{3,2},{4,7},{5,4},{6,5},{7,6},{8,11},{9,8},{10,9... | collective-permute-start | bytes 294920 | tf_op jit(solution)/shard_map/ppermute | solution.py:315
  106.7 0.0 collective-permute-start.4
  106.7 1.2 collective-permute-start.3
  108.0 2.7 %collective-permute-done.5.three_ref = f32[192,128]{1,0:T(8,128)S(1)} collective-permute-done((f32[192,128]{1,0:T(8,128)S(1)}, f32[192,128]{1,0:T(8,128)S(1)}, u32[]{:S(2)}, u32[]{:S(2)}) %collective-permute-start.5) | collective-permute-done | bytes 98336 | tf_op jit(solution)/shard_map/ppermute | solution.py:315
  110.7 3.2 %collective-permute-done.4.two_ref = f32[192,128]{1,0:T(8,128)S(1)} collective-permute-done((f32[192,128]{1,0:T(8,128)S(1)}, f32[192,128]{1,0:T(8,128)S(1)}, u32[]{:S(2)}, u32[]{:S(2)}) %collective-permute-start.4) | collective-permute-done | bytes 98336 | tf_op jit(solution)/shard_map/ppermute | solution.py:315
  113.9 1.4 %collective-permute-done.3.one_ref = f32[192,128]{1,0:T(8,128)S(1)} collective-permute-done((f32[192,128]{1,0:T(8,128)S(1)}, f32[192,128]{1,0:T(8,128)S(1)}, u32[]{:S(2)}, u32[]{:S(2)}) %collective-permute-start.3) | collective-permute-done | bytes 98336 | tf_op jit(solution)/shard_map/ppermute | solution.py:315
  115.4 0.0 copy-done.2
  115.4 1.9 %collective-permute-start.6 = (f32[32,128]{1,0:T(8,128)S(1)}, f32[32,128]{1,0:T(8,128)S(1)}, u32[]{:S(2)}, u32[]{:S(2)}) collective-permute-start(f32[32,128]{1,0:T(8,128)S(1)} %get-tuple-element.13), channel_id=1, source_target_pairs={{0,4},{4,8},{8,12},{12,16},{16,20},{20,24},{24,28},{28,32},{32,36}... | collective-permute-start | bytes 49160 | tf_op jit(solution)/shard_map/ppermute | solution.py:372
  117.3 5.8 %collective-permute-start.7 = (f32[32,128]{1,0:T(8,128)S(1)}, f32[32,128]{1,0:T(8,128)S(1)}, u32[]{:S(2)}, u32[]{:S(2)}) collective-permute-start(f32[32,128]{1,0:T(8,128)S(1)} %get-tuple-element.14), channel_id=1, source_target_pairs={{4,0},{8,4},{12,8},{16,12},{20,16},{24,20},{28,24},{32,28},{36,32}... | collective-permute-start | bytes 49160 | tf_op jit(solution)/shard_map/ppermute | solution.py:373
  123.1 0.0 copy-done
  123.1 0.0 copy-done.5
  123.1 5.7 %inner.1 = (f32[3,64,128]{2,1,0:T(8,128)}, f32[64,256]{1,0:T(8,128)S(1)}) custom-call(s32[2]{0:T(128)S(1)} %pad_add_fusion.where_ref, s32[8,64]{1,0:T(8,128)S(1)} %bitcast.32, f32[3,64,128]{2,1,0:T(8,128)S(1)} %bitcast.28, f32[192,128]{1,0:T(8,128)S(1)} %get-tuple-element.11.d_ref, s32[3,64,256]{2,1,0:T(8,128)S(1)} %bitcast.24), custom_call_target="tpu_custom_call" | custom-call | flops 6000000000 | bytes 6000000 | tf_op jit(solution)/shard_map/inner/pallas_call | solution.py:29
  128.8 0.0 collective-permute-done.6.low_ref
  128.8 0.0 collective-permute-done.7.high_ref
  128.8 2.0 %edges.1 = f32[64,256]{1,0:T(8,128)} custom-call(s32[2]{0:T(128)S(1)} %pad_add_fusion.where_ref, s32[8,64]{1,0:T(8,128)S(1)} %bitcast.33, f32[3,64,128]{2,1,0:T(8,128)S(1)} %bitcast.29, f32[192,128]{1,0:T(8,128)S(1)} %get-tuple-element.11.d_ref, f32[32,128]{1,0:T(8,128)S(1)} %collective-permute-done.6.low_ref, ...), custom_call_target="tpu_custom_call" | custom-call | flops 2000000000 | bytes 2000000 | tf_op jit(solution)/shard_map/edges/pallas_call | solution.py:29
  (6 shorter events, 0.1 us)
Async XLA Ops:
  0.6 0.9 copy-start.1
  1.5 0.7 copy-start.3
  5.0 7.7 %copy-start.10 = (f32[64,3,128]{2,0,1:T(8,128)S(1)}, f32[64,3,128]{2,0,1:T(8,128)}, u32[]{:S(2)}) copy-start(f32[64,3,128]{2,0,1:T(8,128)} %param.9) | copy-start | bytes 294916
  5.0 7.7 %copy-start.11 = (f32[64,3,128]{2,0,1:T(8,128)S(1)}, f32[64,3,128]{2,0,1:T(8,128)}, u32[]{:S(2)}) copy-start(f32[64,3,128]{2,0,1:T(8,128)} %param.8) | copy-start | bytes 294916
  5.0 7.7 %copy-start.12 = (f32[64,128]{1,0:T(8,128)S(1)}, f32[64,128]{1,0:T(8,128)}, u32[]{:S(2)}) copy-start(f32[64,128]{1,0:T(8,128)} %param.10) | copy-start | bytes 98308
  5.0 30.5 %all-to-all-start = ((f32[32,100,1,128]{3,2,1,0:T(1,128)}), f32[32,100,1,128]{3,2,1,0:T(1,128)S(1)}, u32[]{:S(2)}, u32[]{:S(2)}) async-start(f32[32,100,1,128]{3,2,1,0:T(1,128)} %bitcast.7), calls=%async_computation | async-start | bytes 3276800 | tf_op jit(solution)/shard_map/all_to_all | solution.py:310
  12.7 14.2 %collective-permute-start.2 = (f32[448,128]{1,0:T(8,128)S(1)}, f32[448,128]{1,0:T(8,128)S(1)}, u32[]{:S(2)}, u32[]{:S(2)}) collective-permute-start(f32[448,128]{1,0:T(8,128)S(1)} %pad_maximum_fusion.own_ref), channel_id=1, source_target_pairs={{0,3},{1,0},{2,1},{3,2},{4,7},{5,4},{6,5},{7,6},{8,11},{9,8},{10,9... | collective-permute-start | bytes 688136 | tf_op jit(solution)/shard_map/ppermute | solution.py:315
  16.8 10.1 %collective-permute-start.1 = (f32[448,128]{1,0:T(8,128)S(1)}, f32[448,128]{1,0:T(8,128)S(1)}, u32[]{:S(2)}, u32[]{:S(2)}) collective-permute-start(f32[448,128]{1,0:T(8,128)S(1)} %pad_maximum_fusion.own_ref), channel_id=1, source_target_pairs={{0,2},{1,3},{2,0},{3,1},{4,6},{5,7},{6,4},{7,5},{8,10},{9,11},{10,... | collective-permute-start | bytes 688136 | tf_op jit(solution)/shard_map/ppermute | solution.py:315
  16.8 13.5 %collective-permute-start = (f32[448,128]{1,0:T(8,128)S(1)}, f32[448,128]{1,0:T(8,128)S(1)}, u32[]{:S(2)}, u32[]{:S(2)}) collective-permute-start(f32[448,128]{1,0:T(8,128)S(1)} %pad_maximum_fusion.own_ref), channel_id=1, source_target_pairs={{0,1},{1,2},{2,3},{3,0},{4,5},{5,6},{6,7},{7,4},{8,9},{9,10},{10,1... | collective-permute-start | bytes 688136 | tf_op jit(solution)/shard_map/ppermute | solution.py:315
  32.8 1.6 %copy-start.6 = (bf16[12288,128]{1,0:T(8,128)(2,1)}, bf16[12288,128]{1,0:T(8,128)(2,1)S(1)}, u32[]{:S(2)}) copy-start(bf16[12288,128]{1,0:T(8,128)(2,1)S(1)} %get-tuple-element.9.a_ref) | copy-start | bytes 9437188
  34.5 1.0 copy-start.8
  35.5 1.9 %copy-start.7 = (bf16[12288,128]{1,0:T(8,128)(2,1)S(1)}, bf16[12288,128]{1,0:T(8,128)(2,1)}, u32[]{:S(2)}) copy-start(bf16[12288,128]{1,0:T(8,128)(2,1)} %copy-done.6) | copy-start | bytes 9437188
  37.4 1.2 copy-start.9
  75.3 28.1 %copy-start.4 = (s32[1,64,16]{1,2,0:T(8,128)S(1)}, s32[1,64,16]{1,2,0:T(8,128)}, u32[]{:S(2)}) copy-start(s32[1,64,16]{1,2,0:T(8,128)} %param.11) | copy-start | bytes 12292
  103.4 11.9 %copy-start.2 = (f32[64,3,128]{2,0,1:T(8,128)S(1)}, f32[64,3,128]{2,0,1:T(8,128)}, u32[]{:S(2)}) copy-start(f32[64,3,128]{2,0,1:T(8,128)} %param.7) | copy-start | bytes 294916
  104.9 18.1 %copy-start = (s32[64,3,256]{2,0,1:T(8,128)S(1)}, s32[64,3,256]{2,0,1:T(8,128)}, u32[]{:S(2)}) copy-start(s32[64,3,256]{2,0,1:T(8,128)} %param.13) | copy-start | bytes 589828
  104.9 18.1 %copy-start.5 = (s32[64,8]{0,1:T(8,128)S(1)}, s32[64,8]{0,1:T(8,128)}, u32[]{:S(2)}) copy-start(s32[64,8]{0,1:T(8,128)} %param.12) | copy-start | bytes 6148
  105.0 5.7 %collective-permute-start.5 = (f32[192,128]{1,0:T(8,128)S(1)}, f32[192,128]{1,0:T(8,128)S(1)}, u32[]{:S(2)}, u32[]{:S(2)}) collective-permute-start(f32[192,128]{1,0:T(8,128)S(1)} %sums.1.own_ref), channel_id=1, source_target_pairs={{0,3},{1,0},{2,1},{3,2},{4,7},{5,4},{6,5},{7,6},{8,11},{9,8},{10,9... | collective-permute-start | bytes 294920 | tf_op jit(solution)/shard_map/ppermute | solution.py:315
  106.7 7.2 %collective-permute-start.4 = (f32[192,128]{1,0:T(8,128)S(1)}, f32[192,128]{1,0:T(8,128)S(1)}, u32[]{:S(2)}, u32[]{:S(2)}) collective-permute-start(f32[192,128]{1,0:T(8,128)S(1)} %sums.1.own_ref), channel_id=1, source_target_pairs={{0,2},{1,3},{2,0},{3,1},{4,6},{5,7},{6,4},{7,5},{8,10},{9,11},{10,... | collective-permute-start | bytes 294920 | tf_op jit(solution)/shard_map/ppermute | solution.py:315
  106.7 8.6 %collective-permute-start.3 = (f32[192,128]{1,0:T(8,128)S(1)}, f32[192,128]{1,0:T(8,128)S(1)}, u32[]{:S(2)}, u32[]{:S(2)}) collective-permute-start(f32[192,128]{1,0:T(8,128)S(1)} %sums.1.own_ref), channel_id=1, source_target_pairs={{0,1},{1,2},{2,3},{3,0},{4,5},{5,6},{6,7},{7,4},{8,9},{9,10},{10,1... | collective-permute-start | bytes 294920 | tf_op jit(solution)/shard_map/ppermute | solution.py:315
  115.4 13.5 %collective-permute-start.6 = (f32[32,128]{1,0:T(8,128)S(1)}, f32[32,128]{1,0:T(8,128)S(1)}, u32[]{:S(2)}, u32[]{:S(2)}) collective-permute-start(f32[32,128]{1,0:T(8,128)S(1)} %get-tuple-element.13), channel_id=1, source_target_pairs={{0,4},{4,8},{8,12},{12,16},{16,20},{20,24},{24,28},{28,32},{32,36}... | collective-permute-start | bytes 49160 | tf_op jit(solution)/shard_map/ppermute | solution.py:372
  117.3 11.5 %collective-permute-start.7 = (f32[32,128]{1,0:T(8,128)S(1)}, f32[32,128]{1,0:T(8,128)S(1)}, u32[]{:S(2)}, u32[]{:S(2)}) collective-permute-start(f32[32,128]{1,0:T(8,128)S(1)} %get-tuple-element.14), channel_id=1, source_target_pairs={{4,0},{8,4},{12,8},{16,12},{20,16},{24,20},{28,24},{32,28},{36,32}... | collective-permute-start | bytes 49160 | tf_op jit(solution)/shard_map/ppermute | solution.py:373

commit v6 on v5

--- a/solution.py
+++ b/solution.py
@@ -22,10 +22,12 @@
 TINY = 1e-30
 VMEM = pl.BlockSpec(memory_space=pltpu.VMEM)
 SMEM = pl.BlockSpec(memory_space=pltpu.SMEM)
+FAR = pl.BlockSpec(memory_space=pltpu.HBM)
+SPACES = {"v": VMEM, "s": SMEM, "f": FAR}
 
 
 def call(kernel, name, outs, ins, scratch=(), mib=8, us=2):
-    specs = [SMEM if space == "s" else VMEM for space, _ in ins]
+    specs = [SPACES[space] for space, _ in ins]
     return pl.pallas_call(
         kernel,
         name=name,
@@ -110,8 +112,12 @@
 
 
 def terms_kernel(
-    x_ref, a_ref, cf_ref, o_ref, v_ref, b_ref, q_ref, w_ref, r_ref, stage_ref, ids_ref, sem
+    x_ref, far_ref, farc_ref, o_ref, a_ref, cf_ref, v_ref, b_ref, q_ref, w_ref, r_ref, stage_ref, ids_ref, sem, a_sem, c_sem
 ):
+    a_copy = pltpu.make_async_copy(far_ref, a_ref, a_sem)
+    c_copy = pltpu.make_async_copy(farc_ref, cf_ref, c_sem)
+    a_copy.start()
+    c_copy.start()
     stage_ref[...] = x_ref[pl.ds(ASK - 1, DEVICES, stride=ASK), :].T[0:SLOTS].astype(I)
     copy = pltpu.make_async_copy(stage_ref, ids_ref, sem)
     copy.start()
@@ -169,6 +175,8 @@
     slots = range(SLOTS)
     stage0(0, 0)
     stage0(1, 1)
+    a_copy.wait()
+    c_copy.wait()
     for j in slots:
         stage1(0, 0, j)
     stage0(2, 0)
@@ -233,9 +241,9 @@
             cor_ref[k, pl.ds(h * count + at, 8, stride=2 * count), :] = got
 
 
-def volumes(cor_ref, h, count):
+def volumes(refs, h, count):
     def corner(k):
-        part = [cor_ref[k, pl.ds((c * 2 + h) * count, count), :] for c in range(6)]
+        part = [ref[k, pl.ds((c * 2 + h) * count, count), :] for ref in refs for c in range(6 // len(refs))]
         return [part[c] + 0.5 * part[c + 3] for c in range(3)], part[3:6]
 
     (ma, da), (mb, db), (mc, dc) = corner(0), corner(1), corner(2)
@@ -258,24 +266,49 @@
             ]
 
 
-def inner_kernel(where_ref, near_ref, node_ref, d_ref, face_ref, v_ref, s_ref, tab_ref, cor_ref, code_ref):
-    for c in range(6):
-        own = node_ref[c] if c < 3 else d_ref[(c - 3) * BOX_DEV : (c - 2) * BOX_DEV, :]
-        tab_ref[pl.ds(c, BOX_DEV, stride=8), :] = own
-    for c in (6, 7):
-        tab_ref[pl.ds(c, BOX_DEV, stride=8), :] = jnp.zeros((BOX_DEV, 128), F)
+def gather_three(near_ref, face_ref, rows, origin, put, tab_ref, code_ref):
+    zero = jnp.zeros((BOX_DEV, 128), F)
+    for half in range(2):
+        for c in range(4):
+            tab_ref[pl.ds(half * 4 + c, BOX_DEV, stride=8), :] = rows[c] if c < 3 else zero
     split_codes(face_ref, code_ref)
-    origin = where_ref[0] * BOX_DEV
+    upper = lax.broadcasted_iota(I, (8, 128), 0) >= 4
 
     def some(g, carry):
         for u in range(8):
             box = g * 8 + HALO + u
-            corners(near_ref, tab_ref, code_ref, cor_ref, box, box, origin, BOX_DEV)
+            tables = []
+            for j in range(8):
+                row = near_ref[j, box] - origin
+                tables.append(tab_ref[pl.ds(pl.multiple_of(row * 8, 8), 8), :])
+            tables = [jnp.where(upper, tables[j + 4], tables[j]) for j in range(4)]
+            for h in range(2):
+                for k in range(3):
+                    code = code_ref[pl.ds((k * 2 + h) * BOX_DEV + box, 1), :]
+                    code = jnp.broadcast_to(code, (8, 128))
+                    lane = code & 127
+                    which = (code >> 7) & 3
+                    got = None
+                    for j in range(4):
+                        value = jnp.take_along_axis(tables[j], lane, axis=1)
+                        got = value if got is None else jnp.where(which == j, value, got)
+                    got = jnp.where(code >= 512, pltpu.roll(got, 4, 0), got)
+                    put[k, pl.ds(h * BOX_DEV + box, 3, stride=2 * BOX_DEV), :] = got[0:3]
         return carry
 
     lax.fori_loop(0, (BOX_DEV - 2 * HALO) // 8, some, 0)
+
+
+def place_kernel(where_ref, near_ref, node_ref, face_ref, o_ref, tab_ref, code_ref):
+    rows = [node_ref[c] for c in range(3)]
+    gather_three(near_ref, face_ref, rows, where_ref[0] * BOX_DEV, o_ref, tab_ref, code_ref)
+
+
+def inner_kernel(where_ref, near_ref, d_ref, place_ref, face_ref, v_ref, s_ref, tab_ref, cor_ref, code_ref):
+    rows = [d_ref[c * BOX_DEV : (c + 1) * BOX_DEV, :] for c in range(3)]
+    gather_three(near_ref, face_ref, rows, where_ref[0] * BOX_DEV, cor_ref, tab_ref, code_ref)
     for h in range(2):
-        s_ref[:, h * 128 : (h + 1) * 128] = volumes(cor_ref, h, BOX_DEV)
+        s_ref[:, h * 128 : (h + 1) * 128] = volumes((place_ref, cor_ref), h, BOX_DEV)
     for c in range(3):
         v_ref[c] = d_ref[c * BOX_DEV : (c + 1) * BOX_DEV, :] * 2.0
 
@@ -298,7 +331,7 @@
         corners(near_ref, tab_ref, code_ref, cor_ref, box, at, origin, 2 * HALO)
     s_ref[...] = in_ref[...]
     for h in range(2):
-        swept = volumes(cor_ref, h, 2 * HALO)
+        swept = volumes((cor_ref,), h, 2 * HALO)
         s_ref[0:HALO, h * 128 : (h + 1) * 128] = swept[0:HALO]
         s_ref[BOX_DEV - HALO : BOX_DEV, h * 128 : (h + 1) * 128] = swept[HALO:]
 
@@ -332,6 +365,16 @@
         (shape(DEVICES * ASK, 128),),
         [("v", listed), ("v", nodes)],
     )
+    near, codes = neighbours.T, faces.transpose(1, 0, 2)
+    sent, early = lax.optimization_barrier((sent, codes))
+    (place,) = call(
+        place_kernel,
+        "place",
+        (shape(3, 6 * BOX_DEV, 128),),
+        [("s", where), ("s", near), ("v", nodes), ("v", early)],
+        [pltpu.VMEM((8 * BOX_DEV, 128), F), pltpu.VMEM((6 * BOX_DEV, 128), I)],
+        us=4,
+    )
     tables = call(
         feat_kernel,
         "feats",
@@ -343,8 +386,10 @@
         terms_kernel,
         "terms",
         (shape(DEVICES * GIVE, 128),),
-        [("v", to_all(sent)), ("v", tables[0]), ("v", tables[1])],
+        [("v", to_all(sent))] + [("f", pltpu.with_memory_space_constraint(t, pltpu.HBM)) for t in tables],
         [
+            pltpu.VMEM((4 * BOX_DEV * 48, 128), BF),
+            pltpu.VMEM((4 * BOX_DEV * 16, 128), BF),
             pltpu.VMEM((2, 3, 64, 128), F),
             pltpu.VMEM((2, SLOTS, 48, 128), BF),
             pltpu.VMEM((2, SLOTS, 128, 128), F),
@@ -353,6 +398,8 @@
             pltpu.VMEM((SLOTS, 128), I),
             pltpu.SMEM((SLOTS, 128), I),
             pltpu.SemaphoreType.DMA,
+            pltpu.SemaphoreType.DMA,
+            pltpu.SemaphoreType.DMA,
         ],
         mib=16,
         us=45,
@@ -371,18 +418,17 @@
     )
     low = lax.ppermute(up, "vol", [(i, i + 1) for i in range(31)])
     high = lax.ppermute(down, "vol", [(i + 1, i) for i in range(31)])
-    near, codes = neighbours.T, faces.transpose(1, 0, 2)
     velocity, inner = call(
         inner_kernel,
         "inner",
         (shape(3, BOX_DEV, 128), shape(BOX_DEV, 256)),
-        [("s", where), ("s", near), ("v", nodes), ("v", d), ("v", codes)],
+        [("s", where), ("s", near), ("v", d), ("v", place), ("v", codes)],
         [
             pltpu.VMEM((8 * BOX_DEV, 128), F),
-            pltpu.VMEM((3, 16 * BOX_DEV, 128), F),
+            pltpu.VMEM((3, 6 * BOX_DEV, 128), F),
             pltpu.VMEM((6 * BOX_DEV, 128), I),
         ],
-        us=6,
+        us=4,
     )
     (swept,) = call(
         edge_kernel,

time: 131 us -> 127 us (0.969)
  waiting for transfers between devices: 19.5 us -> 11.1 us
  starting transfers between devices: 23.7 us -> 27.6 us
  Pallas kernels: 51.3 us -> 55 us
  local copies, waits for them, and re-layouts: 7.36 us -> 4.24 us
    ppermute x6, waiting for transfers between devices: 19.5 us -> 10.3 us  [around(): lax.ppermute(array, 'surf', [(i, (i + k) % 4) for i in range(4)])]
    ppermute x6, starting transfers between devices: 8.39 us -> 12.3 us  [around(): lax.ppermute(array, 'surf', [(i, (i + k) % 4) for i in range(4)])]
    pallas_call x7 -> x8, Pallas kernels: 51.3 us -> 55 us  [call(): pl.pallas_call(kernel, name=name, out_shape=outs, in_specs=specs, out_spe...]
    unnamed x26 -> x22, local copies, waits for them, and re-layouts: 7.36 us -> 4.24 us
  transfers between devices with their start and end apart: 9 -> 9, of which waited for: 5 -> 4; matrix products, arithmetic and copies ran while one was open for 0% -> 0% of each run, Pallas kernels for 6% -> 8%
where the time goes in v6:
time: 127 us; the launch traced here: 126 us
  Pallas kernels  55 us (43%)
  starting transfers between devices  27.6 us (22%)
  blocking collectives  27.3 us (21%)
  waiting for transfers between devices  11.1 us (9%)
  local copies, waits for them, and re-layouts  4.24 us (3%)
    pallas_call x8, Pallas kernels, call(): pl.pallas_call(kernel, name=name, out_shape=outs, in_specs=specs, out_spe...  55 us
    all_to_all x1, blocking collectives, to_all(): lax.all_to_all(packets, 'vol', split_axis=0, concat_axis=0, tiled=True)  27.3 us
    ppermute x6, starting transfers between devices, around(): lax.ppermute(array, 'surf', [(i, (i + k) % 4) for i in range(4)])  12.3 us
    ppermute x6, waiting for transfers between devices, around(): lax.ppermute(array, 'surf', [(i, (i + k) % 4) for i in range(4)])  10.3 us
    all_to_all x1, starting transfers between devices, to_all(): lax.all_to_all(packets, 'vol', split_axis=0, concat_axis=0, tiled=True)  7.67 us
    ppermute x1, starting transfers between devices, body(): high = lax.ppermute(down, 'vol', [(i + 1, i) for i in range(31)])  5.73 us
    unnamed x22, local copies, waits for them, and re-layouts  4.24 us
  transfers between devices with their start and end apart: 9, of which 4 were waited for; matrix products, arithmetic and copies ran while one was open for 0% of the time, Pallas kernels for 8%

profile of v6, /device:TPU:8, one launch (start us, length us, event | category | flops | bytes accessed | tf_op | source)
XLA Modules:
  0.0 126.2 jit_solution(456823434184135771)
XLA Ops:
  0.6 0.0 copy-start.1
  0.6 0.9 copy-done.1
  1.5 0.0 copy-start.3
  1.5 0.7 copy-done.3
  2.2 2.7 %prep.1 = f32[3200,128]{1,0:T(8,128)} custom-call(s32[16,64]{1,0:T(8,128)S(1)} %bitcast.31, f32[3,64,128]{2,1,0:T(8,128)S(1)} %bitcast.27), custom_call_target="tpu_custom_call" | custom-call | flops 2000000000 | bytes 2000000 | tf_op jit(solution)/shard_map/prep/pallas_call | solution.py:31
  4.9 0.0 copy-start.8
  4.9 0.0 copy-start.9
  4.9 0.0 copy-start.10
  5.0 7.7 %all-to-all-start = ((f32[32,100,1,128]{3,2,1,0:T(1,128)}), f32[32,100,1,128]{3,2,1,0:T(1,128)S(1)}, u32[]{:S(2)}, u32[]{:S(2)}) async-start(f32[32,100,1,128]{3,2,1,0:T(1,128)} %bitcast.8), calls=%async_computation | async-start | bytes 3276800 | tf_op jit(solution)/shard_map/all_to_all | solution.py:343
  12.6 0.0 copy-done.8
  12.6 0.0 copy-done.9
  12.6 0.0 copy-done.10
  12.7 2.0 %collective-permute-start = (f32[448,128]{1,0:T(8,128)S(1)}, f32[448,128]{1,0:T(8,128)S(1)}, u32[]{:S(2)}, u32[]{:S(2)}) collective-permute-start(f32[448,128]{1,0:T(8,128)S(1)} %pad_maximum_fusion.own_ref), channel_id=1, source_target_pairs={{0,1},{1,2},{2,3},{3,0},{4,5},{5,6},{6,7},{7,4},{8,9},{9,10},{10,1... | collective-permute-start | bytes 688136 | tf_op jit(solution)/shard_map/ppermute | solution.py:348
  14.7 3.6 %collective-permute-start.1 = (f32[448,128]{1,0:T(8,128)S(1)}, f32[448,128]{1,0:T(8,128)S(1)}, u32[]{:S(2)}, u32[]{:S(2)}) collective-permute-start(f32[448,128]{1,0:T(8,128)S(1)} %pad_maximum_fusion.own_ref), channel_id=1, source_target_pairs={{0,2},{1,3},{2,0},{3,1},{4,6},{5,7},{6,4},{7,5},{8,10},{9,11},{10,... | collective-permute-start | bytes 688136 | tf_op jit(solution)/shard_map/ppermute | solution.py:348
  18.3 1.0 collective-permute-start.2
  19.3 0.1 pad_add_fusion.where_ref
  19.3 3.3 %collective-permute-done.one_ref = f32[448,128]{1,0:T(8,128)S(1)} collective-permute-done((f32[448,128]{1,0:T(8,128)S(1)}, f32[448,128]{1,0:T(8,128)S(1)}, u32[]{:S(2)}, u32[]{:S(2)}) %collective-permute-start) | collective-permute-done | bytes 229408 | tf_op jit(solution)/shard_map/ppermute | solution.py:348
  22.7 6.1 %collective-permute-done.1.two_ref = f32[448,128]{1,0:T(8,128)S(1)} collective-permute-done((f32[448,128]{1,0:T(8,128)S(1)}, f32[448,128]{1,0:T(8,128)S(1)}, u32[]{:S(2)}, u32[]{:S(2)}) %collective-permute-start.1) | collective-permute-done | bytes 229408 | tf_op jit(solution)/shard_map/ppermute | solution.py:348
  28.8 0.0 collective-permute-done.2.three_ref
  28.8 2.6 %feats.1 = (bf16[12288,128]{1,0:T(8,128)(2,1)S(1)}, bf16[4096,128]{1,0:T(8,128)(2,1)S(1)}) custom-call(s32[2]{0:T(128)S(1)} %pad_add_fusion.where_ref, f32[448,128]{1,0:T(8,128)S(1)} %pad_maximum_fusion.own_ref, f32[448,128]{1,0:T(8,128)S(1)} %collective-permute-done.one_ref, f32[448,128]{1,0:T(8,128)S(1)} %collective-permute-done.1.two_ref, ...), custom_call_target="tpu_custom_call" | custom-call | flops 5000000000 | bytes 5000000 | tf_op jit(solution)/shard_map/feats/pallas_call | solution.py:31
  31.3 0.0 copy-start.6
  31.3 1.6 %copy-done.6 = bf16[12288,128]{1,0:T(8,128)(2,1)} copy-done((bf16[12288,128]{1,0:T(8,128)(2,1)}, bf16[12288,128]{1,0:T(8,128)(2,1)S(1)}, u32[]{:S(2)}) %copy-start.6) | copy-done | bytes 3145752
  33.0 0.0 copy-start.7
  33.0 1.0 copy-done.7
  34.0 0.8 all-to-all-done
  34.7 38.1 %terms.1 = f32[3072,128]{1,0:T(8,128)S(1)} custom-call(f32[3200,128]{1,0:T(8,128)S(1)} %bitcast.21, bf16[12288,128]{1,0:T(8,128)(2,1)} %copy-done.6, bf16[4096,128]{1,0:T(8,128)(2,1)} %copy-done.7), custom_call_target="tpu_custom_call" | custom-call | flops 44999999488 | bytes 45000000 | tf_op jit(solution)/shard_map/terms/pallas_call | solution.py:31
  72.9 0.0 copy-start.4
  72.9 27.3 %all_to_all.10 = f32[32,96,1,128]{3,1,2,0:T(8,128)S(1)} all-to-all(f32[32,96,1,128]{3,1,2,0:T(8,128)S(1)} %bitcast.22), channel_id=1, replica_groups=mesh['vol'=32,'surf'=4] {'vol'}, dimensions={0} | all-to-all | bytes 3145728 | tf_op jit(solution)/shard_map/all_to_all | solution.py:343
  100.2 0.0 copy-done.4
  100.2 0.0 copy-start
  100.2 0.0 copy-start.2
  100.2 1.5 %sums.1.own_ref = f32[192,128]{1,0:T(8,128)S(1)} custom-call(s32[16,64]{1,0:T(8,128)S(1)} %bitcast.32, f32[3072,128]{1,0:T(8,128)S(1)} %bitcast.23), custom_call_target="tpu_custom_call" | custom-call | flops 2000000000 | bytes 2000000 | tf_op jit(solution)/shard_map/sums/pallas_call | solution.py:31
  101.7 1.2 collective-permute-start.3
  102.9 3.4 %collective-permute-start.4 = (f32[192,128]{1,0:T(8,128)S(1)}, f32[192,128]{1,0:T(8,128)S(1)}, u32[]{:S(2)}, u32[]{:S(2)}) collective-permute-start(f32[192,128]{1,0:T(8,128)S(1)} %sums.1.own_ref), channel_id=1, source_target_pairs={{0,2},{1,3},{2,0},{3,1},{4,6},{5,7},{6,4},{7,5},{8,10},{9,11},{10,... | collective-permute-start | bytes 294920 | tf_op jit(solution)/shard_map/ppermute | solution.py:348
  106.4 1.0 collective-permute-start.5
  107.4 0.0 copy-done
  107.4 0.0 copy-done.2
  107.4 0.0 copy-done.5
  107.4 3.8 %place.1.place_ref = f32[3,384,128]{2,1,0:T(8,128)S(1)} custom-call(s32[2]{0:T(128)S(1)} %pad_add_fusion.where_ref, s32[8,64]{1,0:T(8,128)S(1)} %bitcast.33, f32[3,64,128]{2,1,0:T(8,128)S(1)} %bitcast.28, s32[3,64,256]{2,1,0:T(8,128)S(1)} %bitcast.24), custom_call_target="tpu_custom_call" | custom-call | flops 4000000000 | bytes 4000000 | tf_op jit(solution)/shard_map/place/pallas_call | solution.py:31
  111.2 0.0 collective-permute-done.3.one_ref
  111.2 0.9 collective-permute-done.4.two_ref
  112.0 0.0 collective-permute-done.5.three_ref
  112.1 1.9 %collective-permute-start.6 = (f32[32,128]{1,0:T(8,128)S(1)}, f32[32,128]{1,0:T(8,128)S(1)}, u32[]{:S(2)}, u32[]{:S(2)}) collective-permute-start(f32[32,128]{1,0:T(8,128)S(1)} %get-tuple-element.17), channel_id=1, source_target_pairs={{0,4},{4,8},{8,12},{12,16},{16,20},{20,24},{24,28},{28,32},{32,36}... | collective-permute-start | bytes 49160 | tf_op jit(solution)/shard_map/ppermute | solution.py:419
  114.0 5.7 %collective-permute-start.7 = (f32[32,128]{1,0:T(8,128)S(1)}, f32[32,128]{1,0:T(8,128)S(1)}, u32[]{:S(2)}, u32[]{:S(2)}) collective-permute-start(f32[32,128]{1,0:T(8,128)S(1)} %get-tuple-element.18), channel_id=1, source_target_pairs={{4,0},{8,4},{12,8},{16,12},{20,16},{24,20},{28,24},{32,28},{36,32}... | collective-permute-start | bytes 49160 | tf_op jit(solution)/shard_map/ppermute | solution.py:420
  119.8 4.4 %inner.1 = (f32[3,64,128]{2,1,0:T(8,128)}, f32[64,256]{1,0:T(8,128)S(1)}) custom-call(s32[2]{0:T(128)S(1)} %pad_add_fusion.where_ref, s32[8,64]{1,0:T(8,128)S(1)} %bitcast.34, f32[192,128]{1,0:T(8,128)S(1)} %get-tuple-element.14.d_ref, f32[3,384,128]{2,1,0:T(8,128)S(1)} %place.1.place_ref, s32[3,64,256]{2,1,0:T(8,128)S(1)} %bitcast.25), custom_call_target="tpu_custom_call" | custom-call | flops 4000000000 | bytes 4000000 | tf_op jit(solution)/shard_map/inner/pallas_call | solution.py:31
  124.2 0.0 collective-permute-done.6.low_ref
  124.2 0.0 collective-permute-done.7.high_ref
  124.2 2.0 %edges.1 = f32[64,256]{1,0:T(8,128)} custom-call(s32[2]{0:T(128)S(1)} %pad_add_fusion.where_ref, s32[8,64]{1,0:T(8,128)S(1)} %bitcast.35, f32[3,64,128]{2,1,0:T(8,128)S(1)} %bitcast.30, f32[192,128]{1,0:T(8,128)S(1)} %get-tuple-element.14.d_ref, f32[32,128]{1,0:T(8,128)S(1)} %collective-permute-done.6.low_ref, ...), custom_call_target="tpu_custom_call" | custom-call | flops 2000000000 | bytes 2000000 | tf_op jit(solution)/shard_map/edges/pallas_call | solution.py:31
  (3 shorter events, 0.0 us)
Async XLA Ops:
  0.6 0.9 copy-start.1
  1.5 0.7 copy-start.3
  4.9 7.7 %copy-start.8 = (f32[64,3,128]{2,0,1:T(8,128)S(1)}, f32[64,3,128]{2,0,1:T(8,128)}, u32[]{:S(2)}) copy-start(f32[64,3,128]{2,0,1:T(8,128)} %param.9) | copy-start | bytes 294916
  4.9 7.7 %copy-start.9 = (f32[64,3,128]{2,0,1:T(8,128)S(1)}, f32[64,3,128]{2,0,1:T(8,128)}, u32[]{:S(2)}) copy-start(f32[64,3,128]{2,0,1:T(8,128)} %param.8) | copy-start | bytes 294916
  4.9 7.7 %copy-start.10 = (f32[64,128]{1,0:T(8,128)S(1)}, f32[64,128]{1,0:T(8,128)}, u32[]{:S(2)}) copy-start(f32[64,128]{1,0:T(8,128)} %param.10) | copy-start | bytes 98308
  5.0 29.8 %all-to-all-start = ((f32[32,100,1,128]{3,2,1,0:T(1,128)}), f32[32,100,1,128]{3,2,1,0:T(1,128)S(1)}, u32[]{:S(2)}, u32[]{:S(2)}) async-start(f32[32,100,1,128]{3,2,1,0:T(1,128)} %bitcast.8), calls=%async_computation | async-start | bytes 3276800 | tf_op jit(solution)/shard_map/all_to_all | solution.py:343
  12.7 10.0 %collective-permute-start = (f32[448,128]{1,0:T(8,128)S(1)}, f32[448,128]{1,0:T(8,128)S(1)}, u32[]{:S(2)}, u32[]{:S(2)}) collective-permute-start(f32[448,128]{1,0:T(8,128)S(1)} %pad_maximum_fusion.own_ref), channel_id=1, source_target_pairs={{0,1},{1,2},{2,3},{3,0},{4,5},{5,6},{6,7},{7,4},{8,9},{9,10},{10,1... | collective-permute-start | bytes 688136 | tf_op jit(solution)/shard_map/ppermute | solution.py:348
  14.7 14.1 %collective-permute-start.1 = (f32[448,128]{1,0:T(8,128)S(1)}, f32[448,128]{1,0:T(8,128)S(1)}, u32[]{:S(2)}, u32[]{:S(2)}) collective-permute-start(f32[448,128]{1,0:T(8,128)S(1)} %pad_maximum_fusion.own_ref), channel_id=1, source_target_pairs={{0,2},{1,3},{2,0},{3,1},{4,6},{5,7},{6,4},{7,5},{8,10},{9,11},{10,... | collective-permute-start | bytes 688136 | tf_op jit(solution)/shard_map/ppermute | solution.py:348
  18.3 10.5 %collective-permute-start.2 = (f32[448,128]{1,0:T(8,128)S(1)}, f32[448,128]{1,0:T(8,128)S(1)}, u32[]{:S(2)}, u32[]{:S(2)}) collective-permute-start(f32[448,128]{1,0:T(8,128)S(1)} %pad_maximum_fusion.own_ref), channel_id=1, source_target_pairs={{0,3},{1,0},{2,1},{3,2},{4,7},{5,4},{6,5},{7,6},{8,11},{9,8},{10,9... | collective-permute-start | bytes 688136 | tf_op jit(solution)/shard_map/ppermute | solution.py:348
  31.3 1.6 %copy-start.6 = (bf16[12288,128]{1,0:T(8,128)(2,1)}, bf16[12288,128]{1,0:T(8,128)(2,1)S(1)}, u32[]{:S(2)}) copy-start(bf16[12288,128]{1,0:T(8,128)(2,1)S(1)} %get-tuple-element.12.far_ref) | copy-start | bytes 9437188
  33.0 1.0 copy-start.7
  72.9 27.3 %copy-start.4 = (s32[1,64,16]{1,2,0:T(8,128)S(1)}, s32[1,64,16]{1,2,0:T(8,128)}, u32[]{:S(2)}) copy-start(s32[1,64,16]{1,2,0:T(8,128)} %param.11) | copy-start | bytes 12292
  100.2 7.2 %copy-start = (s32[64,3,256]{2,0,1:T(8,128)S(1)}, s32[64,3,256]{2,0,1:T(8,128)}, u32[]{:S(2)}) copy-start(s32[64,3,256]{2,0,1:T(8,128)} %param.13) | copy-start | bytes 589828
  100.2 7.2 %copy-start.2 = (f32[64,3,128]{2,0,1:T(8,128)S(1)}, f32[64,3,128]{2,0,1:T(8,128)}, u32[]{:S(2)}) copy-start(f32[64,3,128]{2,0,1:T(8,128)} %param.7) | copy-start | bytes 294916
  100.2 7.2 %copy-start.5 = (s32[64,8]{0,1:T(8,128)S(1)}, s32[64,8]{0,1:T(8,128)}, u32[]{:S(2)}) copy-start(s32[64,8]{0,1:T(8,128)} %param.12) | copy-start | bytes 6148
  101.7 9.5 %collective-permute-start.3 = (f32[192,128]{1,0:T(8,128)S(1)}, f32[192,128]{1,0:T(8,128)S(1)}, u32[]{:S(2)}, u32[]{:S(2)}) collective-permute-start(f32[192,128]{1,0:T(8,128)S(1)} %sums.1.own_ref), channel_id=1, source_target_pairs={{0,1},{1,2},{2,3},{3,0},{4,5},{5,6},{6,7},{7,4},{8,9},{9,10},{10,1... | collective-permute-start | bytes 294920 | tf_op jit(solution)/shard_map/ppermute | solution.py:348
  102.9 9.1 %collective-permute-start.4 = (f32[192,128]{1,0:T(8,128)S(1)}, f32[192,128]{1,0:T(8,128)S(1)}, u32[]{:S(2)}, u32[]{:S(2)}) collective-permute-start(f32[192,128]{1,0:T(8,128)S(1)} %sums.1.own_ref), channel_id=1, source_target_pairs={{0,2},{1,3},{2,0},{3,1},{4,6},{5,7},{6,4},{7,5},{8,10},{9,11},{10,... | collective-permute-start | bytes 294920 | tf_op jit(solution)/shard_map/ppermute | solution.py:348
  106.4 5.7 %collective-permute-start.5 = (f32[192,128]{1,0:T(8,128)S(1)}, f32[192,128]{1,0:T(8,128)S(1)}, u32[]{:S(2)}, u32[]{:S(2)}) collective-permute-start(f32[192,128]{1,0:T(8,128)S(1)} %sums.1.own_ref), channel_id=1, source_target_pairs={{0,3},{1,0},{2,1},{3,2},{4,7},{5,4},{6,5},{7,6},{8,11},{9,8},{10,9... | collective-permute-start | bytes 294920 | tf_op jit(solution)/shard_map/ppermute | solution.py:348
  112.1 12.1 %collective-permute-start.6 = (f32[32,128]{1,0:T(8,128)S(1)}, f32[32,128]{1,0:T(8,128)S(1)}, u32[]{:S(2)}, u32[]{:S(2)}) collective-permute-start(f32[32,128]{1,0:T(8,128)S(1)} %get-tuple-element.17), channel_id=1, source_target_pairs={{0,4},{4,8},{8,12},{12,16},{16,20},{20,24},{24,28},{28,32},{32,36}... | collective-permute-start | bytes 49160 | tf_op jit(solution)/shard_map/ppermute | solution.py:419
  114.0 10.1 %collective-permute-start.7 = (f32[32,128]{1,0:T(8,128)S(1)}, f32[32,128]{1,0:T(8,128)S(1)}, u32[]{:S(2)}, u32[]{:S(2)}) collective-permute-start(f32[32,128]{1,0:T(8,128)S(1)} %get-tuple-element.18), channel_id=1, source_target_pairs={{4,0},{8,4},{12,8},{16,12},{20,16},{24,20},{28,24},{32,28},{36,32}... | collective-permute-start | bytes 49160 | tf_op jit(solution)/shard_map/ppermute | solution.py:420

commit v7 on v6

--- a/solution.py
+++ b/solution.py
@@ -15,6 +15,7 @@
 SLOTS = 8
 ASK = 3 * SLOTS + 1
 GIVE = 3 * SLOTS
+FEATS = 32
 UNROLL = 8
 BOX_DEV = 64
 HALO = 4
@@ -26,14 +27,14 @@
 SPACES = {"v": VMEM, "s": SMEM, "f": FAR}
 
 
-def call(kernel, name, outs, ins, scratch=(), mib=8, us=2):
+def call(kernel, name, outs, ins, scratch=(), mib=8, us=2, out=VMEM):
     specs = [SPACES[space] for space, _ in ins]
     return pl.pallas_call(
         kernel,
         name=name,
         out_shape=outs,
         in_specs=specs,
-        out_specs=tuple(VMEM for _ in outs),
+        out_specs=tuple(out for _ in outs),
         scratch_shapes=list(scratch),
         compiler_params=pltpu.CompilerParams(vmem_limit_bytes=mib << 20),
         cost_estimate=pl.CostEstimate(flops=us * 10**9, bytes_accessed=us * 10**6, transcendentals=0),
@@ -82,9 +83,10 @@
     o_ref[pl.ds(ASK - 1, DEVICES, stride=ASK), :] = stacked
 
 
-def feat_kernel(where_ref, own_ref, one_ref, two_ref, three_ref, a_ref, cf_ref):
+def feat_kernel(own_ref, one_ref, two_ref, three_ref, far_ref, farc_ref, a_ref, cf_ref, sems):
+    copies = []
     for k, ref in enumerate((own_ref, one_ref, two_ref, three_ref)):
-        first = ((where_ref[1] + 4 - k) & 3) * BOX_DEV
+        first = k * BOX_DEV
 
         def some(h, carry):
             base = pl.multiple_of(h * 8, 8)
@@ -95,13 +97,10 @@
             rows = [split3(t) for t in rows]
             ks = [split3(4.0 * t) for t in (kx, ky, kz)]
             for u in range(8):
-                def part(n):
-                    return [t[n][u : u + 1] for t in rows] + [jnp.zeros((3, 128), F)]
-
-                p, q, t = part(0), part(1), part(2)
-                s = jnp.concatenate(p * 3 + q * 2 + t, 0).astype(BF)
+                s = [t[n][u : u + 1] for t in rows[0:4] for n in (0, 0, 0, 1, 1, 2)]
+                s += [rows[4][n][u : u + 1] for n in range(3)] + [jnp.zeros((5, 128), F)]
                 at = first + base + u
-                a_ref[pl.ds(pl.multiple_of(at * 48, 16), 48), :] = s
+                a_ref[pl.ds(pl.multiple_of(at * FEATS, FEATS), FEATS), :] = jnp.concatenate(s, 0).astype(BF)
                 c = jnp.concatenate(
                     [t[n][u : u + 1] for n in range(2) for t in ks] + [jnp.zeros((10, 128), F)], 0
                 ).astype(BF)
@@ -109,10 +108,17 @@
             return carry
 
         lax.fori_loop(0, BOX_DEV // 8, some, 0)
+        for n, (near, far, height) in enumerate(((a_ref, far_ref, FEATS), (cf_ref, farc_ref, 16))):
+            part = pl.ds(first * height, BOX_DEV * height)
+            copy = pltpu.make_async_copy(near.at[part, :], far.at[part, :], sems.at[2 * k + n])
+            copy.start()
+            copies.append(copy)
+    for copy in copies:
+        copy.wait()
 
 
 def terms_kernel(
-    x_ref, far_ref, farc_ref, o_ref, a_ref, cf_ref, v_ref, b_ref, q_ref, w_ref, r_ref, stage_ref, ids_ref, sem, a_sem, c_sem
+    where_ref, x_ref, far_ref, farc_ref, o_ref, a_ref, cf_ref, v_ref, b_ref, q_ref, w_ref, r_ref, stage_ref, ids_ref, sem, a_sem, c_sem
 ):
     a_copy = pltpu.make_async_copy(far_ref, a_ref, a_sem)
     c_copy = pltpu.make_async_copy(farc_ref, cf_ref, c_sem)
@@ -122,10 +128,10 @@
     copy = pltpu.make_async_copy(stage_ref, ids_ref, sem)
     copy.start()
     for buf in range(2):
-        for k in range(3):
-            v_ref[buf, k, pl.ds(32, 32), :] = jnp.zeros((32, 128), F)
-        v_ref[buf, 0, pl.ds(32, 8), :] = jnp.ones((8, 128), F)
+        v_ref[buf, pl.ds(192, 24), :] = jnp.ones((24, 128), F)
+        v_ref[buf, pl.ds(216, 40), :] = jnp.zeros((40, 128), F)
     copy.wait()
+    surf = where_ref[1]
 
     def stage0(i, buf):
         i = jnp.minimum(i, DEVICES - 1)
@@ -135,18 +141,17 @@
             first = value.astype(BF).astype(F)
             rest = value - first
             second = rest.astype(BF).astype(F)
-            for k, part in enumerate((first, second, rest - second)):
-                v_ref[buf, k, pl.ds(f * 8, 8), :] = part
+            third = rest - second
+            for k, part in enumerate((first, second, third, first, second, first)):
+                v_ref[buf, pl.ds((f * 6 + k) * 8, 8), :] = part
         for j in range(SLOTS):
-            v = [v_ref[buf, k, pl.ds(j, 8, stride=8), :] for k in range(3)]
-            b_ref[buf, j] = jnp.concatenate(
-                [v[0], v[1], v[2], v[0], v[1], v[0]], 0
-            ).astype(BF)
+            v = [v_ref[buf, pl.ds(n * 64 + j, 8, stride=8), :] for n in range(4)]
+            b_ref[buf, j] = jnp.concatenate(v, 0).astype(BF)
 
     def stage1(i, buf, j):
         i = jnp.minimum(i, DEVICES - 1)
-        g = (i & 3) * BOX_DEV + ids_ref[j, i]
-        a = a_ref[pl.ds(pl.multiple_of(g * 48, 16), 48), :]
+        g = ((surf - i) & 3) * BOX_DEV + ids_ref[j, i]
+        a = a_ref[pl.ds(pl.multiple_of(g * FEATS, FEATS), FEATS), :]
         q_ref[buf, j] = lax.dot_general(
             a, b_ref[buf, j], (((0,), (0,)), ((), ())), preferred_element_type=F
         )
@@ -162,7 +167,7 @@
         w_ref[buf, j, 128:256, :] = (w - high.astype(F)).astype(BF)
 
     def stage3(i, buf, j):
-        g = (i & 3) * BOX_DEV + ids_ref[j, i]
+        g = ((surf - i) & 3) * BOX_DEV + ids_ref[j, i]
         c = cf_ref[pl.ds(pl.multiple_of(g * 16, 16), 16), :]
         c = jnp.concatenate([c, c], 1)
         r = jnp.dot(c, w_ref[buf, j], preferred_element_type=F)
@@ -375,23 +380,26 @@
         [pltpu.VMEM((8 * BOX_DEV, 128), F), pltpu.VMEM((6 * BOX_DEV, 128), I)],
         us=4,
     )
+    sizes = (4 * BOX_DEV * FEATS, 128), (4 * BOX_DEV * 16, 128)
     tables = call(
         feat_kernel,
         "feats",
-        (shape(4 * BOX_DEV * 48, 128, kind=BF), shape(4 * BOX_DEV * 16, 128, kind=BF)),
-        [("s", where), ("v", blocks)] + [("v", r) for r in around(blocks)],
+        tuple(pltpu.HBM(size, BF) for size in sizes),
+        [("v", blocks)] + [("v", r) for r in around(blocks)],
+        [pltpu.VMEM(size, BF) for size in sizes] + [pltpu.SemaphoreType.DMA((8,))],
         us=5,
+        out=FAR,
     )
     (terms,) = call(
         terms_kernel,
         "terms",
         (shape(DEVICES * GIVE, 128),),
-        [("v", to_all(sent))] + [("f", pltpu.with_memory_space_constraint(t, pltpu.HBM)) for t in tables],
+        [("s", where), ("v", to_all(sent))] + [("f", pltpu.with_memory_space_constraint(t, pltpu.HBM)) for t in tables],
         [
-            pltpu.VMEM((4 * BOX_DEV * 48, 128), BF),
+            pltpu.VMEM((4 * BOX_DEV * FEATS, 128), BF),
             pltpu.VMEM((4 * BOX_DEV * 16, 128), BF),
-            pltpu.VMEM((2, 3, 64, 128), F),
-            pltpu.VMEM((2, SLOTS, 48, 128), BF),
+            pltpu.VMEM((2, 8 * FEATS, 128), F),
+            pltpu.VMEM((2, SLOTS, FEATS, 128), BF),
             pltpu.VMEM((2, SLOTS, 128, 128), F),
             pltpu.VMEM((2, SLOTS, 256, 128), BF),
             pltpu.VMEM((2, 2 * GIVE, 128), F),

time: 127 us -> 127 us (level)
  local copies, waits for them, and re-layouts: 4.24 us -> 1.61 us
  waiting for transfers between devices: 11.1 us -> 13 us
  Pallas kernels: 55 us -> 56.3 us
    unnamed x22 -> x18, local copies, waits for them, and re-layouts: 4.24 us -> 1.61 us
    all_to_all x1, waiting for transfers between devices: 0.77 us -> 2.65 us  [to_all(): lax.all_to_all(packets, 'vol', split_axis=0, concat_axis=0, tiled=True)]
  transfers between devices with their start and end apart: 9 -> 9, of which waited for: 4 -> 4; matrix products, arithmetic and copies ran while one was open for 0% -> 0% of each run, Pallas kernels for 8% -> 9%
where the time goes in v7:
time: 127 us
  Pallas kernels  56.3 us (44%)
  starting transfers between devices  28.5 us (22%)
  blocking collectives  26.4 us (21%)
  waiting for transfers between devices  13 us (10%)
  local copies, waits for them, and re-layouts  1.61 us (1%)
    pallas_call x8, Pallas kernels, call(): pl.pallas_call(kernel, name=name, out_shape=outs, in_specs=specs, out_spe...  56.3 us
    all_to_all x1, blocking collectives, to_all(): lax.all_to_all(packets, 'vol', split_axis=0, concat_axis=0, tiled=True)  26.4 us
    ppermute x6, starting transfers between devices, around(): lax.ppermute(array, 'surf', [(i, (i + k) % 4) for i in range(4)])  13.1 us
    ppermute x6, waiting for transfers between devices, around(): lax.ppermute(array, 'surf', [(i, (i + k) % 4) for i in range(4)])  10.3 us
    all_to_all x1, starting transfers between devices, to_all(): lax.all_to_all(packets, 'vol', split_axis=0, concat_axis=0, tiled=True)  7.67 us
    ppermute x1, starting transfers between devices, body(): high = lax.ppermute(down, 'vol', [(i + 1, i) for i in range(31)])  5.73 us
    all_to_all x1, waiting for transfers between devices, to_all(): lax.all_to_all(packets, 'vol', split_axis=0, concat_axis=0, tiled=True)  2.65 us
  transfers between devices with their start and end apart: 9, of which 4 were waited for; matrix products, arithmetic and copies ran while one was open for 0% of the time, Pallas kernels for 9%

profile of v7, /device:TPU:8, one launch (start us, length us, event | category | flops | bytes accessed | tf_op | source)
XLA Modules:
  0.0 126.7 jit_solution(7611997973125975488)
XLA Ops:
  0.6 0.0 copy-start.1
  0.6 0.9 copy-done.1
  1.5 0.0 copy-start.3
  1.5 0.7 copy-done.3
  2.2 2.7 %prep.1 = f32[3200,128]{1,0:T(8,128)} custom-call(s32[16,64]{1,0:T(8,128)S(1)} %bitcast.31, f32[3,64,128]{2,1,0:T(8,128)S(1)} %bitcast.27), custom_call_target="tpu_custom_call" | custom-call | flops 2000000000 | bytes 2000000 | tf_op jit(solution)/shard_map/prep/pallas_call | solution.py:32
  4.9 0.0 copy-start.6
  4.9 0.0 copy-start.7
  4.9 0.0 copy-start.8
  4.9 7.7 %all-to-all-start = ((f32[32,100,1,128]{3,2,1,0:T(1,128)}), f32[32,100,1,128]{3,2,1,0:T(1,128)S(1)}, u32[]{:S(2)}, u32[]{:S(2)}) async-start(f32[32,100,1,128]{3,2,1,0:T(1,128)} %bitcast.8), calls=%async_computation | async-start | bytes 3276800 | tf_op jit(solution)/shard_map/all_to_all | solution.py:348
  12.6 0.0 copy-done.6
  12.6 0.0 copy-done.7
  12.6 0.0 copy-done.8
  12.6 2.0 %collective-permute-start = (f32[448,128]{1,0:T(8,128)S(1)}, f32[448,128]{1,0:T(8,128)S(1)}, u32[]{:S(2)}, u32[]{:S(2)}) collective-permute-start(f32[448,128]{1,0:T(8,128)S(1)} %pad_maximum_fusion.own_ref), channel_id=1, source_target_pairs={{0,1},{1,2},{2,3},{3,0},{4,5},{5,6},{6,7},{7,4},{8,9},{9,10},{10,1... | collective-permute-start | bytes 688136 | tf_op jit(solution)/shard_map/ppermute | solution.py:353
  14.6 3.6 %collective-permute-start.1 = (f32[448,128]{1,0:T(8,128)S(1)}, f32[448,128]{1,0:T(8,128)S(1)}, u32[]{:S(2)}, u32[]{:S(2)}) collective-permute-start(f32[448,128]{1,0:T(8,128)S(1)} %pad_maximum_fusion.own_ref), channel_id=1, source_target_pairs={{0,2},{1,3},{2,0},{3,1},{4,6},{5,7},{6,4},{7,5},{8,10},{9,11},{10,... | collective-permute-start | bytes 688136 | tf_op jit(solution)/shard_map/ppermute | solution.py:353
  18.2 1.0 collective-permute-start.2
  19.2 0.1 pad_add_fusion.where_ref
  19.3 3.3 %collective-permute-done.one_ref = f32[448,128]{1,0:T(8,128)S(1)} collective-permute-done((f32[448,128]{1,0:T(8,128)S(1)}, f32[448,128]{1,0:T(8,128)S(1)}, u32[]{:S(2)}, u32[]{:S(2)}) %collective-permute-start) | collective-permute-done | bytes 229408 | tf_op jit(solution)/shard_map/ppermute | solution.py:353
  22.6 6.1 %collective-permute-done.1.two_ref = f32[448,128]{1,0:T(8,128)S(1)} collective-permute-done((f32[448,128]{1,0:T(8,128)S(1)}, f32[448,128]{1,0:T(8,128)S(1)}, u32[]{:S(2)}, u32[]{:S(2)}) %collective-permute-start.1) | collective-permute-done | bytes 229408 | tf_op jit(solution)/shard_map/ppermute | solution.py:353
  28.7 0.0 collective-permute-done.2.three_ref
  28.7 3.3 %feats.1 = (bf16[8192,128]{1,0:T(8,128)(2,1)}, bf16[4096,128]{1,0:T(8,128)(2,1)}) custom-call(f32[448,128]{1,0:T(8,128)S(1)} %pad_maximum_fusion.own_ref, f32[448,128]{1,0:T(8,128)S(1)} %collective-permute-done.one_ref, f32[448,128]{1,0:T(8,128)S(1)} %collective-permute-done.1.two_ref, f32[448,128]{1,0:T(8,128)S(1)} %collective-permute-done.2.three_ref), custom_call_target="tpu_custom_call" | custom-call | flops 5000000000 | bytes 5000000 | tf_op jit(solution)/shard_map/feats/pallas_call | solution.py:32
  32.1 2.7 %all-to-all-done = f32[32,100,1,128]{3,2,1,0:T(1,128)S(1)} async-done(((f32[32,100,1,128]{3,2,1,0:T(1,128)}), f32[32,100,1,128]{3,2,1,0:T(1,128)S(1)}, u32[]{:S(2)}, u32[]{:S(2)}) %all-to-all-start) | async-done | bytes 1638432 | tf_op jit(solution)/shard_map/all_to_all | solution.py:348
  34.7 38.6 %terms.1 = f32[3072,128]{1,0:T(8,128)S(1)} custom-call(s32[2]{0:T(128)S(1)} %pad_add_fusion.where_ref, f32[3200,128]{1,0:T(8,128)S(1)} %bitcast.21, bf16[8192,128]{1,0:T(8,128)(2,1)} %get-tuple-element.12.far_ref, bf16[4096,128]{1,0:T(8,128)(2,1)} %get-tuple-element.13.farc_ref), custom_call_target="tpu_custom_call" | custom-call | flops 44999999488 | bytes 45000000 | tf_op jit(solution)/shard_map/terms/pallas_call | solution.py:32
  73.4 0.0 copy-start.4
  73.4 26.4 %all_to_all.10 = f32[32,96,1,128]{3,1,2,0:T(8,128)S(1)} all-to-all(f32[32,96,1,128]{3,1,2,0:T(8,128)S(1)} %bitcast.22), channel_id=1, replica_groups=mesh['vol'=32,'surf'=4] {'vol'}, dimensions={0} | all-to-all | bytes 3145728 | tf_op jit(solution)/shard_map/all_to_all | solution.py:348
  99.8 0.0 copy-done.4
  99.8 0.0 copy-start
  99.8 0.0 copy-start.2
  99.8 0.0 copy-start.5
  99.8 1.5 %sums.1.own_ref = f32[192,128]{1,0:T(8,128)S(1)} custom-call(s32[16,64]{1,0:T(8,128)S(1)} %bitcast.32, f32[3072,128]{1,0:T(8,128)S(1)} %bitcast.23), custom_call_target="tpu_custom_call" | custom-call | flops 2000000000 | bytes 2000000 | tf_op jit(solution)/shard_map/sums/pallas_call | solution.py:32
  101.3 2.0 %collective-permute-start.3 = (f32[192,128]{1,0:T(8,128)S(1)}, f32[192,128]{1,0:T(8,128)S(1)}, u32[]{:S(2)}, u32[]{:S(2)}) collective-permute-start(f32[192,128]{1,0:T(8,128)S(1)} %sums.1.own_ref), channel_id=1, source_target_pairs={{0,1},{1,2},{2,3},{3,0},{4,5},{5,6},{6,7},{7,4},{8,9},{9,10},{10,1... | collective-permute-start | bytes 294920 | tf_op jit(solution)/shard_map/ppermute | solution.py:353
  103.3 3.6 %collective-permute-start.4 = (f32[192,128]{1,0:T(8,128)S(1)}, f32[192,128]{1,0:T(8,128)S(1)}, u32[]{:S(2)}, u32[]{:S(2)}) collective-permute-start(f32[192,128]{1,0:T(8,128)S(1)} %sums.1.own_ref), channel_id=1, source_target_pairs={{0,2},{1,3},{2,0},{3,1},{4,6},{5,7},{6,4},{7,5},{8,10},{9,11},{10,... | collective-permute-start | bytes 294920 | tf_op jit(solution)/shard_map/ppermute | solution.py:353
  106.9 1.0 collective-permute-start.5
  107.9 0.0 copy-done
  107.9 0.0 copy-done.2
  107.9 0.0 copy-done.5
  107.9 3.8 %place.1.place_ref = f32[3,384,128]{2,1,0:T(8,128)S(1)} custom-call(s32[2]{0:T(128)S(1)} %pad_add_fusion.where_ref, s32[8,64]{1,0:T(8,128)S(1)} %bitcast.33, f32[3,64,128]{2,1,0:T(8,128)S(1)} %bitcast.28, s32[3,64,256]{2,1,0:T(8,128)S(1)} %bitcast.24), custom_call_target="tpu_custom_call" | custom-call | flops 4000000000 | bytes 4000000 | tf_op jit(solution)/shard_map/place/pallas_call | solution.py:32
  111.7 0.0 collective-permute-done.3.one_ref
  111.7 0.9 collective-permute-done.4.two_ref
  112.6 0.0 collective-permute-done.5.three_ref
  112.6 1.9 %collective-permute-start.6 = (f32[32,128]{1,0:T(8,128)S(1)}, f32[32,128]{1,0:T(8,128)S(1)}, u32[]{:S(2)}, u32[]{:S(2)}) collective-permute-start(f32[32,128]{1,0:T(8,128)S(1)} %get-tuple-element.17), channel_id=1, source_target_pairs={{0,4},{4,8},{8,12},{12,16},{16,20},{20,24},{24,28},{28,32},{32,36}... | collective-permute-start | bytes 49160 | tf_op jit(solution)/shard_map/ppermute | solution.py:427
  114.5 5.7 %collective-permute-start.7 = (f32[32,128]{1,0:T(8,128)S(1)}, f32[32,128]{1,0:T(8,128)S(1)}, u32[]{:S(2)}, u32[]{:S(2)}) collective-permute-start(f32[32,128]{1,0:T(8,128)S(1)} %get-tuple-element.18), channel_id=1, source_target_pairs={{4,0},{8,4},{12,8},{16,12},{20,16},{24,20},{28,24},{32,28},{36,32}... | collective-permute-start | bytes 49160 | tf_op jit(solution)/shard_map/ppermute | solution.py:428
  120.3 4.4 %inner.1 = (f32[3,64,128]{2,1,0:T(8,128)}, f32[64,256]{1,0:T(8,128)S(1)}) custom-call(s32[2]{0:T(128)S(1)} %pad_add_fusion.where_ref, s32[8,64]{1,0:T(8,128)S(1)} %bitcast.34, f32[192,128]{1,0:T(8,128)S(1)} %get-tuple-element.14.d_ref, f32[3,384,128]{2,1,0:T(8,128)S(1)} %place.1.place_ref, s32[3,64,256]{2,1,0:T(8,128)S(1)} %bitcast.25), custom_call_target="tpu_custom_call" | custom-call | flops 4000000000 | bytes 4000000 | tf_op jit(solution)/shard_map/inner/pallas_call | solution.py:32
  124.7 0.0 collective-permute-done.6.low_ref
  124.7 0.0 collective-permute-done.7.high_ref
  124.7 2.0 %edges.1 = f32[64,256]{1,0:T(8,128)} custom-call(s32[2]{0:T(128)S(1)} %pad_add_fusion.where_ref, s32[8,64]{1,0:T(8,128)S(1)} %bitcast.35, f32[3,64,128]{2,1,0:T(8,128)S(1)} %bitcast.30, f32[192,128]{1,0:T(8,128)S(1)} %get-tuple-element.14.d_ref, f32[32,128]{1,0:T(8,128)S(1)} %collective-permute-done.6.low_ref, ...), custom_call_target="tpu_custom_call" | custom-call | flops 2000000000 | bytes 2000000 | tf_op jit(solution)/shard_map/edges/pallas_call | solution.py:32
  (2 shorter events, 0.0 us)
Async XLA Ops:
  0.6 0.9 copy-start.1
  1.5 0.7 copy-start.3
  4.9 7.7 %copy-start.6 = (f32[64,3,128]{2,0,1:T(8,128)S(1)}, f32[64,3,128]{2,0,1:T(8,128)}, u32[]{:S(2)}) copy-start(f32[64,3,128]{2,0,1:T(8,128)} %param.9) | copy-start | bytes 294916
  4.9 7.7 %copy-start.7 = (f32[64,3,128]{2,0,1:T(8,128)S(1)}, f32[64,3,128]{2,0,1:T(8,128)}, u32[]{:S(2)}) copy-start(f32[64,3,128]{2,0,1:T(8,128)} %param.8) | copy-start | bytes 294916
  4.9 7.7 %copy-start.8 = (f32[64,128]{1,0:T(8,128)S(1)}, f32[64,128]{1,0:T(8,128)}, u32[]{:S(2)}) copy-start(f32[64,128]{1,0:T(8,128)} %param.10) | copy-start | bytes 98308
  4.9 29.8 %all-to-all-start = ((f32[32,100,1,128]{3,2,1,0:T(1,128)}), f32[32,100,1,128]{3,2,1,0:T(1,128)S(1)}, u32[]{:S(2)}, u32[]{:S(2)}) async-start(f32[32,100,1,128]{3,2,1,0:T(1,128)} %bitcast.8), calls=%async_computation | async-start | bytes 3276800 | tf_op jit(solution)/shard_map/all_to_all | solution.py:348
  12.6 10.0 %collective-permute-start = (f32[448,128]{1,0:T(8,128)S(1)}, f32[448,128]{1,0:T(8,128)S(1)}, u32[]{:S(2)}, u32[]{:S(2)}) collective-permute-start(f32[448,128]{1,0:T(8,128)S(1)} %pad_maximum_fusion.own_ref), channel_id=1, source_target_pairs={{0,1},{1,2},{2,3},{3,0},{4,5},{5,6},{6,7},{7,4},{8,9},{9,10},{10,1... | collective-permute-start | bytes 688136 | tf_op jit(solution)/shard_map/ppermute | solution.py:353
  14.6 14.1 %collective-permute-start.1 = (f32[448,128]{1,0:T(8,128)S(1)}, f32[448,128]{1,0:T(8,128)S(1)}, u32[]{:S(2)}, u32[]{:S(2)}) collective-permute-start(f32[448,128]{1,0:T(8,128)S(1)} %pad_maximum_fusion.own_ref), channel_id=1, source_target_pairs={{0,2},{1,3},{2,0},{3,1},{4,6},{5,7},{6,4},{7,5},{8,10},{9,11},{10,... | collective-permute-start | bytes 688136 | tf_op jit(solution)/shard_map/ppermute | solution.py:353
  18.2 10.5 %collective-permute-start.2 = (f32[448,128]{1,0:T(8,128)S(1)}, f32[448,128]{1,0:T(8,128)S(1)}, u32[]{:S(2)}, u32[]{:S(2)}) collective-permute-start(f32[448,128]{1,0:T(8,128)S(1)} %pad_maximum_fusion.own_ref), channel_id=1, source_target_pairs={{0,3},{1,0},{2,1},{3,2},{4,7},{5,4},{6,5},{7,6},{8,11},{9,8},{10,9... | collective-permute-start | bytes 688136 | tf_op jit(solution)/shard_map/ppermute | solution.py:353
  73.4 26.4 %copy-start.4 = (s32[1,64,16]{1,2,0:T(8,128)S(1)}, s32[1,64,16]{1,2,0:T(8,128)}, u32[]{:S(2)}) copy-start(s32[1,64,16]{1,2,0:T(8,128)} %param.11) | copy-start | bytes 12292
  99.8 8.1 %copy-start = (s32[64,3,256]{2,0,1:T(8,128)S(1)}, s32[64,3,256]{2,0,1:T(8,128)}, u32[]{:S(2)}) copy-start(s32[64,3,256]{2,0,1:T(8,128)} %param.13) | copy-start | bytes 589828
  99.8 8.1 %copy-start.2 = (f32[64,3,128]{2,0,1:T(8,128)S(1)}, f32[64,3,128]{2,0,1:T(8,128)}, u32[]{:S(2)}) copy-start(f32[64,3,128]{2,0,1:T(8,128)} %param.7) | copy-start | bytes 294916
  99.8 8.1 %copy-start.5 = (s32[64,8]{0,1:T(8,128)S(1)}, s32[64,8]{0,1:T(8,128)}, u32[]{:S(2)}) copy-start(s32[64,8]{0,1:T(8,128)} %param.12) | copy-start | bytes 6148
  101.3 10.3 %collective-permute-start.3 = (f32[192,128]{1,0:T(8,128)S(1)}, f32[192,128]{1,0:T(8,128)S(1)}, u32[]{:S(2)}, u32[]{:S(2)}) collective-permute-start(f32[192,128]{1,0:T(8,128)S(1)} %sums.1.own_ref), channel_id=1, source_target_pairs={{0,1},{1,2},{2,3},{3,0},{4,5},{5,6},{6,7},{7,4},{8,9},{9,10},{10,1... | collective-permute-start | bytes 294920 | tf_op jit(solution)/shard_map/ppermute | solution.py:353
  103.3 9.2 %collective-permute-start.4 = (f32[192,128]{1,0:T(8,128)S(1)}, f32[192,128]{1,0:T(8,128)S(1)}, u32[]{:S(2)}, u32[]{:S(2)}) collective-permute-start(f32[192,128]{1,0:T(8,128)S(1)} %sums.1.own_ref), channel_id=1, source_target_pairs={{0,2},{1,3},{2,0},{3,1},{4,6},{5,7},{6,4},{7,5},{8,10},{9,11},{10,... | collective-permute-start | bytes 294920 | tf_op jit(solution)/shard_map/ppermute | solution.py:353
  106.9 5.7 %collective-permute-start.5 = (f32[192,128]{1,0:T(8,128)S(1)}, f32[192,128]{1,0:T(8,128)S(1)}, u32[]{:S(2)}, u32[]{:S(2)}) collective-permute-start(f32[192,128]{1,0:T(8,128)S(1)} %sums.1.own_ref), channel_id=1, source_target_pairs={{0,3},{1,0},{2,1},{3,2},{4,7},{5,4},{6,5},{7,6},{8,11},{9,8},{10,9... | collective-permute-start | bytes 294920 | tf_op jit(solution)/shard_map/ppermute | solution.py:353
  112.6 12.1 %collective-permute-start.6 = (f32[32,128]{1,0:T(8,128)S(1)}, f32[32,128]{1,0:T(8,128)S(1)}, u32[]{:S(2)}, u32[]{:S(2)}) collective-permute-start(f32[32,128]{1,0:T(8,128)S(1)} %get-tuple-element.17), channel_id=1, source_target_pairs={{0,4},{4,8},{8,12},{12,16},{16,20},{20,24},{24,28},{28,32},{32,36}... | collective-permute-start | bytes 49160 | tf_op jit(solution)/shard_map/ppermute | solution.py:427
  114.5 10.1 %collective-permute-start.7 = (f32[32,128]{1,0:T(8,128)S(1)}, f32[32,128]{1,0:T(8,128)S(1)}, u32[]{:S(2)}, u32[]{:S(2)}) collective-permute-start(f32[32,128]{1,0:T(8,128)S(1)} %get-tuple-element.18), channel_id=1, source_target_pairs={{4,0},{8,4},{12,8},{16,12},{20,16},{24,20},{28,24},{32,28},{36,32}... | collective-permute-start | bytes 49160 | tf_op jit(solution)/shard_map/ppermute | solution.py:428

commit v8 on v7

--- a/solution.py
+++ b/solution.py
@@ -66,21 +66,37 @@
     return table, jnp.where(used, rank, -1.0)
 
 
-def prep_kernel(list_ref, node_ref, o_ref):
+def prep_kernel(list_far, node_far, o_far, list_ref, node_ref, low_ref, high_ref, sems):
+    list_copy = pltpu.make_async_copy(list_far, list_ref, sems.at[0])
+    node_copy = pltpu.make_async_copy(node_far, node_ref, sems.at[1])
+    list_copy.start()
+    node_copy.start()
+    list_copy.wait()
     table, slot = slot_table(list_ref[...])
     slot_t = slot.T
+    ids = [
+        jnp.sum(jnp.where(slot == float(j), table - 1.0, 0.0), axis=0, keepdims=True)
+        for j in range(SLOTS)
+    ]
+    stacked = jnp.concatenate(ids + [jnp.zeros((128 - SLOTS, 128), F)], 0).T
+    node_copy.wait()
     nodes = jnp.concatenate([node_ref[c] for c in range(3)], 1)
     parts = [p.astype(BF) for p in split3(nodes)]
-    ids = []
-    for j in range(SLOTS):
-        at = float(j)
-        ids.append(jnp.sum(jnp.where(slot == at, table - 1.0, 0.0), axis=0, keepdims=True))
-        sel = (slot_t == at).astype(F).astype(BF)
-        got = sum(jnp.dot(sel, p, preferred_element_type=F) for p in parts)
-        for c in range(3):
-            o_ref[pl.ds(c * SLOTS + j, DEVICES, stride=ASK), :] = got[:, c * 128 : (c + 1) * 128]
-    stacked = jnp.concatenate(ids + [jnp.zeros((128 - SLOTS, 128), F)], 0).T
-    o_ref[pl.ds(ASK - 1, DEVICES, stride=ASK), :] = stacked
+    owners = DEVICES // 2
+    copies = []
+    for half, ref in enumerate((low_ref, high_ref)):
+        rows = slice(half * owners, (half + 1) * owners)
+        for j in range(SLOTS):
+            sel = (slot_t[rows] == float(j)).astype(F).astype(BF)
+            got = sum(jnp.dot(sel, p, preferred_element_type=F) for p in parts)
+            for c in range(3):
+                ref[pl.ds(c * SLOTS + j, owners, stride=ASK), :] = got[:, c * 128 : (c + 1) * 128]
+        ref[pl.ds(ASK - 1, owners, stride=ASK), :] = stacked[rows]
+        part = pl.ds(half * owners * ASK, owners * ASK)
+        copies.append(pltpu.make_async_copy(ref, o_far.at[part, :], sems.at[2 + half]))
+        copies[half].start()
+    for copy in copies:
+        copy.wait()
 
 
 def feat_kernel(own_ref, one_ref, two_ref, three_ref, far_ref, farc_ref, a_ref, cf_ref, sems):
@@ -181,7 +197,6 @@
     stage0(0, 0)
     stage0(1, 1)
     a_copy.wait()
-    c_copy.wait()
     for j in slots:
         stage1(0, 0, j)
     stage0(2, 0)
@@ -189,6 +204,7 @@
         stage1(1, 1, j)
     for j in slots:
         stage2(0, j)
+    c_copy.wait()
 
     def some(h, carry):
         for u in range(UNROLL):
@@ -367,8 +383,16 @@
     (sent,) = call(
         prep_kernel,
         "prep",
-        (shape(DEVICES * ASK, 128),),
-        [("v", listed), ("v", nodes)],
+        (pltpu.HBM((DEVICES * ASK, 128), F),),
+        [("f", pltpu.with_memory_space_constraint(a, pltpu.HBM)) for a in (listed, nodes)],
+        [
+            pltpu.VMEM(listed.shape, I),
+            pltpu.VMEM(nodes.shape, F),
+            pltpu.VMEM((DEVICES // 2 * ASK, 128), F),
+            pltpu.VMEM((DEVICES // 2 * ASK, 128), F),
+            pltpu.SemaphoreType.DMA((4,)),
+        ],
+        out=FAR,
     )
     near, codes = neighbours.T, faces.transpose(1, 0, 2)
     sent, early = lax.optimization_barrier((sent, codes))

time: 127 us -> 126 us (level)
  local copies, waits for them, and re-layouts: 1.61 us -> 0.04 us
    unnamed x18 -> x14, local copies, waits for them, and re-layouts: 1.61 us -> 0.04 us
where the time goes in v8:
time: 126 us; the launch traced here: 125 us
  Pallas kernels  56.6 us (45%)
  starting transfers between devices  28.5 us (23%)
  blocking collectives  26.4 us (21%)
  waiting for transfers between devices  13 us (10%)
    pallas_call x8, Pallas kernels, call(): pl.pallas_call(kernel, name=name, out_shape=outs, in_specs=specs, out_spe...  56.6 us
    all_to_all x1, blocking collectives, to_all(): lax.all_to_all(packets, 'vol', split_axis=0, concat_axis=0, tiled=True)  26.4 us
    ppermute x6, starting transfers between devices, around(): lax.ppermute(array, 'surf', [(i, (i + k) % 4) for i in range(4)])  13.1 us
    ppermute x6, waiting for transfers between devices, around(): lax.ppermute(array, 'surf', [(i, (i + k) % 4) for i in range(4)])  10.4 us
    all_to_all x1, starting transfers between devices, to_all(): lax.all_to_all(packets, 'vol', split_axis=0, concat_axis=0, tiled=True)  7.68 us
    ppermute x1, starting transfers between devices, body(): high = lax.ppermute(down, 'vol', [(i + 1, i) for i in range(31)])  5.74 us
    all_to_all x1, waiting for transfers between devices, to_all(): lax.all_to_all(packets, 'vol', split_axis=0, concat_axis=0, tiled=True)  2.66 us
  transfers between devices with their start and end apart: 9, of which 4 were waited for; matrix products, arithmetic and copies ran while one was open for 0% of the time, Pallas kernels for 9%

profile of v8, /device:TPU:8, one launch (start us, length us, event | category | flops | bytes accessed | tf_op | source)
XLA Modules:
  0.0 125.5 jit_solution(15476524045805360730)
XLA Ops:
  0.6 3.1 %prep.1 = f32[3200,128]{1,0:T(8,128)} custom-call(s32[16,64]{1,0:T(8,128)} %bitcast.31, f32[3,64,128]{2,1,0:T(8,128)} %bitcast.27), custom_call_target="tpu_custom_call" | custom-call | flops 2000000000 | bytes 2000000 | tf_op jit(solution)/shard_map/prep/pallas_call | solution.py:32
  3.8 0.0 copy-start.4
  3.8 0.0 copy-start.5
  3.8 0.0 copy-start.6
  3.8 7.7 %all-to-all-start = ((f32[32,100,1,128]{3,2,1,0:T(1,128)}), f32[32,100,1,128]{3,2,1,0:T(1,128)S(1)}, u32[]{:S(2)}, u32[]{:S(2)}) async-start(f32[32,100,1,128]{3,2,1,0:T(1,128)} %bitcast.36), calls=%async_computation | async-start | bytes 3276800 | tf_op jit(solution)/shard_map/all_to_all | solution.py:364
  11.5 0.0 copy-done.4
  11.5 0.0 copy-done.5
  11.5 0.0 copy-done.6
  11.6 2.0 %collective-permute-start = (f32[448,128]{1,0:T(8,128)S(1)}, f32[448,128]{1,0:T(8,128)S(1)}, u32[]{:S(2)}, u32[]{:S(2)}) collective-permute-start(f32[448,128]{1,0:T(8,128)S(1)} %pad_maximum_fusion.own_ref), channel_id=1, source_target_pairs={{0,1},{1,2},{2,3},{3,0},{4,5},{5,6},{6,7},{7,4},{8,9},{9,10},{10,1... | collective-permute-start | bytes 688136 | tf_op jit(solution)/shard_map/ppermute | solution.py:369
  13.5 3.6 %collective-permute-start.1 = (f32[448,128]{1,0:T(8,128)S(1)}, f32[448,128]{1,0:T(8,128)S(1)}, u32[]{:S(2)}, u32[]{:S(2)}) collective-permute-start(f32[448,128]{1,0:T(8,128)S(1)} %pad_maximum_fusion.own_ref), channel_id=1, source_target_pairs={{0,2},{1,3},{2,0},{3,1},{4,6},{5,7},{6,4},{7,5},{8,10},{9,11},{10,... | collective-permute-start | bytes 688136 | tf_op jit(solution)/shard_map/ppermute | solution.py:369
  17.1 1.0 collective-permute-start.2
  18.1 0.1 pad_add_fusion.where_ref
  18.2 3.3 %collective-permute-done.one_ref = f32[448,128]{1,0:T(8,128)S(1)} collective-permute-done((f32[448,128]{1,0:T(8,128)S(1)}, f32[448,128]{1,0:T(8,128)S(1)}, u32[]{:S(2)}, u32[]{:S(2)}) %collective-permute-start) | collective-permute-done | bytes 229408 | tf_op jit(solution)/shard_map/ppermute | solution.py:369
  21.5 6.1 %collective-permute-done.1.two_ref = f32[448,128]{1,0:T(8,128)S(1)} collective-permute-done((f32[448,128]{1,0:T(8,128)S(1)}, f32[448,128]{1,0:T(8,128)S(1)}, u32[]{:S(2)}, u32[]{:S(2)}) %collective-permute-start.1) | collective-permute-done | bytes 229408 | tf_op jit(solution)/shard_map/ppermute | solution.py:369
  27.6 0.0 collective-permute-done.2.three_ref
  27.6 3.3 %feats.1 = (bf16[8192,128]{1,0:T(8,128)(2,1)}, bf16[4096,128]{1,0:T(8,128)(2,1)}) custom-call(f32[448,128]{1,0:T(8,128)S(1)} %pad_maximum_fusion.own_ref, f32[448,128]{1,0:T(8,128)S(1)} %collective-permute-done.one_ref, f32[448,128]{1,0:T(8,128)S(1)} %collective-permute-done.1.two_ref, f32[448,128]{1,0:T(8,128)S(1)} %collective-permute-done.2.three_ref), custom_call_target="tpu_custom_call" | custom-call | flops 5000000000 | bytes 5000000 | tf_op jit(solution)/shard_map/feats/pallas_call | solution.py:32
  31.0 2.7 %all-to-all-done = f32[32,100,1,128]{3,2,1,0:T(1,128)S(1)} async-done(((f32[32,100,1,128]{3,2,1,0:T(1,128)}), f32[32,100,1,128]{3,2,1,0:T(1,128)S(1)}, u32[]{:S(2)}, u32[]{:S(2)}) %all-to-all-start) | async-done | bytes 1638432 | tf_op jit(solution)/shard_map/all_to_all | solution.py:364
  33.6 38.5 %terms.1 = f32[3072,128]{1,0:T(8,128)S(1)} custom-call(s32[2]{0:T(128)S(1)} %pad_add_fusion.where_ref, f32[3200,128]{1,0:T(8,128)S(1)} %bitcast.21, bf16[8192,128]{1,0:T(8,128)(2,1)} %get-tuple-element.12.far_ref, bf16[4096,128]{1,0:T(8,128)(2,1)} %get-tuple-element.13.farc_ref), custom_call_target="tpu_custom_call" | custom-call | flops 44999999488 | bytes 45000000 | tf_op jit(solution)/shard_map/terms/pallas_call | solution.py:32
  72.2 0.0 copy-start.2
  72.2 26.4 %all_to_all.10 = f32[32,96,1,128]{3,1,2,0:T(8,128)S(1)} all-to-all(f32[32,96,1,128]{3,1,2,0:T(8,128)S(1)} %bitcast.22), channel_id=1, replica_groups=mesh['vol'=32,'surf'=4] {'vol'}, dimensions={0} | all-to-all | bytes 3145728 | tf_op jit(solution)/shard_map/all_to_all | solution.py:364
  98.6 0.0 copy-done.2
  98.6 0.0 copy-start
  98.6 0.0 copy-start.1
  98.6 0.0 copy-start.3
  98.6 1.5 %sums.1.own_ref = f32[192,128]{1,0:T(8,128)S(1)} custom-call(s32[16,64]{1,0:T(8,128)S(1)} %bitcast.32, f32[3072,128]{1,0:T(8,128)S(1)} %bitcast.23), custom_call_target="tpu_custom_call" | custom-call | flops 2000000000 | bytes 2000000 | tf_op jit(solution)/shard_map/sums/pallas_call | solution.py:32
  100.1 2.0 %collective-permute-start.3 = (f32[192,128]{1,0:T(8,128)S(1)}, f32[192,128]{1,0:T(8,128)S(1)}, u32[]{:S(2)}, u32[]{:S(2)}) collective-permute-start(f32[192,128]{1,0:T(8,128)S(1)} %sums.1.own_ref), channel_id=1, source_target_pairs={{0,1},{1,2},{2,3},{3,0},{4,5},{5,6},{6,7},{7,4},{8,9},{9,10},{10,1... | collective-permute-start | bytes 294920 | tf_op jit(solution)/shard_map/ppermute | solution.py:369
  102.1 3.6 %collective-permute-start.4 = (f32[192,128]{1,0:T(8,128)S(1)}, f32[192,128]{1,0:T(8,128)S(1)}, u32[]{:S(2)}, u32[]{:S(2)}) collective-permute-start(f32[192,128]{1,0:T(8,128)S(1)} %sums.1.own_ref), channel_id=1, source_target_pairs={{0,2},{1,3},{2,0},{3,1},{4,6},{5,7},{6,4},{7,5},{8,10},{9,11},{10,... | collective-permute-start | bytes 294920 | tf_op jit(solution)/shard_map/ppermute | solution.py:369
  105.7 1.0 collective-permute-start.5
  106.7 0.0 copy-done
  106.7 0.0 copy-done.1
  106.7 0.0 copy-done.3
  106.7 3.8 %place.1.place_ref = f32[3,384,128]{2,1,0:T(8,128)S(1)} custom-call(s32[2]{0:T(128)S(1)} %pad_add_fusion.where_ref, s32[8,64]{1,0:T(8,128)S(1)} %bitcast.33, f32[3,64,128]{2,1,0:T(8,128)S(1)} %bitcast.28, s32[3,64,256]{2,1,0:T(8,128)S(1)} %bitcast.24), custom_call_target="tpu_custom_call" | custom-call | flops 4000000000 | bytes 4000000 | tf_op jit(solution)/shard_map/place/pallas_call | solution.py:32
  110.5 0.0 collective-permute-done.3.one_ref
  110.5 0.9 collective-permute-done.4.two_ref
  111.4 0.0 collective-permute-done.5.three_ref
  111.4 1.9 %collective-permute-start.6 = (f32[32,128]{1,0:T(8,128)S(1)}, f32[32,128]{1,0:T(8,128)S(1)}, u32[]{:S(2)}, u32[]{:S(2)}) collective-permute-start(f32[32,128]{1,0:T(8,128)S(1)} %get-tuple-element.17), channel_id=1, source_target_pairs={{0,4},{4,8},{8,12},{12,16},{16,20},{20,24},{24,28},{28,32},{32,36}... | collective-permute-start | bytes 49160 | tf_op jit(solution)/shard_map/ppermute | solution.py:451
  113.4 5.7 %collective-permute-start.7 = (f32[32,128]{1,0:T(8,128)S(1)}, f32[32,128]{1,0:T(8,128)S(1)}, u32[]{:S(2)}, u32[]{:S(2)}) collective-permute-start(f32[32,128]{1,0:T(8,128)S(1)} %get-tuple-element.18), channel_id=1, source_target_pairs={{4,0},{8,4},{12,8},{16,12},{20,16},{24,20},{28,24},{32,28},{36,32}... | collective-permute-start | bytes 49160 | tf_op jit(solution)/shard_map/ppermute | solution.py:452
  119.1 4.4 %inner.1 = (f32[3,64,128]{2,1,0:T(8,128)}, f32[64,256]{1,0:T(8,128)S(1)}) custom-call(s32[2]{0:T(128)S(1)} %pad_add_fusion.where_ref, s32[8,64]{1,0:T(8,128)S(1)} %bitcast.34, f32[192,128]{1,0:T(8,128)S(1)} %get-tuple-element.14.d_ref, f32[3,384,128]{2,1,0:T(8,128)S(1)} %place.1.place_ref, s32[3,64,256]{2,1,0:T(8,128)S(1)} %bitcast.25), custom_call_target="tpu_custom_call" | custom-call | flops 4000000000 | bytes 4000000 | tf_op jit(solution)/shard_map/inner/pallas_call | solution.py:32
  123.5 0.0 collective-permute-done.6.low_ref
  123.5 0.0 collective-permute-done.7.high_ref
  123.5 2.0 %edges.1 = f32[64,256]{1,0:T(8,128)} custom-call(s32[2]{0:T(128)S(1)} %pad_add_fusion.where_ref, s32[8,64]{1,0:T(8,128)S(1)} %bitcast.35, f32[3,64,128]{2,1,0:T(8,128)S(1)} %bitcast.30, f32[192,128]{1,0:T(8,128)S(1)} %get-tuple-element.14.d_ref, f32[32,128]{1,0:T(8,128)S(1)} %collective-permute-done.6.low_ref, ...), custom_call_target="tpu_custom_call" | custom-call | flops 2000000000 | bytes 2000000 | tf_op jit(solution)/shard_map/edges/pallas_call | solution.py:32
  (2 shorter events, 0.0 us)
Async XLA Ops:
  3.8 7.7 %copy-start.4 = (f32[64,3,128]{2,0,1:T(8,128)S(1)}, f32[64,3,128]{2,0,1:T(8,128)}, u32[]{:S(2)}) copy-start(f32[64,3,128]{2,0,1:T(8,128)} %param.9) | copy-start | bytes 294916
  3.8 7.7 %copy-start.5 = (f32[64,3,128]{2,0,1:T(8,128)S(1)}, f32[64,3,128]{2,0,1:T(8,128)}, u32[]{:S(2)}) copy-start(f32[64,3,128]{2,0,1:T(8,128)} %param.8) | copy-start | bytes 294916
  3.8 7.7 %copy-start.6 = (f32[64,128]{1,0:T(8,128)S(1)}, f32[64,128]{1,0:T(8,128)}, u32[]{:S(2)}) copy-start(f32[64,128]{1,0:T(8,128)} %param.10) | copy-start | bytes 98308
  3.8 29.8 %all-to-all-start = ((f32[32,100,1,128]{3,2,1,0:T(1,128)}), f32[32,100,1,128]{3,2,1,0:T(1,128)S(1)}, u32[]{:S(2)}, u32[]{:S(2)}) async-start(f32[32,100,1,128]{3,2,1,0:T(1,128)} %bitcast.36), calls=%async_computation | async-start | bytes 3276800 | tf_op jit(solution)/shard_map/all_to_all | solution.py:364
  11.6 10.0 %collective-permute-start = (f32[448,128]{1,0:T(8,128)S(1)}, f32[448,128]{1,0:T(8,128)S(1)}, u32[]{:S(2)}, u32[]{:S(2)}) collective-permute-start(f32[448,128]{1,0:T(8,128)S(1)} %pad_maximum_fusion.own_ref), channel_id=1, source_target_pairs={{0,1},{1,2},{2,3},{3,0},{4,5},{5,6},{6,7},{7,4},{8,9},{9,10},{10,1... | collective-permute-start | bytes 688136 | tf_op jit(solution)/shard_map/ppermute | solution.py:369
  13.5 14.1 %collective-permute-start.1 = (f32[448,128]{1,0:T(8,128)S(1)}, f32[448,128]{1,0:T(8,128)S(1)}, u32[]{:S(2)}, u32[]{:S(2)}) collective-permute-start(f32[448,128]{1,0:T(8,128)S(1)} %pad_maximum_fusion.own_ref), channel_id=1, source_target_pairs={{0,2},{1,3},{2,0},{3,1},{4,6},{5,7},{6,4},{7,5},{8,10},{9,11},{10,... | collective-permute-start | bytes 688136 | tf_op jit(solution)/shard_map/ppermute | solution.py:369
  17.1 10.5 %collective-permute-start.2 = (f32[448,128]{1,0:T(8,128)S(1)}, f32[448,128]{1,0:T(8,128)S(1)}, u32[]{:S(2)}, u32[]{:S(2)}) collective-permute-start(f32[448,128]{1,0:T(8,128)S(1)} %pad_maximum_fusion.own_ref), channel_id=1, source_target_pairs={{0,3},{1,0},{2,1},{3,2},{4,7},{5,4},{6,5},{7,6},{8,11},{9,8},{10,9... | collective-permute-start | bytes 688136 | tf_op jit(solution)/shard_map/ppermute | solution.py:369
  72.2 26.4 %copy-start.2 = (s32[1,64,16]{1,2,0:T(8,128)S(1)}, s32[1,64,16]{1,2,0:T(8,128)}, u32[]{:S(2)}) copy-start(s32[1,64,16]{1,2,0:T(8,128)} %param.11) | copy-start | bytes 12292
  98.6 8.1 %copy-start = (s32[64,3,256]{2,0,1:T(8,128)S(1)}, s32[64,3,256]{2,0,1:T(8,128)}, u32[]{:S(2)}) copy-start(s32[64,3,256]{2,0,1:T(8,128)} %param.13) | copy-start | bytes 589828
  98.6 8.1 %copy-start.1 = (f32[64,3,128]{2,0,1:T(8,128)S(1)}, f32[64,3,128]{2,0,1:T(8,128)}, u32[]{:S(2)}) copy-start(f32[64,3,128]{2,0,1:T(8,128)} %param.7) | copy-start | bytes 294916
  98.6 8.1 %copy-start.3 = (s32[64,8]{0,1:T(8,128)S(1)}, s32[64,8]{0,1:T(8,128)}, u32[]{:S(2)}) copy-start(s32[64,8]{0,1:T(8,128)} %param.12) | copy-start | bytes 6148
  100.1 10.3 %collective-permute-start.3 = (f32[192,128]{1,0:T(8,128)S(1)}, f32[192,128]{1,0:T(8,128)S(1)}, u32[]{:S(2)}, u32[]{:S(2)}) collective-permute-start(f32[192,128]{1,0:T(8,128)S(1)} %sums.1.own_ref), channel_id=1, source_target_pairs={{0,1},{1,2},{2,3},{3,0},{4,5},{5,6},{6,7},{7,4},{8,9},{9,10},{10,1... | collective-permute-start | bytes 294920 | tf_op jit(solution)/shard_map/ppermute | solution.py:369
  102.1 9.3 %collective-permute-start.4 = (f32[192,128]{1,0:T(8,128)S(1)}, f32[192,128]{1,0:T(8,128)S(1)}, u32[]{:S(2)}, u32[]{:S(2)}) collective-permute-start(f32[192,128]{1,0:T(8,128)S(1)} %sums.1.own_ref), channel_id=1, source_target_pairs={{0,2},{1,3},{2,0},{3,1},{4,6},{5,7},{6,4},{7,5},{8,10},{9,11},{10,... | collective-permute-start | bytes 294920 | tf_op jit(solution)/shard_map/ppermute | solution.py:369
  105.7 5.7 %collective-permute-start.5 = (f32[192,128]{1,0:T(8,128)S(1)}, f32[192,128]{1,0:T(8,128)S(1)}, u32[]{:S(2)}, u32[]{:S(2)}) collective-permute-start(f32[192,128]{1,0:T(8,128)S(1)} %sums.1.own_ref), channel_id=1, source_target_pairs={{0,3},{1,0},{2,1},{3,2},{4,7},{5,4},{6,5},{7,6},{8,11},{9,8},{10,9... | collective-permute-start | bytes 294920 | tf_op jit(solution)/shard_map/ppermute | solution.py:369
  111.4 12.1 %collective-permute-start.6 = (f32[32,128]{1,0:T(8,128)S(1)}, f32[32,128]{1,0:T(8,128)S(1)}, u32[]{:S(2)}, u32[]{:S(2)}) collective-permute-start(f32[32,128]{1,0:T(8,128)S(1)} %get-tuple-element.17), channel_id=1, source_target_pairs={{0,4},{4,8},{8,12},{12,16},{16,20},{20,24},{24,28},{28,32},{32,36}... | collective-permute-start | bytes 49160 | tf_op jit(solution)/shard_map/ppermute | solution.py:451
  113.4 10.2 %collective-permute-start.7 = (f32[32,128]{1,0:T(8,128)S(1)}, f32[32,128]{1,0:T(8,128)S(1)}, u32[]{:S(2)}, u32[]{:S(2)}) collective-permute-start(f32[32,128]{1,0:T(8,128)S(1)} %get-tuple-element.18), channel_id=1, source_target_pairs={{4,0},{8,4},{12,8},{16,12},{20,16},{24,20},{28,24},{32,28},{36,32}... | collective-permute-start | bytes 49160 | tf_op jit(solution)/shard_map/ppermute | solution.py:452

commit v9 on v8

--- a/solution.py
+++ b/solution.py
@@ -229,7 +229,7 @@
         terms = jnp.concatenate(
             [back_ref[pl.ds(c * SLOTS + j, DEVICES, stride=GIVE), :] for c in range(3)], 1
         )
-        for part in split3(terms):
+        for part in split3(terms)[0:2]:
             acc = acc + jnp.dot(sel, part.astype(BF), preferred_element_type=F)
     for c in range(3):
         o_ref[c * BOX_DEV : (c + 1) * BOX_DEV, :] = acc[:, c * 128 : (c + 1) * 128]

time: 126 us -> 126 us (level)
  no operation moved by 1% of the time
where the time goes in v9:
time: 126 us; the launch traced here: 125 us
  Pallas kernels  56.5 us (45%)
  starting transfers between devices  28.5 us (23%)
  blocking collectives  26.4 us (21%)
  waiting for transfers between devices  13 us (10%)
    pallas_call x8, Pallas kernels, call(): pl.pallas_call(kernel, name=name, out_shape=outs, in_specs=specs, out_spe...  56.5 us
    all_to_all x1, blocking collectives, to_all(): lax.all_to_all(packets, 'vol', split_axis=0, concat_axis=0, tiled=True)  26.4 us
    ppermute x6, starting transfers between devices, around(): lax.ppermute(array, 'surf', [(i, (i + k) % 4) for i in range(4)])  13.1 us
    ppermute x6, waiting for transfers between devices, around(): lax.ppermute(array, 'surf', [(i, (i + k) % 4) for i in range(4)])  10.3 us
    all_to_all x1, starting transfers between devices, to_all(): lax.all_to_all(packets, 'vol', split_axis=0, concat_axis=0, tiled=True)  7.68 us
    ppermute x1, starting transfers between devices, body(): high = lax.ppermute(down, 'vol', [(i + 1, i) for i in range(31)])  5.73 us
    all_to_all x1, waiting for transfers between devices, to_all(): lax.all_to_all(packets, 'vol', split_axis=0, concat_axis=0, tiled=True)  2.66 us
  transfers between devices with their start and end apart: 9, of which 4 were waited for; matrix products, arithmetic and copies ran while one was open for 0% of the time, Pallas kernels for 9%

profile of v9, /device:TPU:8, one launch (start us, length us, event | category | flops | bytes accessed | tf_op | source)
XLA Modules:
  0.0 125.3 jit_solution(1982768216839564621)
XLA Ops:
  0.6 3.1 %prep.1 = f32[3200,128]{1,0:T(8,128)} custom-call(s32[16,64]{1,0:T(8,128)} %bitcast.31, f32[3,64,128]{2,1,0:T(8,128)} %bitcast.27), custom_call_target="tpu_custom_call" | custom-call | flops 2000000000 | bytes 2000000 | tf_op jit(solution)/shard_map/prep/pallas_call | solution.py:32
  3.8 0.0 copy-start.4
  3.8 0.0 copy-start.5
  3.8 0.0 copy-start.6
  3.8 7.7 %all-to-all-start = ((f32[32,100,1,128]{3,2,1,0:T(1,128)}), f32[32,100,1,128]{3,2,1,0:T(1,128)S(1)}, u32[]{:S(2)}, u32[]{:S(2)}) async-start(f32[32,100,1,128]{3,2,1,0:T(1,128)} %bitcast.36), calls=%async_computation | async-start | bytes 3276800 | tf_op jit(solution)/shard_map/all_to_all | solution.py:364
  11.5 0.0 copy-done.4
  11.5 0.0 copy-done.5
  11.5 0.0 copy-done.6
  11.6 2.0 %collective-permute-start = (f32[448,128]{1,0:T(8,128)S(1)}, f32[448,128]{1,0:T(8,128)S(1)}, u32[]{:S(2)}, u32[]{:S(2)}) collective-permute-start(f32[448,128]{1,0:T(8,128)S(1)} %pad_maximum_fusion.own_ref), channel_id=1, source_target_pairs={{0,1},{1,2},{2,3},{3,0},{4,5},{5,6},{6,7},{7,4},{8,9},{9,10},{10,1... | collective-permute-start | bytes 688136 | tf_op jit(solution)/shard_map/ppermute | solution.py:369
  13.5 3.6 %collective-permute-start.1 = (f32[448,128]{1,0:T(8,128)S(1)}, f32[448,128]{1,0:T(8,128)S(1)}, u32[]{:S(2)}, u32[]{:S(2)}) collective-permute-start(f32[448,128]{1,0:T(8,128)S(1)} %pad_maximum_fusion.own_ref), channel_id=1, source_target_pairs={{0,2},{1,3},{2,0},{3,1},{4,6},{5,7},{6,4},{7,5},{8,10},{9,11},{10,... | collective-permute-start | bytes 688136 | tf_op jit(solution)/shard_map/ppermute | solution.py:369
  17.1 1.0 collective-permute-start.2
  18.1 0.1 pad_add_fusion.where_ref
  18.2 3.3 %collective-permute-done.one_ref = f32[448,128]{1,0:T(8,128)S(1)} collective-permute-done((f32[448,128]{1,0:T(8,128)S(1)}, f32[448,128]{1,0:T(8,128)S(1)}, u32[]{:S(2)}, u32[]{:S(2)}) %collective-permute-start) | collective-permute-done | bytes 229408 | tf_op jit(solution)/shard_map/ppermute | solution.py:369
  21.5 6.1 %collective-permute-done.1.two_ref = f32[448,128]{1,0:T(8,128)S(1)} collective-permute-done((f32[448,128]{1,0:T(8,128)S(1)}, f32[448,128]{1,0:T(8,128)S(1)}, u32[]{:S(2)}, u32[]{:S(2)}) %collective-permute-start.1) | collective-permute-done | bytes 229408 | tf_op jit(solution)/shard_map/ppermute | solution.py:369
  27.6 0.0 collective-permute-done.2.three_ref
  27.6 3.3 %feats.1 = (bf16[8192,128]{1,0:T(8,128)(2,1)}, bf16[4096,128]{1,0:T(8,128)(2,1)}) custom-call(f32[448,128]{1,0:T(8,128)S(1)} %pad_maximum_fusion.own_ref, f32[448,128]{1,0:T(8,128)S(1)} %collective-permute-done.one_ref, f32[448,128]{1,0:T(8,128)S(1)} %collective-permute-done.1.two_ref, f32[448,128]{1,0:T(8,128)S(1)} %collective-permute-done.2.three_ref), custom_call_target="tpu_custom_call" | custom-call | flops 5000000000 | bytes 5000000 | tf_op jit(solution)/shard_map/feats/pallas_call | solution.py:32
  31.0 2.7 %all-to-all-done = f32[32,100,1,128]{3,2,1,0:T(1,128)S(1)} async-done(((f32[32,100,1,128]{3,2,1,0:T(1,128)}), f32[32,100,1,128]{3,2,1,0:T(1,128)S(1)}, u32[]{:S(2)}, u32[]{:S(2)}) %all-to-all-start) | async-done | bytes 1638432 | tf_op jit(solution)/shard_map/all_to_all | solution.py:364
  33.6 38.5 %terms.1 = f32[3072,128]{1,0:T(8,128)S(1)} custom-call(s32[2]{0:T(128)S(1)} %pad_add_fusion.where_ref, f32[3200,128]{1,0:T(8,128)S(1)} %bitcast.21, bf16[8192,128]{1,0:T(8,128)(2,1)} %get-tuple-element.12.far_ref, bf16[4096,128]{1,0:T(8,128)(2,1)} %get-tuple-element.13.farc_ref), custom_call_target="tpu_custom_call" | custom-call | flops 44999999488 | bytes 45000000 | tf_op jit(solution)/shard_map/terms/pallas_call | solution.py:32
  72.2 0.0 copy-start.2
  72.2 26.4 %all_to_all.10 = f32[32,96,1,128]{3,1,2,0:T(8,128)S(1)} all-to-all(f32[32,96,1,128]{3,1,2,0:T(8,128)S(1)} %bitcast.22), channel_id=1, replica_groups=mesh['vol'=32,'surf'=4] {'vol'}, dimensions={0} | all-to-all | bytes 3145728 | tf_op jit(solution)/shard_map/all_to_all | solution.py:364
  98.6 0.0 copy-done.2
  98.6 0.0 copy-start
  98.6 0.0 copy-start.1
  98.6 0.0 copy-start.3
  98.6 1.4 %sums.1.own_ref = f32[192,128]{1,0:T(8,128)S(1)} custom-call(s32[16,64]{1,0:T(8,128)S(1)} %bitcast.32, f32[3072,128]{1,0:T(8,128)S(1)} %bitcast.23), custom_call_target="tpu_custom_call" | custom-call | flops 2000000000 | bytes 2000000 | tf_op jit(solution)/shard_map/sums/pallas_call | solution.py:32
  100.0 2.0 %collective-permute-start.3 = (f32[192,128]{1,0:T(8,128)S(1)}, f32[192,128]{1,0:T(8,128)S(1)}, u32[]{:S(2)}, u32[]{:S(2)}) collective-permute-start(f32[192,128]{1,0:T(8,128)S(1)} %sums.1.own_ref), channel_id=1, source_target_pairs={{0,1},{1,2},{2,3},{3,0},{4,5},{5,6},{6,7},{7,4},{8,9},{9,10},{10,1... | collective-permute-start | bytes 294920 | tf_op jit(solution)/shard_map/ppermute | solution.py:369
  102.0 3.6 %collective-permute-start.4 = (f32[192,128]{1,0:T(8,128)S(1)}, f32[192,128]{1,0:T(8,128)S(1)}, u32[]{:S(2)}, u32[]{:S(2)}) collective-permute-start(f32[192,128]{1,0:T(8,128)S(1)} %sums.1.own_ref), channel_id=1, source_target_pairs={{0,2},{1,3},{2,0},{3,1},{4,6},{5,7},{6,4},{7,5},{8,10},{9,11},{10,... | collective-permute-start | bytes 294920 | tf_op jit(solution)/shard_map/ppermute | solution.py:369
  105.5 1.0 collective-permute-start.5
  106.5 0.0 copy-done
  106.6 0.0 copy-done.1
  106.6 0.0 copy-done.3
  106.6 3.8 %place.1.place_ref = f32[3,384,128]{2,1,0:T(8,128)S(1)} custom-call(s32[2]{0:T(128)S(1)} %pad_add_fusion.where_ref, s32[8,64]{1,0:T(8,128)S(1)} %bitcast.33, f32[3,64,128]{2,1,0:T(8,128)S(1)} %bitcast.28, s32[3,64,256]{2,1,0:T(8,128)S(1)} %bitcast.24), custom_call_target="tpu_custom_call" | custom-call | flops 4000000000 | bytes 4000000 | tf_op jit(solution)/shard_map/place/pallas_call | solution.py:32
  110.3 0.0 collective-permute-done.3.one_ref
  110.3 0.9 collective-permute-done.4.two_ref
  111.2 0.0 collective-permute-done.5.three_ref
  111.2 1.9 %collective-permute-start.6 = (f32[32,128]{1,0:T(8,128)S(1)}, f32[32,128]{1,0:T(8,128)S(1)}, u32[]{:S(2)}, u32[]{:S(2)}) collective-permute-start(f32[32,128]{1,0:T(8,128)S(1)} %get-tuple-element.17), channel_id=1, source_target_pairs={{0,4},{4,8},{8,12},{12,16},{16,20},{20,24},{24,28},{28,32},{32,36}... | collective-permute-start | bytes 49160 | tf_op jit(solution)/shard_map/ppermute | solution.py:451
  113.2 5.7 %collective-permute-start.7 = (f32[32,128]{1,0:T(8,128)S(1)}, f32[32,128]{1,0:T(8,128)S(1)}, u32[]{:S(2)}, u32[]{:S(2)}) collective-permute-start(f32[32,128]{1,0:T(8,128)S(1)} %get-tuple-element.18), channel_id=1, source_target_pairs={{4,0},{8,4},{12,8},{16,12},{20,16},{24,20},{28,24},{32,28},{36,32}... | collective-permute-start | bytes 49160 | tf_op jit(solution)/shard_map/ppermute | solution.py:452
  118.9 4.4 %inner.1 = (f32[3,64,128]{2,1,0:T(8,128)}, f32[64,256]{1,0:T(8,128)S(1)}) custom-call(s32[2]{0:T(128)S(1)} %pad_add_fusion.where_ref, s32[8,64]{1,0:T(8,128)S(1)} %bitcast.34, f32[192,128]{1,0:T(8,128)S(1)} %get-tuple-element.14.d_ref, f32[3,384,128]{2,1,0:T(8,128)S(1)} %place.1.place_ref, s32[3,64,256]{2,1,0:T(8,128)S(1)} %bitcast.25), custom_call_target="tpu_custom_call" | custom-call | flops 4000000000 | bytes 4000000 | tf_op jit(solution)/shard_map/inner/pallas_call | solution.py:32
  123.3 0.0 collective-permute-done.6.low_ref
  123.3 0.0 collective-permute-done.7.high_ref
  123.3 2.0 %edges.1 = f32[64,256]{1,0:T(8,128)} custom-call(s32[2]{0:T(128)S(1)} %pad_add_fusion.where_ref, s32[8,64]{1,0:T(8,128)S(1)} %bitcast.35, f32[3,64,128]{2,1,0:T(8,128)S(1)} %bitcast.30, f32[192,128]{1,0:T(8,128)S(1)} %get-tuple-element.14.d_ref, f32[32,128]{1,0:T(8,128)S(1)} %collective-permute-done.6.low_ref, ...), custom_call_target="tpu_custom_call" | custom-call | flops 2000000000 | bytes 2000000 | tf_op jit(solution)/shard_map/edges/pallas_call | solution.py:32
  (2 shorter events, 0.0 us)
Async XLA Ops:
  3.8 7.7 %copy-start.4 = (f32[64,3,128]{2,0,1:T(8,128)S(1)}, f32[64,3,128]{2,0,1:T(8,128)}, u32[]{:S(2)}) copy-start(f32[64,3,128]{2,0,1:T(8,128)} %param.9) | copy-start | bytes 294916
  3.8 7.7 %copy-start.5 = (f32[64,3,128]{2,0,1:T(8,128)S(1)}, f32[64,3,128]{2,0,1:T(8,128)}, u32[]{:S(2)}) copy-start(f32[64,3,128]{2,0,1:T(8,128)} %param.8) | copy-start | bytes 294916
  3.8 7.7 %copy-start.6 = (f32[64,128]{1,0:T(8,128)S(1)}, f32[64,128]{1,0:T(8,128)}, u32[]{:S(2)}) copy-start(f32[64,128]{1,0:T(8,128)} %param.10) | copy-start | bytes 98308
  3.8 29.8 %all-to-all-start = ((f32[32,100,1,128]{3,2,1,0:T(1,128)}), f32[32,100,1,128]{3,2,1,0:T(1,128)S(1)}, u32[]{:S(2)}, u32[]{:S(2)}) async-start(f32[32,100,1,128]{3,2,1,0:T(1,128)} %bitcast.36), calls=%async_computation | async-start | bytes 3276800 | tf_op jit(solution)/shard_map/all_to_all | solution.py:364
  11.6 10.0 %collective-permute-start = (f32[448,128]{1,0:T(8,128)S(1)}, f32[448,128]{1,0:T(8,128)S(1)}, u32[]{:S(2)}, u32[]{:S(2)}) collective-permute-start(f32[448,128]{1,0:T(8,128)S(1)} %pad_maximum_fusion.own_ref), channel_id=1, source_target_pairs={{0,1},{1,2},{2,3},{3,0},{4,5},{5,6},{6,7},{7,4},{8,9},{9,10},{10,1... | collective-permute-start | bytes 688136 | tf_op jit(solution)/shard_map/ppermute | solution.py:369
  13.5 14.1 %collective-permute-start.1 = (f32[448,128]{1,0:T(8,128)S(1)}, f32[448,128]{1,0:T(8,128)S(1)}, u32[]{:S(2)}, u32[]{:S(2)}) collective-permute-start(f32[448,128]{1,0:T(8,128)S(1)} %pad_maximum_fusion.own_ref), channel_id=1, source_target_pairs={{0,2},{1,3},{2,0},{3,1},{4,6},{5,7},{6,4},{7,5},{8,10},{9,11},{10,... | collective-permute-start | bytes 688136 | tf_op jit(solution)/shard_map/ppermute | solution.py:369
  17.1 10.5 %collective-permute-start.2 = (f32[448,128]{1,0:T(8,128)S(1)}, f32[448,128]{1,0:T(8,128)S(1)}, u32[]{:S(2)}, u32[]{:S(2)}) collective-permute-start(f32[448,128]{1,0:T(8,128)S(1)} %pad_maximum_fusion.own_ref), channel_id=1, source_target_pairs={{0,3},{1,0},{2,1},{3,2},{4,7},{5,4},{6,5},{7,6},{8,11},{9,8},{10,9... | collective-permute-start | bytes 688136 | tf_op jit(solution)/shard_map/ppermute | solution.py:369
  72.2 26.5 %copy-start.2 = (s32[1,64,16]{1,2,0:T(8,128)S(1)}, s32[1,64,16]{1,2,0:T(8,128)}, u32[]{:S(2)}) copy-start(s32[1,64,16]{1,2,0:T(8,128)} %param.11) | copy-start | bytes 12292
  98.6 7.9 %copy-start = (s32[64,3,256]{2,0,1:T(8,128)S(1)}, s32[64,3,256]{2,0,1:T(8,128)}, u32[]{:S(2)}) copy-start(s32[64,3,256]{2,0,1:T(8,128)} %param.13) | copy-start | bytes 589828
  98.6 7.9 %copy-start.1 = (f32[64,3,128]{2,0,1:T(8,128)S(1)}, f32[64,3,128]{2,0,1:T(8,128)}, u32[]{:S(2)}) copy-start(f32[64,3,128]{2,0,1:T(8,128)} %param.7) | copy-start | bytes 294916
  98.6 7.9 %copy-start.3 = (s32[64,8]{0,1:T(8,128)S(1)}, s32[64,8]{0,1:T(8,128)}, u32[]{:S(2)}) copy-start(s32[64,8]{0,1:T(8,128)} %param.12) | copy-start | bytes 6148
  100.0 10.3 %collective-permute-start.3 = (f32[192,128]{1,0:T(8,128)S(1)}, f32[192,128]{1,0:T(8,128)S(1)}, u32[]{:S(2)}, u32[]{:S(2)}) collective-permute-start(f32[192,128]{1,0:T(8,128)S(1)} %sums.1.own_ref), channel_id=1, source_target_pairs={{0,1},{1,2},{2,3},{3,0},{4,5},{5,6},{6,7},{7,4},{8,9},{9,10},{10,1... | collective-permute-start | bytes 294920 | tf_op jit(solution)/shard_map/ppermute | solution.py:369
  102.0 9.2 %collective-permute-start.4 = (f32[192,128]{1,0:T(8,128)S(1)}, f32[192,128]{1,0:T(8,128)S(1)}, u32[]{:S(2)}, u32[]{:S(2)}) collective-permute-start(f32[192,128]{1,0:T(8,128)S(1)} %sums.1.own_ref), channel_id=1, source_target_pairs={{0,2},{1,3},{2,0},{3,1},{4,6},{5,7},{6,4},{7,5},{8,10},{9,11},{10,... | collective-permute-start | bytes 294920 | tf_op jit(solution)/shard_map/ppermute | solution.py:369
  105.5 5.7 %collective-permute-start.5 = (f32[192,128]{1,0:T(8,128)S(1)}, f32[192,128]{1,0:T(8,128)S(1)}, u32[]{:S(2)}, u32[]{:S(2)}) collective-permute-start(f32[192,128]{1,0:T(8,128)S(1)} %sums.1.own_ref), channel_id=1, source_target_pairs={{0,3},{1,0},{2,1},{3,2},{4,7},{5,4},{6,5},{7,6},{8,11},{9,8},{10,9... | collective-permute-start | bytes 294920 | tf_op jit(solution)/shard_map/ppermute | solution.py:369
  111.2 12.1 %collective-permute-start.6 = (f32[32,128]{1,0:T(8,128)S(1)}, f32[32,128]{1,0:T(8,128)S(1)}, u32[]{:S(2)}, u32[]{:S(2)}) collective-permute-start(f32[32,128]{1,0:T(8,128)S(1)} %get-tuple-element.17), channel_id=1, source_target_pairs={{0,4},{4,8},{8,12},{12,16},{16,20},{20,24},{24,28},{28,32},{32,36}... | collective-permute-start | bytes 49160 | tf_op jit(solution)/shard_map/ppermute | solution.py:451
  113.2 10.1 %collective-permute-start.7 = (f32[32,128]{1,0:T(8,128)S(1)}, f32[32,128]{1,0:T(8,128)S(1)}, u32[]{:S(2)}, u32[]{:S(2)}) collective-permute-start(f32[32,128]{1,0:T(8,128)S(1)} %get-tuple-element.18), channel_id=1, source_target_pairs={{4,0},{8,4},{12,8},{16,12},{20,16},{24,20},{28,24},{32,28},{36,32}... | collective-permute-start | bytes 49160 | tf_op jit(solution)/shard_map/ppermute | solution.py:452
